TPU v7x, 512 devices: a whole 4x8x8 slice. The times are simulated.
512 devices in a mesh: ctx: 32 (over x, z), ch: 16 (over y, core).
Axes of the slice: x: 4, y: 8, z: 8, core: 2. Of those that a mesh axis runs over, the one named last changes fastest.
Arguments:
- tokens: bfloat16 [4096, 4096], P('ctx'), may hold values from -6 to 6
- projections: bfloat16 [3, 4096, 4096], P(None, 'ctx', 'ch'), may hold values from -0.09375 to 0.09375
- decay_rates: float32 [4096, 16], P('ch'), may hold values from 0.00012207031 to 0.03
- residues: float32 [4096, 16], P('ch'), may hold values from -1.5 to 1.5
- short_filter: bfloat16 [4096, 128], P('ch'), may hold values from -0.5 to 0.5
Outputs:
- mixed: bfloat16 [4096, 4096], P('ctx', 'ch')
All inputs are finite; a program needn't handle non-finite values.
Results may differ from a plain program's by a relative error of at most 0.0068.
Values may be sent and summed in bfloat16 or wider, within the bound.
No kernel may reach another device: no remote copies, remote signals or barrier semaphores. Data moves between devices by JAX's collectives and lax.ppermute only.
A program may use at most 64 MiB of HBM per device.

v0:
```python
import math

import jax
import jax.numpy as jnp
import numpy as np
from jax import lax
from jax.experimental import pallas as pl
from jax.experimental.pallas import tpu as pltpu
from jax.sharding import PartitionSpec as P

f32, bf16 = jnp.float32, jnp.bfloat16
highest = lax.Precision.HIGHEST

NX, NZ, NC = 4, 8, 2
ROWS = 128
LANES = 128
HALF = 64
SPAN = 2 * ROWS
MODES = 16
SHIFTS = (1, 3, 2)

x_groups = [[x * NZ + z for x in range(NX)] for z in range(NZ)]
z_groups = [[x * NZ + z for z in range(NZ)] for x in range(NX)]


def real_transform():
    bins, places = np.arange(ROWS)[:, None], np.arange(SPAN)[None, :]
    angles = 2 * math.pi * (bins * places % SPAN) / SPAN
    real, imag = np.cos(angles), -np.sin(angles)
    imag[0] = np.where(np.arange(SPAN) % 2 == 0, 1.0, -1.0)
    return np.concatenate([real, imag]).astype(np.float32)


def inverse_transform():
    places, bins = np.arange(SPAN)[:, None], np.arange(ROWS)[None, :]
    angles = 2 * math.pi * (bins * places % SPAN) / SPAN
    real, imag = 2 * np.cos(angles), -2 * np.sin(angles)
    real[:, 0] = 1.0
    imag[:, 0] = np.where(np.arange(SPAN) % 2 == 0, 1.0, -1.0)
    return (np.concatenate([real, imag], axis=1) / SPAN).astype(np.float32)


def dot32(a, b):
    return jnp.dot(a, b, precision=highest, preferred_element_type=f32)


def multiply_spectra(u, h):
    first = lax.broadcasted_iota(jnp.int32, (ROWS, u.shape[1]), 0) == 0
    ur, ui, hr, hi = u[:ROWS], u[ROWS:], h[:ROWS], h[ROWS:]
    both = ui * hi
    real = ur * hr - jnp.where(first, 0.0, both)
    imag = jnp.where(first, both, ur * hi + ui * hr)
    return jnp.concatenate([real, imag], axis=0)


def lower_lanes(shape):
    return lax.broadcasted_iota(jnp.int32, shape, len(shape) - 1) < HALF


def swap_halves(v):
    return pltpu.roll(v, HALF, v.ndim - 1)


def call(body, outs, name, *args, scratch=(), flops=10**9):
    return pl.pallas_call(
        body,
        out_shape=outs,
        in_specs=[pl.BlockSpec(memory_space=pltpu.VMEM)] * len(args),
        out_specs=jax.tree.map(lambda _: pl.BlockSpec(memory_space=pltpu.VMEM), outs),
        scratch_shapes=scratch,
        compiler_params=pltpu.CompilerParams(vmem_limit_bytes=8 << 20),
        cost_estimate=pl.CostEstimate(flops=flops, bytes_accessed=flops // 200, transcendentals=0),
        name=name,
    )(*args)


def spread_weights(w_ref, out_ref):
    low = lower_lanes((ROWS, LANES))
    low_half = lower_lanes((HALF, LANES))
    for x in range(NX):
        at = pl.ds(LANES * (x // 2), LANES)
        a, v, o = (w_ref[k, :, at].astype(f32) for k in range(3))
        if x % 2 == 0:
            both = jnp.where(low, a, swap_halves(v))
            packed = jnp.where(low_half, o[:HALF], swap_halves(o[HALF:]))
        else:
            both = jnp.where(low, swap_halves(a), v)
            packed = jnp.where(low_half, swap_halves(o[:HALF]), o[HALF:])
        both, packed = both.astype(bf16), packed.astype(bf16)
        for z in range(NZ):
            out_ref[x * NZ + z, :ROWS] = both
            out_ref[x * NZ + z, ROWS:] = packed


def build_tables(a_ref, w_ref, taps_ref, fwd_ref, into_ref, out_ref, long_ref, short_ref):
    t = lax.broadcasted_iota(jnp.int32, (ROWS, LANES), 0).astype(f32)
    impulse = jnp.zeros((ROWS, LANES), f32)
    for m in range(MODES):
        rate, weight = a_ref[m : m + 1, :], w_ref[m : m + 1, :]
        into_ref[m] = jnp.exp(-rate * (ROWS - 1.0 - t))
        out_ref[m] = weight * jnp.exp(-rate * (t + 1.0))
        impulse = impulse + weight * jnp.exp(-rate * t)
    transform = fwd_ref[:, :ROWS]
    long_ref[...] = dot32(transform, impulse)
    short_ref[...] = dot32(transform, taps_ref[...])


def positions():
    ctx, ch = lax.axis_index("ctx"), lax.axis_index("ch")
    return lax.div(ctx, NZ), lax.rem(ctx, NZ), lax.rem(ch, NC)


def fill_products(tokens_ref, near_refs, far_refs, weight_ref, product_ref):
    x, _, core = positions()
    width = near_refs[0].shape[1]
    near = pl.ds(pl.multiple_of(core * width, width), width)
    far = pl.ds(pl.multiple_of((1 - core) * width, width), width)
    product_ref[x] = jnp.dot(tokens_ref[...], weight_ref[...], preferred_element_type=f32)
    for shift, near_ref, far_ref in zip(SHIFTS, near_refs, far_refs):
        product_ref[lax.rem(x + (NX - shift), NX)] = jnp.dot(
            near_ref[...], weight_ref[near, :], preferred_element_type=f32
        ) + jnp.dot(far_ref[...], weight_ref[far, :], preferred_element_type=f32)


def make_signal(tokens_ref, n0, n1, n2, f0, f1, f2, blocks_ref, into_ref, signal_ref, state_ref, weight_ref, product_ref):
    for block in range(NX * NZ):
        weight_ref[ROWS * block : ROWS * (block + 1), :] = blocks_ref[block, :ROWS]
    fill_products(tokens_ref, (n0, n1, n2), (f0, f1, f2), weight_ref, product_ref)
    low = lower_lanes((ROWS, LANES))
    for pair in range(NX // 2):
        parts = []
        for chunk in (2 * pair, 2 * pair + 1):
            both = product_ref[chunk].astype(bf16).astype(f32)
            parts.append(both * swap_halves(both))
        signal = jnp.where(low, parts[0], parts[1])
        signal_ref[:, LANES * pair : LANES * (pair + 1)] = signal
        for m in range(MODES):
            state = jnp.sum(signal * into_ref[m], axis=0, keepdims=True)
            for z in range(NZ):
                state_ref[z, pair * MODES + m : pair * MODES + m + 1, :] = state


def make_gates(tokens_ref, n0, n1, n2, f0, f1, f2, blocks_ref, signal_ref, fwd_ref, inv_ref, long_ref, both_ref, weight_ref, product_ref):
    low_half = lower_lanes((HALF, LANES))
    for block in range(NX * NZ):
        packed = blocks_ref[block, ROWS:].astype(f32)
        turned = swap_halves(packed)
        weight_ref[ROWS * block : ROWS * block + HALF, :] = jnp.where(low_half, packed, turned).astype(bf16)
        weight_ref[ROWS * block + HALF : ROWS * (block + 1), :] = jnp.where(low_half, turned, packed).astype(bf16)
    fill_products(tokens_ref, (n0, n1, n2), (f0, f1, f2), weight_ref, product_ref)
    spectrum = dot32(fwd_ref[:, :ROWS], signal_ref[...])
    response = jnp.concatenate([long_ref[...]] * 2, axis=1)
    both_ref[:, : 2 * LANES] = dot32(inv_ref[:ROWS, :], multiply_spectra(spectrum, response))
    low = lower_lanes((ROWS, LANES))
    for pair in range(NX // 2):
        gate = jnp.where(low, product_ref[2 * pair], product_ref[2 * pair + 1])
        both_ref[:, LANES * (2 + pair) : LANES * (3 + pair)] = gate.astype(bf16).astype(f32)


def carry_in(states_ref, a_ref, z):
    low = lower_lanes((MODES, LANES))
    rate = a_ref[...] * float(ROWS)
    decay = jnp.exp(-rate)
    decay_row = jnp.exp(-rate * float(NZ))
    decay_here = jnp.exp(-rate * z.astype(f32))
    before, whole = [], []
    for pair in range(NX // 2):
        upto = jnp.zeros((MODES, LANES), f32)
        total = jnp.zeros((MODES, LANES), f32)
        for k in range(NZ):
            step = states_ref[k, pair * MODES : (pair + 1) * MODES, :]
            upto = jnp.where(k < z, upto * decay + step, upto)
            total = total * decay + step
        before.append(upto)
        whole.append(total)
    swapped = [swap_halves(v) for v in whole]
    first = jnp.where(low, 0.0, swapped[0])
    second = jnp.where(
        low,
        swapped[0] + decay_row * whole[0],
        swapped[1] + decay_row * (whole[0] + decay_row * swapped[0]),
    )
    return [before[0] + decay_here * first, before[1] + decay_here * second]


def gate_rows(both_ref, carries, out_ref):
    parts = []
    for pair in range(NX // 2):
        value = both_ref[:, LANES * pair : LANES * (pair + 1)]
        for m in range(MODES):
            value = value + out_ref[m] * carries[pair][m : m + 1, :]
        gate = both_ref[:, LANES * (2 + pair) : LANES * (3 + pair)]
        parts.append((gate * value).astype(bf16).astype(f32))
    return parts


def finish(both_ref, arrived_ref, states_ref, a_ref, out_ref, fwd_ref, inv_ref, short_ref, packed_ref):
    _, z, _ = positions()
    low = lower_lanes((ROWS, LANES))
    own = gate_rows(both_ref, carry_in(states_ref, a_ref, z), out_ref)
    arrived = gate_rows(arrived_ref, carry_in(states_ref, a_ref, lax.rem(z + NZ - 1, NZ)), out_ref)
    turned = [swap_halves(v) for v in arrived]
    shifted = [jnp.where(low, 0.0, turned[0]), jnp.where(low, turned[0], turned[1])]
    previous = jnp.concatenate([jnp.where(z == 0, s, a) for s, a in zip(shifted, arrived)], axis=1)
    window = jnp.concatenate([previous, jnp.concatenate(own, axis=1)], axis=0)
    response = jnp.concatenate([short_ref[...]] * 2, axis=1)
    mixed = dot32(inv_ref[ROWS:, :], multiply_spectra(dot32(fwd_ref[...], window), response))
    low_half = lower_lanes((HALF, LANES))
    for pair in range(2):
        top = mixed[:HALF, LANES * pair : LANES * (pair + 1)]
        bottom = mixed[HALF:, LANES * pair : LANES * (pair + 1)]
        packed_ref[2 * pair] = jnp.where(low_half, top, swap_halves(bottom)).astype(bf16)
        packed_ref[2 * pair + 1] = jnp.where(low_half, swap_halves(top), bottom).astype(bf16)


def unpack_rows(packed_ref, out_ref):
    low = lower_lanes((HALF, LANES))
    for pair in range(2):
        a, b = (packed_ref[2 * pair + h].astype(f32) for h in range(2))
        lanes = slice(LANES * pair, LANES * (pair + 1))
        out_ref[:HALF, lanes] = jnp.where(low, a, swap_halves(b)).astype(bf16)
        out_ref[HALF:, lanes] = jnp.where(low, swap_halves(a), b).astype(bf16)


def per_device(tokens, projections, decay_rates, residues, short_filter):
    sds = jax.ShapeDtypeStruct
    x = lax.axis_index("ctx") // NZ
    core = lax.axis_index("ch") % NC
    width = tokens.shape[1] // NC
    count = NX * NZ
    depth = count * ROWS
    blocks = call(spread_weights, sds((count, ROWS + HALF, LANES), bf16), "spread_weights", projections)
    blocks = lax.all_to_all(blocks, "ctx", 0, 0, tiled=True)
    half = lax.dynamic_slice_in_dim(tokens, core * width, width, 1)
    swap = [(k, k ^ 1) for k in range(lax.axis_size("ch"))]
    near, far = [], []
    for shift in SHIFTS:
        moves = [(a * NZ + b, (a + shift) % NX * NZ + b) for a in range(NX) for b in range(NZ)]
        near.append(lax.ppermute(half, "ctx", moves))
        far.append(lax.ppermute(near[-1], "ch", swap))

    rates = lax.dynamic_slice_in_dim(decay_rates, x * HALF, HALF, 0).T
    weights = lax.dynamic_slice_in_dim(residues, x * HALF, HALF, 0).T * jnp.sqrt(2.0 * rates)
    taps = lax.dynamic_slice_in_dim(short_filter, x * HALF, HALF, 0).T.astype(f32)
    rates, weights, taps = (jnp.concatenate([v, v], axis=1) for v in (rates, weights, taps))
    forward, inverse = jnp.asarray(real_transform()), jnp.asarray(inverse_transform())
    table = sds((MODES, ROWS, LANES), f32)
    spectrum = sds((SPAN, LANES), f32)
    into, out, long_spectrum, short_spectrum = call(
        build_tables, (table, table, spectrum, spectrum), "build_tables", rates, weights, taps, forward
    )
    scratch = [pltpu.VMEM((depth, LANES), bf16), pltpu.VMEM((NX, ROWS, LANES), f32)]
    operands = (tokens, *near, *far, blocks)
    signal, states = call(
        make_signal,
        (sds((ROWS, 2 * LANES), f32), sds((NZ, 2 * MODES, LANES), f32)),
        "make_signal",
        *operands,
        into,
        scratch=scratch,
    )
    states = lax.all_to_all(states, "ctx", 0, 0, tiled=True, axis_index_groups=z_groups)
    both = call(
        make_gates,
        sds((ROWS, 4 * LANES), f32),
        "make_gates",
        *operands,
        signal,
        forward,
        inverse,
        long_spectrum,
        scratch=scratch,
        flops=5 * 10**9,
    )
    onward = [(a * NZ + b, a * NZ + (b + 1) % NZ) for a in range(NX) for b in range(NZ)]
    arrived = lax.ppermute(both, "ctx", onward)
    packed = call(
        finish,
        sds((NX, HALF, LANES), bf16),
        "finish",
        both,
        arrived,
        states,
        rates,
        out,
        forward,
        inverse,
        short_spectrum,
    )
    packed = lax.all_to_all(packed, "ctx", 0, 0, tiled=True, axis_index_groups=x_groups)
    return call(unpack_rows, sds((ROWS, 2 * LANES), bf16), "unpack_rows", packed)


def solution(mesh):
    in_specs = (P("ctx", None), P(None, "ctx", "ch"), P("ch", None), P("ch", None), P("ch", None))
    return jax.shard_map(per_device, mesh=mesh, in_specs=in_specs, out_specs=P("ctx", "ch"), check_vma=False)
```

profile of v0, /device:TPU:32, one launch (start us, length us, event | category | flops | bytes accessed | tf_op | source)
XLA Modules:
  0.0 109.7 jit_solution(1815953110735286178)
XLA Ops:
  0.0 1.0 copy-done.13
  1.0 0.2 spread_weights.1
  1.2 1.2 %copy-done.2 = bf16[32,192,128]{2,1,0:T(8,128)(2,1)} copy-done((bf16[32,192,128]{2,1,0:T(8,128)(2,1)}, bf16[32,192,128]{2,1,0:T(8,128)(2,1)S(1)}, u32[]{:S(2)}) %copy-start.2) | copy-done | bytes 1572888
  2.3 13.3 %all-to-all-start = ((bf16[32,192,128]{2,1,0:T(8,128)(2,1)}), bf16[32,192,128]{2,1,0:T(8,128)(2,1)S(1)}, u32[]{:S(2)}, u32[]{:S(2)}) async-start(bf16[32,192,128]{2,1,0:T(8,128)(2,1)} %copy-done.2), calls=%async_computation | async-start | bytes 3145728 | tf_op jit(solution)/shard_map/all_to_all | solution.py:233
  15.7 0.8 constant_dynamic-slice_fusion.1
  16.5 5.2 %collective-permute-start.2 = (bf16[128,2048]{1,0:T(8,128)(2,1)}, bf16[128,2048]{1,0:T(8,128)(2,1)S(1)}, u32[]{:S(2)}, u32[]{:S(2)}) collective-permute-start(bf16[128,2048]{1,0:T(8,128)(2,1)} %constant_dynamic-slice_fusion.1), channel_id=1, source_target_pairs={{0,256},{16,272},{32,288},{48,304},{64,320},{80,336},{96,352},{112... | collective-permute-start | bytes 1572872 | tf_op jit(solution)/shard_map/ppermute | solution.py:239
  21.7 3.1 %collective-permute-start.1 = (bf16[128,2048]{1,0:T(8,128)(2,1)}, bf16[128,2048]{1,0:T(8,128)(2,1)}, u32[]{:S(2)}, u32[]{:S(2)}) collective-permute-start(bf16[128,2048]{1,0:T(8,128)(2,1)} %constant_dynamic-slice_fusion.1), channel_id=1, source_target_pairs={{0,384},{16,400},{32,416},{48,432},{64,448},{80,464},{96,480},{112... | collective-permute-start | bytes 1572872 | tf_op jit(solution)/shard_map/ppermute | solution.py:239
  24.8 2.8 %collective-permute-start = (bf16[128,2048]{1,0:T(8,128)(2,1)}, bf16[128,2048]{1,0:T(8,128)(2,1)}, u32[]{:S(2)}, u32[]{:S(2)}) collective-permute-start(bf16[128,2048]{1,0:T(8,128)(2,1)} %constant_dynamic-slice_fusion.1), channel_id=1, source_target_pairs={{0,128},{16,144},{32,160},{48,176},{64,192},{80,208},{96,224},{112... | collective-permute-start | bytes 1572872 | tf_op jit(solution)/shard_map/ppermute | solution.py:239
  27.8 17.0 %collective-permute-done.2.n2 = bf16[128,2048]{1,0:T(8,128)(2,1)S(1)} collective-permute-done((bf16[128,2048]{1,0:T(8,128)(2,1)}, bf16[128,2048]{1,0:T(8,128)(2,1)S(1)}, u32[]{:S(2)}, u32[]{:S(2)}) %collective-permute-start.2) | collective-permute-done | bytes 524320 | tf_op jit(solution)/shard_map/ppermute | solution.py:239
  44.8 1.9 %collective-permute-start.5 = (bf16[128,2048]{1,0:T(8,128)(2,1)S(1)}, bf16[128,2048]{1,0:T(8,128)(2,1)S(1)}, u32[]{:S(2)}, u32[]{:S(2)}) collective-permute-start(bf16[128,2048]{1,0:T(8,128)(2,1)S(1)} %collective-permute-done.2.n2), channel_id=1, source_target_pairs={{0,1},{1,0},{2,3},{3,2},{4,5},{5,4},{6,7},{7,6},{8,9},{9,8},{10,11... | collective-permute-start | bytes 1572872 | tf_op jit(solution)/shard_map/ppermute | solution.py:240
  46.7 12.4 %collective-permute-done.1.n1 = bf16[128,2048]{1,0:T(8,128)(2,1)} collective-permute-done((bf16[128,2048]{1,0:T(8,128)(2,1)}, bf16[128,2048]{1,0:T(8,128)(2,1)}, u32[]{:S(2)}, u32[]{:S(2)}) %collective-permute-start.1) | collective-permute-done | bytes 524320 | tf_op jit(solution)/shard_map/ppermute | solution.py:239
  59.1 1.9 %collective-permute-start.4 = (bf16[128,2048]{1,0:T(8,128)(2,1)}, bf16[128,2048]{1,0:T(8,128)(2,1)S(1)}, u32[]{:S(2)}, u32[]{:S(2)}) collective-permute-start(bf16[128,2048]{1,0:T(8,128)(2,1)} %collective-permute-done.1.n1), channel_id=1, source_target_pairs={{0,1},{1,0},{2,3},{3,2},{4,5},{5,4},{6,7},{7,6},{8,9},{9,8},{10,11... | collective-permute-start | bytes 1572872 | tf_op jit(solution)/shard_map/ppermute | solution.py:240
  61.1 2.4 %collective-permute-start.3 = (bf16[128,2048]{1,0:T(8,128)(2,1)}, bf16[128,2048]{1,0:T(8,128)(2,1)S(1)}, u32[]{:S(2)}, u32[]{:S(2)}) collective-permute-start(bf16[128,2048]{1,0:T(8,128)(2,1)} %collective-permute-done.n0), channel_id=1, source_target_pairs={{0,1},{1,0},{2,3},{3,2},{4,5},{5,4},{6,7},{7,6},{8,9},{9,8},{10,11... | collective-permute-start | bytes 1572872 | tf_op jit(solution)/shard_map/ppermute | solution.py:240
  63.8 0.8 build_tables.1
  64.7 1.0 copy-done.3
  65.6 1.0 copy-done.16
  66.6 0.7 copy-done.18
  67.3 0.6 copy-done.20
  67.9 0.8 copy-done.5
  68.8 0.8 copy-done.8
  69.6 0.8 copy-done.11
  70.4 1.2 %copy-done.4 = f32[16,128,128]{2,1,0:T(8,128)S(1)} copy-done((f32[16,128,128]{2,1,0:T(8,128)S(1)}, f32[16,128,128]{2,1,0:T(8,128)}, u32[]{:S(2)}) %copy-start.4) | copy-done | bytes 1048600
  71.6 1.0 copy-done.6
  72.7 1.0 copy-done.9
  73.7 1.0 copy-done.12
  74.7 2.9 %make_signal.1 = (f32[128,256]{1,0:T(8,128)S(1)}, f32[8,32,128]{2,1,0:T(8,128)S(1)}) custom-call(bf16[128,4096]{1,0:T(8,128)(2,1)S(1)} %copy-done.1, bf16[128,2048]{1,0:T(8,128)(2,1)} %collective-permute-done.n0, bf16[128,2048]{1,0:T(8,128)(2,1)} %collective-permute-done.1.n1, bf16[128,2048]{1,0:T(8,128)(2,1)S(1)} %collective-permute-done.2.n2, ...), custom_call_target="tpu_custom_call" | custom-call | flops 1000000000 | bytes 5000000 | tf_op jit(solution)/shard_map/make_signal/pallas_call | solution.py:65
  77.7 3.4 %make_gates.1.both_ref = f32[128,512]{1,0:T(8,128)S(1)} custom-call(bf16[128,4096]{1,0:T(8,128)(2,1)S(1)} %copy-done.1, bf16[128,2048]{1,0:T(8,128)(2,1)} %collective-permute-done.n0, bf16[128,2048]{1,0:T(8,128)(2,1)} %collective-permute-done.1.n1, bf16[128,2048]{1,0:T(8,128)(2,1)S(1)} %collective-permute-done.2.n2, bf16[128,2048]{1,0:T(8,128)(2,1)S(1)} %copy-done.12, ...), custom_call_target="tpu_custom_call" | custom-call | flops 5000000000 | bytes 25000000 | tf_op jit(solution)/shard_map/make_gates/pallas_call | solution.py:65
  81.1 2.3 %collective-permute-start.6 = (f32[128,512]{1,0:T(8,128)S(1)}, f32[128,512]{1,0:T(8,128)S(1)}, u32[]{:S(2)}, u32[]{:S(2)}) collective-permute-start(f32[128,512]{1,0:T(8,128)S(1)} %make_gates.1.both_ref), channel_id=1, source_target_pairs={{0,16},{16,32},{32,48},{48,64},{64,80},{80,96},{96,112},{112,0},{1... | collective-permute-start | bytes 786440 | tf_op jit(solution)/shard_map/ppermute | solution.py:276
  83.4 14.9 %all_to_all.15.states_ref = f32[8,32,128]{2,1,0:T(8,128)S(1)} all-to-all(f32[8,32,128]{2,1,0:T(8,128)S(1)} %get-tuple-element.14), channel_id=1, replica_groups={{0,16,32,48,64,80,96,112},{128,144,160,176,192,208,224,240},{256,272,28..., dimensions={0} | all-to-all | bytes 262144 | tf_op jit(solution)/shard_map/all_to_all | solution.py:262
  98.3 1.3 %finish.1 = bf16[4,64,128]{2,1,0:T(8,128)(2,1)S(1)} custom-call(f32[128,512]{1,0:T(8,128)S(1)} %make_gates.1.both_ref, f32[128,512]{1,0:T(8,128)S(1)} %collective-permute-done.6.arrived_ref, f32[8,32,128]{2,1,0:T(8,128)S(1)} %all_to_all.15.states_ref, f32[16,128]{1,0:T(8,128)S(1)} %pad_maximum_fusion.a_ref, f32[16,128,128]{2,1,0:T(8,128)S(1)} %copy-done.17, ...), custom_call_target="tpu_custom_call" | custom-call | flops 1000000000 | bytes 5000000 | tf_op jit(solution)/shard_map/finish/pallas_call | solution.py:65
  99.6 9.4 %all_to_all.16.packed_ref = bf16[4,64,128]{2,1,0:T(8,128)(2,1)S(1)} all-to-all(bf16[4,64,128]{2,1,0:T(8,128)(2,1)S(1)} %finish.1), channel_id=1, replica_groups={{0,128,256,384},{16,144,272,400},{32,160,288,416},{48,176,304,432},{64,..., dimensions={0} | all-to-all | bytes 131072 | tf_op jit(solution)/shard_map/all_to_all | solution.py:290
  109.0 0.7 unpack_rows.1
  (48 shorter events, 0.6 us)
Async XLA Ops:
  0.0 27.6 %copy-start = (bf16[256,128]{1,0:T(8,128)(2,1)S(1)}, bf16[256,128]{1,0:T(8,128)(2,1)}, u32[]{:S(2)}) copy-start(bf16[256,128]{1,0:T(8,128)(2,1)} %param.11) | copy-start | bytes 196612
  0.0 1.0 copy-start.13
  1.1 1.2 %copy-start.2 = (bf16[32,192,128]{2,1,0:T(8,128)(2,1)}, bf16[32,192,128]{2,1,0:T(8,128)(2,1)S(1)}, u32[]{:S(2)}) copy-start(bf16[32,192,128]{2,1,0:T(8,128)(2,1)S(1)} %spread_weights.1) | copy-start | bytes 4718596
  2.3 13.3 %copy-start.1 = (bf16[128,4096]{1,0:T(8,128)(2,1)S(1)}, bf16[128,4096]{1,0:T(8,128)(2,1)}, u32[]{:S(2)}) copy-start(bf16[128,4096]{1,0:T(8,128)(2,1)} %tokens_ref.3) | copy-start | bytes 3145732
  2.3 25.4 %copy-start.22 = (f32[256,16]{0,1:T(8,128)S(1)}, f32[256,16]{0,1:T(8,128)}, u32[]{:S(2)}) copy-start(f32[256,16]{0,1:T(8,128)} %param.9) | copy-start | bytes 49156
  2.3 61.2 %copy-start.23 = (f32[256,16]{0,1:T(8,128)S(1)}, f32[256,16]{0,1:T(8,128)}, u32[]{:S(2)}) copy-start(f32[256,16]{0,1:T(8,128)} %param.10) | copy-start | bytes 49156
  2.3 61.5 %copy-start.14 = (f32[256,256]{1,0:T(8,128)S(1)}, f32[256,256]{1,0:T(8,128)}, u32[]{:S(2)}) copy-start(f32[256,256]{1,0:T(8,128)} %constant.51.clone.fwd_ref) | copy-start | bytes 786436
  2.3 68.0 %all-to-all-start = ((bf16[32,192,128]{2,1,0:T(8,128)(2,1)}), bf16[32,192,128]{2,1,0:T(8,128)(2,1)S(1)}, u32[]{:S(2)}, u32[]{:S(2)}) async-start(bf16[32,192,128]{2,1,0:T(8,128)(2,1)} %copy-done.2), calls=%async_computation | async-start | bytes 3145728 | tf_op jit(solution)/shard_map/all_to_all | solution.py:233
  16.5 28.3 %collective-permute-start.2 = (bf16[128,2048]{1,0:T(8,128)(2,1)}, bf16[128,2048]{1,0:T(8,128)(2,1)S(1)}, u32[]{:S(2)}, u32[]{:S(2)}) collective-permute-start(bf16[128,2048]{1,0:T(8,128)(2,1)} %constant_dynamic-slice_fusion.1), channel_id=1, source_target_pairs={{0,256},{16,272},{32,288},{48,304},{64,320},{80,336},{96,352},{112... | collective-permute-start | bytes 1572872 | tf_op jit(solution)/shard_map/ppermute | solution.py:239
  21.7 37.4 %collective-permute-start.1 = (bf16[128,2048]{1,0:T(8,128)(2,1)}, bf16[128,2048]{1,0:T(8,128)(2,1)}, u32[]{:S(2)}, u32[]{:S(2)}) collective-permute-start(bf16[128,2048]{1,0:T(8,128)(2,1)} %constant_dynamic-slice_fusion.1), channel_id=1, source_target_pairs={{0,384},{16,400},{32,416},{48,432},{64,448},{80,464},{96,480},{112... | collective-permute-start | bytes 1572872 | tf_op jit(solution)/shard_map/ppermute | solution.py:239
  24.8 36.3 %collective-permute-start = (bf16[128,2048]{1,0:T(8,128)(2,1)}, bf16[128,2048]{1,0:T(8,128)(2,1)}, u32[]{:S(2)}, u32[]{:S(2)}) collective-permute-start(bf16[128,2048]{1,0:T(8,128)(2,1)} %constant_dynamic-slice_fusion.1), channel_id=1, source_target_pairs={{0,128},{16,144},{32,160},{48,176},{64,192},{80,208},{96,224},{112... | collective-permute-start | bytes 1572872 | tf_op jit(solution)/shard_map/ppermute | solution.py:239
  44.8 23.2 %collective-permute-start.5 = (bf16[128,2048]{1,0:T(8,128)(2,1)S(1)}, bf16[128,2048]{1,0:T(8,128)(2,1)S(1)}, u32[]{:S(2)}, u32[]{:S(2)}) collective-permute-start(bf16[128,2048]{1,0:T(8,128)(2,1)S(1)} %collective-permute-done.2.n2), channel_id=1, source_target_pairs={{0,1},{1,0},{2,3},{3,2},{4,5},{5,4},{6,7},{7,6},{8,9},{9,8},{10,11... | collective-permute-start | bytes 1572872 | tf_op jit(solution)/shard_map/ppermute | solution.py:240
  59.1 9.6 %collective-permute-start.4 = (bf16[128,2048]{1,0:T(8,128)(2,1)}, bf16[128,2048]{1,0:T(8,128)(2,1)S(1)}, u32[]{:S(2)}, u32[]{:S(2)}) collective-permute-start(bf16[128,2048]{1,0:T(8,128)(2,1)} %collective-permute-done.1.n1), channel_id=1, source_target_pairs={{0,1},{1,0},{2,3},{3,2},{4,5},{5,4},{6,7},{7,6},{8,9},{9,8},{10,11... | collective-permute-start | bytes 1572872 | tf_op jit(solution)/shard_map/ppermute | solution.py:240
  61.1 8.5 %collective-permute-start.3 = (bf16[128,2048]{1,0:T(8,128)(2,1)}, bf16[128,2048]{1,0:T(8,128)(2,1)S(1)}, u32[]{:S(2)}, u32[]{:S(2)}) collective-permute-start(bf16[128,2048]{1,0:T(8,128)(2,1)} %collective-permute-done.n0), channel_id=1, source_target_pairs={{0,1},{1,0},{2,3},{3,2},{4,5},{5,4},{6,7},{7,6},{8,9},{9,8},{10,11... | collective-permute-start | bytes 1572872 | tf_op jit(solution)/shard_map/ppermute | solution.py:240
  64.7 1.0 copy-start.3
  65.6 1.0 copy-start.16
  66.6 0.7 copy-start.18
  67.3 0.6 copy-start.20
  67.9 0.8 copy-start.5
  68.7 0.8 copy-start.8
  69.6 0.8 copy-start.11
  70.4 1.2 %copy-start.4 = (f32[16,128,128]{2,1,0:T(8,128)S(1)}, f32[16,128,128]{2,1,0:T(8,128)}, u32[]{:S(2)}) copy-start(f32[16,128,128]{2,1,0:T(8,128)} %copy-done.3) | copy-start | bytes 3145732
  71.6 1.0 copy-start.6
  72.7 1.0 copy-start.9
  73.7 1.0 copy-start.12
  74.7 2.9 %copy-start.7 = (bf16[128,2048]{1,0:T(8,128)(2,1)S(1)}, bf16[128,2048]{1,0:T(8,128)(2,1)}, u32[]{:S(2)}) copy-start(bf16[128,2048]{1,0:T(8,128)(2,1)} %copy-done.5) | copy-start | bytes 1572868
  74.7 2.9 %copy-start.10 = (bf16[128,2048]{1,0:T(8,128)(2,1)S(1)}, bf16[128,2048]{1,0:T(8,128)(2,1)}, u32[]{:S(2)}) copy-start(bf16[128,2048]{1,0:T(8,128)(2,1)} %copy-done.8) | copy-start | bytes 1572868
  74.7 2.9 %copy-start.15 = (f32[256,256]{1,0:T(8,128)S(1)}, f32[256,256]{1,0:T(8,128)}, u32[]{:S(2)}) copy-start(f32[256,256]{1,0:T(8,128)} %constant.52.clone.inv_ref) | copy-start | bytes 786436
  74.7 2.9 %copy-start.21 = (f32[256,128]{1,0:T(8,128)S(1)}, f32[256,128]{1,0:T(8,128)}, u32[]{:S(2)}) copy-start(f32[256,128]{1,0:T(8,128)} %copy-done.20) | copy-start | bytes 393220
  77.7 20.6 %copy-start.17 = (f32[16,128,128]{2,1,0:T(8,128)S(1)}, f32[16,128,128]{2,1,0:T(8,128)}, u32[]{:S(2)}) copy-start(f32[16,128,128]{2,1,0:T(8,128)} %copy-done.16) | copy-start | bytes 3145732
  77.7 20.6 %copy-start.19 = (f32[256,128]{1,0:T(8,128)S(1)}, f32[256,128]{1,0:T(8,128)}, u32[]{:S(2)}) copy-start(f32[256,128]{1,0:T(8,128)} %copy-done.18) | copy-start | bytes 393220
  81.1 17.2 %collective-permute-start.6 = (f32[128,512]{1,0:T(8,128)S(1)}, f32[128,512]{1,0:T(8,128)S(1)}, u32[]{:S(2)}, u32[]{:S(2)}) collective-permute-start(f32[128,512]{1,0:T(8,128)S(1)} %make_gates.1.both_ref), channel_id=1, source_target_pairs={{0,16},{16,32},{32,48},{48,64},{64,80},{80,96},{96,112},{112,0},{1... | collective-permute-start | bytes 786440 | tf_op jit(solution)/shard_map/ppermute | solution.py:276
where the time goes:
time: 110 us
  starting transfers between devices  32.9 us (30%)
  waiting for transfers between devices  29.4 us (27%)
  blocking collectives  24.2 us (22%)
  local copies, waits for them, and re-layouts  13.2 us (12%)
  Pallas kernels  9.32 us (8%)
    ppermute x3, waiting for transfers between devices, per_device(): near.append(lax.ppermute(half, 'ctx', moves))  29.4 us
    all_to_all x1, blocking collectives, per_device(): lax.all_to_all(states, 'ctx', 0, 0, tiled=True, axis_index_groups=z_groups)  14.9 us
    all_to_all x1, starting transfers between devices, per_device(): blocks = lax.all_to_all(blocks, 'ctx', 0, 0, tiled=True)  13.3 us
    unnamed x49, local copies, waits for them, and re-layouts  12.3 us
    ppermute x3, starting transfers between devices, per_device(): near.append(lax.ppermute(half, 'ctx', moves))  11 us
    all_to_all x1, blocking collectives, per_device(): lax.all_to_all(packed, 'ctx', 0, 0, tiled=True, axis_index_groups=x_groups)  9.38 us
    pallas_call x6, Pallas kernels, call(): pl.pallas_call(body, out_shape=outs, in_specs=[pl.BlockSpec(memory_space=...  9.32 us
    ppermute x3, starting transfers between devices, per_device(): far.append(lax.ppermute(near[-1], 'ch', swap))  6.22 us
  transfers between devices with their start and end apart: 8, of which 2 were waited for; matrix products, arithmetic and copies ran while one was open for 1% of the time, Pallas kernels for 1%

commit v1 on v0

--- a/solution.py
+++ b/solution.py
@@ -17,7 +17,6 @@
 HALF = 64
 SPAN = 2 * ROWS
 MODES = 16
-SHIFTS = (1, 3, 2)
 
 x_groups = [[x * NZ + z for x in range(NX)] for z in range(NZ)]
 z_groups = [[x * NZ + z for z in range(NZ)] for x in range(NX)]
@@ -61,20 +60,22 @@
     return pltpu.roll(v, HALF, v.ndim - 1)
 
 
-def call(body, outs, name, *args, scratch=(), flops=10**9):
+VMEM, ANY = pl.BlockSpec(memory_space=pltpu.VMEM), pl.BlockSpec(memory_space=pl.ANY)
+
+
+def call(body, outs, *args, scratch=(), flops=10**8, far=0, out_specs=None):
     return pl.pallas_call(
         body,
         out_shape=outs,
-        in_specs=[pl.BlockSpec(memory_space=pltpu.VMEM)] * len(args),
-        out_specs=jax.tree.map(lambda _: pl.BlockSpec(memory_space=pltpu.VMEM), outs),
+        in_specs=[ANY] * far + [VMEM] * (len(args) - far),
+        out_specs=jax.tree.map(lambda _: VMEM, outs) if out_specs is None else out_specs,
         scratch_shapes=scratch,
-        compiler_params=pltpu.CompilerParams(vmem_limit_bytes=8 << 20),
+        compiler_params=pltpu.CompilerParams(vmem_limit_bytes=(60 if far else 16) << 20),
         cost_estimate=pl.CostEstimate(flops=flops, bytes_accessed=flops // 200, transcendentals=0),
-        name=name,
     )(*args)
 
 
-def spread_weights(w_ref, out_ref):
+def spread_weights(w_ref, out_ref, block_ref, sems):
     low = lower_lanes((ROWS, LANES))
     low_half = lower_lanes((HALF, LANES))
     for x in range(NX):
@@ -87,17 +88,20 @@
             both = jnp.where(low, swap_halves(a), v)
             packed = jnp.where(low_half, swap_halves(o[:HALF]), o[HALF:])
         both, packed = both.astype(bf16), packed.astype(bf16)
+        block_ref[x, :ROWS] = both
+        block_ref[x, ROWS:] = packed
         for z in range(NZ):
-            out_ref[x * NZ + z, :ROWS] = both
-            out_ref[x * NZ + z, ROWS:] = packed
-
-
-def build_tables(a_ref, w_ref, taps_ref, fwd_ref, into_ref, out_ref, long_ref, short_ref):
+            pltpu.make_async_copy(block_ref.at[x], out_ref.at[x * NZ + z], sems.at[x * NZ + z]).start()
+    for x in range(NX):
+        for z in range(NZ):
+            pltpu.make_async_copy(block_ref.at[x], out_ref.at[x * NZ + z], sems.at[x * NZ + z]).wait()
+
+
+def build_tables(a_ref, w_ref, taps_ref, fwd_ref, out_ref, long_ref, short_ref):
     t = lax.broadcasted_iota(jnp.int32, (ROWS, LANES), 0).astype(f32)
     impulse = jnp.zeros((ROWS, LANES), f32)
     for m in range(MODES):
         rate, weight = a_ref[m : m + 1, :], w_ref[m : m + 1, :]
-        into_ref[m] = jnp.exp(-rate * (ROWS - 1.0 - t))
         out_ref[m] = weight * jnp.exp(-rate * (t + 1.0))
         impulse = impulse + weight * jnp.exp(-rate * t)
     transform = fwd_ref[:, :ROWS]
@@ -110,22 +114,39 @@
     return lax.div(ctx, NZ), lax.rem(ctx, NZ), lax.rem(ch, NC)
 
 
-def fill_products(tokens_ref, near_refs, far_refs, weight_ref, product_ref):
+def token_copies(refs, bufs, sems):
+    return [pltpu.make_async_copy(r, b, sems.at[k]) for k, (r, b) in enumerate(zip(refs, bufs))]
+
+
+def fill_products(copies, bufs, weights_of, product_ref):
     x, _, core = positions()
-    width = near_refs[0].shape[1]
-    near = pl.ds(pl.multiple_of(core * width, width), width)
-    far = pl.ds(pl.multiple_of((1 - core) * width, width), width)
-    product_ref[x] = jnp.dot(tokens_ref[...], weight_ref[...], preferred_element_type=f32)
-    for shift, near_ref, far_ref in zip(SHIFTS, near_refs, far_refs):
-        product_ref[lax.rem(x + (NX - shift), NX)] = jnp.dot(
-            near_ref[...], weight_ref[near, :], preferred_element_type=f32
-        ) + jnp.dot(far_ref[...], weight_ref[far, :], preferred_element_type=f32)
-
-
-def make_signal(tokens_ref, n0, n1, n2, f0, f1, f2, blocks_ref, into_ref, signal_ref, state_ref, weight_ref, product_ref):
-    for block in range(NX * NZ):
-        weight_ref[ROWS * block : ROWS * (block + 1), :] = blocks_ref[block, :ROWS]
-    fill_products(tokens_ref, (n0, n1, n2), (f0, f1, f2), weight_ref, product_ref)
+    near = lax.rem(x + NX - 1 + 2 * core, NX)
+    far = lax.rem(x + NX + 1 - 2 * core, NX)
+    whole = weights_of(0, NX * NZ)
+    for k, place in ((0, x), (1, near), (2, far)):
+        copies[k].wait()
+        product_ref[place] = jnp.dot(bufs[k][...], whole, preferred_element_type=f32)
+    count = NX * NZ // NC
+    copies[3].wait()
+    total = jnp.dot(bufs[3][...], weights_of(core * count, count), preferred_element_type=f32)
+    copies[4].wait()
+    total = total + jnp.dot(bufs[4][...], weights_of((1 - core) * count, count), preferred_element_type=f32)
+    product_ref[lax.rem(x + 2, NX)] = total
+
+
+def make_signal(t0, t1, t2, t3, t4, blocks_ref, a_ref, signal_ref, state_ref, b0, b1, b2, b3, b4, into_ref, product_ref, sems):
+    bufs = (b0, b1, b2, b3, b4)
+    copies = token_copies((t0, t1, t2, t3, t4), bufs, sems)
+    for copy in copies:
+        copy.start()
+    back = ROWS - 1.0 - lax.broadcasted_iota(jnp.int32, (ROWS, LANES), 0).astype(f32)
+    for m in range(MODES):
+        into_ref[m] = jnp.exp(-a_ref[m : m + 1, :] * back)
+
+    def weights_of(first, count):
+        return blocks_ref[pl.ds(first, count), :ROWS, :].reshape(count * ROWS, LANES)
+
+    fill_products(copies, bufs, weights_of, product_ref)
     low = lower_lanes((ROWS, LANES))
     for pair in range(NX // 2):
         parts = []
@@ -140,14 +161,22 @@
                 state_ref[z, pair * MODES + m : pair * MODES + m + 1, :] = state
 
 
-def make_gates(tokens_ref, n0, n1, n2, f0, f1, f2, blocks_ref, signal_ref, fwd_ref, inv_ref, long_ref, both_ref, weight_ref, product_ref):
+def make_gates(t0, t1, t2, t3, t4, blocks_ref, signal_ref, fwd_ref, inv_ref, long_ref, both_ref, b0, b1, b2, b3, b4, weight_ref, product_ref, sems):
+    bufs = (b0, b1, b2, b3, b4)
+    copies = token_copies((t0, t1, t2, t3, t4), bufs, sems)
+    for copy in copies:
+        copy.start()
     low_half = lower_lanes((HALF, LANES))
     for block in range(NX * NZ):
         packed = blocks_ref[block, ROWS:].astype(f32)
         turned = swap_halves(packed)
-        weight_ref[ROWS * block : ROWS * block + HALF, :] = jnp.where(low_half, packed, turned).astype(bf16)
-        weight_ref[ROWS * block + HALF : ROWS * (block + 1), :] = jnp.where(low_half, turned, packed).astype(bf16)
-    fill_products(tokens_ref, (n0, n1, n2), (f0, f1, f2), weight_ref, product_ref)
+        weight_ref[block, :HALF, :] = jnp.where(low_half, packed, turned).astype(bf16)
+        weight_ref[block, HALF:, :] = jnp.where(low_half, turned, packed).astype(bf16)
+
+    def weights_of(first, count):
+        return weight_ref[pl.ds(first, count)].reshape(count * ROWS, LANES)
+
+    fill_products(copies, bufs, weights_of, product_ref)
     spectrum = dot32(fwd_ref[:, :ROWS], signal_ref[...])
     response = jnp.concatenate([long_ref[...]] * 2, axis=1)
     both_ref[:, : 2 * LANES] = dot32(inv_ref[:ROWS, :], multiply_spectra(spectrum, response))
@@ -226,18 +255,30 @@
     sds = jax.ShapeDtypeStruct
     x = lax.axis_index("ctx") // NZ
     core = lax.axis_index("ch") % NC
-    width = tokens.shape[1] // NC
+    rows, features = tokens.shape
+    width = features // NC
     count = NX * NZ
-    depth = count * ROWS
-    blocks = call(spread_weights, sds((count, ROWS + HALF, LANES), bf16), "spread_weights", projections)
+    wide = lax.axis_size("ch")
+
+    def place(a, b, k):
+        return (a % NX * NZ + b) * wide + k
+
+    outward = [
+        (place(a, b, k), place(a + 1 - 2 * (k % NC), b, k)) for a in range(NX) for b in range(NZ) for k in range(wide)
+    ]
+    swap = [(k, k ^ 1) for k in range(wide)]
+    near = lax.ppermute(tokens, ("ctx", "ch"), outward)
+    blocks = call(
+        spread_weights,
+        sds((count, ROWS + HALF, LANES), bf16),
+        projections,
+        scratch=[pltpu.VMEM((NX, ROWS + HALF, LANES), bf16), pltpu.SemaphoreType.DMA((count,))],
+        out_specs=ANY,
+    )
     blocks = lax.all_to_all(blocks, "ctx", 0, 0, tiled=True)
-    half = lax.dynamic_slice_in_dim(tokens, core * width, width, 1)
-    swap = [(k, k ^ 1) for k in range(lax.axis_size("ch"))]
-    near, far = [], []
-    for shift in SHIFTS:
-        moves = [(a * NZ + b, (a + shift) % NX * NZ + b) for a in range(NX) for b in range(NZ)]
-        near.append(lax.ppermute(half, "ctx", moves))
-        far.append(lax.ppermute(near[-1], "ch", swap))
+    far = lax.ppermute(near, "ch", swap)
+    half = lax.ppermute(lax.dynamic_slice_in_dim(near, core * width, width, 1), ("ctx", "ch"), outward)
+    other = lax.ppermute(half, "ch", swap)
 
     rates = lax.dynamic_slice_in_dim(decay_rates, x * HALF, HALF, 0).T
     weights = lax.dynamic_slice_in_dim(residues, x * HALF, HALF, 0).T * jnp.sqrt(2.0 * rates)
@@ -246,49 +287,38 @@
     forward, inverse = jnp.asarray(real_transform()), jnp.asarray(inverse_transform())
     table = sds((MODES, ROWS, LANES), f32)
     spectrum = sds((SPAN, LANES), f32)
-    into, out, long_spectrum, short_spectrum = call(
-        build_tables, (table, table, spectrum, spectrum), "build_tables", rates, weights, taps, forward
-    )
-    scratch = [pltpu.VMEM((depth, LANES), bf16), pltpu.VMEM((NX, ROWS, LANES), f32)]
-    operands = (tokens, *near, *far, blocks)
+    out, long_spectrum, short_spectrum = call(build_tables, (table, spectrum, spectrum), rates, weights, taps, forward)
+    buffers = [pltpu.VMEM((rows, features), bf16)] * 3 + [pltpu.VMEM((rows, width), bf16)] * 2
+    products = pltpu.VMEM((NX, ROWS, LANES), f32)
+    arrivals = pltpu.SemaphoreType.DMA((5,))
+    operands = (tokens, near, far, half, other, blocks)
     signal, states = call(
         make_signal,
         (sds((ROWS, 2 * LANES), f32), sds((NZ, 2 * MODES, LANES), f32)),
-        "make_signal",
         *operands,
-        into,
-        scratch=scratch,
+        rates,
+        scratch=[*buffers, pltpu.VMEM((MODES, ROWS, LANES), f32), products, arrivals],
+        far=5,
     )
     states = lax.all_to_all(states, "ctx", 0, 0, tiled=True, axis_index_groups=z_groups)
     both = call(
         make_gates,
         sds((ROWS, 4 * LANES), f32),
-        "make_gates",
         *operands,
         signal,
         forward,
         inverse,
         long_spectrum,
-        scratch=scratch,
-        flops=5 * 10**9,
+        scratch=[*buffers, pltpu.VMEM((count, ROWS, LANES), bf16), products, arrivals],
+        far=5,
     )
     onward = [(a * NZ + b, a * NZ + (b + 1) % NZ) for a in range(NX) for b in range(NZ)]
     arrived = lax.ppermute(both, "ctx", onward)
     packed = call(
-        finish,
-        sds((NX, HALF, LANES), bf16),
-        "finish",
-        both,
-        arrived,
-        states,
-        rates,
-        out,
-        forward,
-        inverse,
-        short_spectrum,
+        finish, sds((NX, HALF, LANES), bf16), both, arrived, states, rates, out, forward, inverse, short_spectrum
     )
     packed = lax.all_to_all(packed, "ctx", 0, 0, tiled=True, axis_index_groups=x_groups)
-    return call(unpack_rows, sds((ROWS, 2 * LANES), bf16), "unpack_rows", packed)
+    return call(unpack_rows, sds((ROWS, 2 * LANES), bf16), packed)
 
 
 def solution(mesh):

time: 110 us -> 107 us (0.973)
  the two profiles are of different devices: /device:TPU:32 before, /device:TPU:40 now
where the time goes in v1:
time: 107 us; the launch traced here: 106 us
  waiting for transfers between devices  32.1 us (30%)
  starting transfers between devices  29.2 us (27%)
  blocking collectives  22.4 us (21%)
  Pallas kernels  16.2 us (15%)
  local copies, waits for them, and re-layouts  5.84 us (5%)
    ppermute x1, waiting for transfers between devices, per_device(): near = lax.ppermute(tokens, ('ctx', 'ch'), outward)  24.1 us
    pallas_call x6, Pallas kernels, call(): pl.pallas_call(body, out_shape=outs, in_specs=[ANY] * far + [VMEM] * (len...  16.2 us
    all_to_all x1, blocking collectives, per_device(): lax.all_to_all(states, 'ctx', 0, 0, tiled=True, axis_index_groups=z_groups)  14.4 us
    all_to_all x1, starting transfers between devices, per_device(): blocks = lax.all_to_all(blocks, 'ctx', 0, 0, tiled=True)  13.3 us
    all_to_all x1, blocking collectives, per_device(): lax.all_to_all(packed, 'ctx', 0, 0, tiled=True, axis_index_groups=x_groups)  7.99 us
    ppermute x1, waiting for transfers between devices, per_device(): lax.ppermute(lax.dynamic_slice_in_dim(near, core * width, width, 1), ('ct...  7.7 us
    ppermute x1, starting transfers between devices, per_device(): arrived = lax.ppermute(both, 'ctx', onward)  4.84 us
    unnamed x31, local copies, waits for them, and re-layouts  4.68 us
  transfers between devices with their start and end apart: 6, of which 3 were waited for; matrix products, arithmetic and copies ran while one was open for 2% of the time, Pallas kernels for 1%

profile of v1, /device:TPU:40, one launch (start us, length us, event | category | flops | bytes accessed | tf_op | source)
XLA Modules:
  0.0 106.3 jit_solution(7148719674373918345)
XLA Ops:
  0.0 1.0 copy-done.5
  1.0 1.5 %shard_map.73 = bf16[32,192,128]{2,1,0:T(8,128)(2,1)} custom-call(bf16[3,128,256]{2,1,0:T(8,128)(2,1)S(1)} %copy-done.5), custom_call_target="tpu_custom_call" | custom-call | flops 100000000 | bytes 500000 | tf_op jit(solution)/shard_map/pallas_call | solution.py:67
  2.5 0.0 copy-start.1
  2.5 13.3 %all-to-all-start = ((bf16[32,192,128]{2,1,0:T(8,128)(2,1)}), bf16[32,192,128]{2,1,0:T(8,128)(2,1)S(1)}, u32[]{:S(2)}, u32[]{:S(2)}) async-start(bf16[32,192,128]{2,1,0:T(8,128)(2,1)} %shard_map.73), calls=%async_computation | async-start | bytes 3145728 | tf_op jit(solution)/shard_map/all_to_all | solution.py:278
  15.9 3.7 %collective-permute-start = (bf16[128,4096]{1,0:T(8,128)(2,1)S(1)}, bf16[128,4096]{1,0:T(8,128)(2,1)}, u32[]{:S(2)}, u32[]{:S(2)}) collective-permute-start(bf16[128,4096]{1,0:T(8,128)(2,1)S(1)} %copy-done.10), channel_id=1, source_target_pairs={{0,128},{1,385},{2,130},{3,387},{4,132},{5,389},{6,134},{7,391},{8... | collective-permute-start | bytes 3145736 | tf_op jit(solution)/shard_map/ppermute | solution.py:270
  19.6 24.1 %collective-permute-done.t1 = bf16[128,4096]{1,0:T(8,128)(2,1)} collective-permute-done((bf16[128,4096]{1,0:T(8,128)(2,1)S(1)}, bf16[128,4096]{1,0:T(8,128)(2,1)}, u32[]{:S(2)}, u32[]{:S(2)}) %collective-permute-start) | collective-permute-done | bytes 1048608 | tf_op jit(solution)/shard_map/ppermute | solution.py:270
  43.7 1.1 %constant_dynamic-slice_fusion.1 = bf16[128,2048]{1,0:T(8,128)(2,1)S(1)} fusion(bf16[128,4096]{1,0:T(8,128)(2,1)} %collective-permute-done.t1, s32[]{:T(128)S(6)} %select_n.20), kind=kLoop, calls=%fused_computation.6 | loop fusion | bytes 1048580 | tf_op jit(solution)/shard_map/dynamic_slice | solution.py:280
  44.8 2.2 %collective-permute-start.2 = (bf16[128,2048]{1,0:T(8,128)(2,1)S(1)}, bf16[128,2048]{1,0:T(8,128)(2,1)}, u32[]{:S(2)}, u32[]{:S(2)}) collective-permute-start(bf16[128,2048]{1,0:T(8,128)(2,1)S(1)} %constant_dynamic-slice_fusion.1), channel_id=1, source_target_pairs={{0,128},{1,385},{2,130},{3,387},{4,132},{5,389},{6,134},{7,391},{8... | collective-permute-start | bytes 1572872 | tf_op jit(solution)/shard_map/ppermute | solution.py:280
  47.0 3.3 %collective-permute-start.1 = (bf16[128,4096]{1,0:T(8,128)(2,1)}, bf16[128,4096]{1,0:T(8,128)(2,1)}, u32[]{:S(2)}, u32[]{:S(2)}) collective-permute-start(bf16[128,4096]{1,0:T(8,128)(2,1)} %collective-permute-done.t1), channel_id=1, source_target_pairs={{0,1},{1,0},{2,3},{3,2},{4,5},{5,4},{6,7},{7,6},{8,9},{9,8},{10,11... | collective-permute-start | bytes 3145736 | tf_op jit(solution)/shard_map/ppermute | solution.py:279
  50.3 0.1 copy.9
  50.4 7.7 %collective-permute-done.2.t3 = bf16[128,2048]{1,0:T(8,128)(2,1)} collective-permute-done((bf16[128,2048]{1,0:T(8,128)(2,1)S(1)}, bf16[128,2048]{1,0:T(8,128)(2,1)}, u32[]{:S(2)}, u32[]{:S(2)}) %collective-permute-start.2) | collective-permute-done | bytes 524320 | tf_op jit(solution)/shard_map/ppermute | solution.py:280
  58.1 1.9 %collective-permute-start.3 = (bf16[128,2048]{1,0:T(8,128)(2,1)}, bf16[128,2048]{1,0:T(8,128)(2,1)S(1)}, u32[]{:S(2)}, u32[]{:S(2)}) collective-permute-start(bf16[128,2048]{1,0:T(8,128)(2,1)} %collective-permute-done.2.t3), channel_id=1, source_target_pairs={{0,1},{1,0},{2,3},{3,2},{4,5},{5,4},{6,7},{7,6},{8,9},{9,8},{10,11... | collective-permute-start | bytes 1572872 | tf_op jit(solution)/shard_map/ppermute | solution.py:281
  60.1 0.1 dynamic-slice_bitcast_fusion
  60.1 0.1 pad_maximum_fusion.a_ref
  60.2 0.1 bitcast_multiply_fusion
  60.3 0.1 pad_maximum_fusion.1.w_ref
  60.4 0.1 maximum_convert_fusion.taps_ref
  60.5 0.7 shard_map.75
  61.2 0.6 copy-done.6
  61.9 0.3 collective-permute-done.3.t4
  62.1 0.8 copy-done.11
  63.0 1.2 %copy-done.9 = bf16[32,192,128]{2,1,0:T(8,128)(2,1)} copy-done((bf16[32,192,128]{2,1,0:T(8,128)(2,1)}, bf16[32,192,128]{2,1,0:T(8,128)(2,1)S(1)}, u32[]{:S(2)}) %copy-start.9) | copy-done | bytes 1572888
  64.1 5.5 %shard_map.74 = (f32[128,256]{1,0:T(8,128)}, f32[8,32,128]{2,1,0:T(8,128)}) custom-call(bf16[128,4096]{1,0:T(8,128)(2,1)} %t0.3, bf16[128,4096]{1,0:T(8,128)(2,1)} %collective-permute-done.t1, bf16[128,4096]{1,0:T(8,128)(2,1)} %collective-permute-done.1.t2, bf16[128,2048]{1,0:T(8,128)(2,1)} %collective-permute-done.2.t3, bf16[128,2048]{1,0:T(8,128)(2,1)} %copy-done.11, ...), custom_call_target="tpu_custom_call" | custom-call | flops 100000000 | bytes 500000 | tf_op jit(solution)/shard_map/pallas_call | solution.py:67
  69.6 0.0 copy-start.2
  69.6 0.0 copy-start.3
  69.6 6.4 %shard_map.76.both_ref = f32[128,512]{1,0:T(8,128)} custom-call(bf16[128,4096]{1,0:T(8,128)(2,1)} %t0.3, bf16[128,4096]{1,0:T(8,128)(2,1)} %collective-permute-done.t1, bf16[128,4096]{1,0:T(8,128)(2,1)} %collective-permute-done.1.t2, bf16[128,2048]{1,0:T(8,128)(2,1)} %collective-permute-done.2.t3, bf16[128,2048]{1,0:T(8,128)(2,1)} %copy-done.11, ...), custom_call_target="tpu_custom_call" | custom-call | flops 100000000 | bytes 500000 | tf_op jit(solution)/shard_map/pallas_call | solution.py:67
  76.1 4.8 %collective-permute-start.4 = (f32[128,512]{1,0:T(8,128)}, f32[128,512]{1,0:T(8,128)S(1)}, u32[]{:S(2)}, u32[]{:S(2)}) collective-permute-start(f32[128,512]{1,0:T(8,128)} %shard_map.76.both_ref), channel_id=1, source_target_pairs={{0,16},{16,32},{32,48},{48,64},{64,80},{80,96},{96,112},{112,0},{1... | collective-permute-start | bytes 786440 | tf_op jit(solution)/shard_map/ppermute | solution.py:316
  80.9 14.4 %all_to_all.15.states_ref = f32[8,32,128]{2,1,0:T(8,128)S(1)} all-to-all(f32[8,32,128]{2,1,0:T(8,128)S(1)} %copy-done.12), channel_id=1, replica_groups={{0,16,32,48,64,80,96,112},{128,144,160,176,192,208,224,240},{256,272,28..., dimensions={0} | all-to-all | bytes 262144 | tf_op jit(solution)/shard_map/all_to_all | solution.py:303
  95.3 0.9 copy-done.4
  96.3 1.3 %shard_map.77 = bf16[4,64,128]{2,1,0:T(8,128)(2,1)S(1)} custom-call(f32[128,512]{1,0:T(8,128)S(1)} %copy-done.4, f32[128,512]{1,0:T(8,128)S(1)} %collective-permute-done.4.arrived_ref, f32[8,32,128]{2,1,0:T(8,128)S(1)} %all_to_all.15.states_ref, f32[16,128]{1,0:T(8,128)S(1)} %copy-done.8, f32[16,128,128]{2,1,0:T(8,128)S(1)} %get-tuple-element.13.out_ref, ...), custom_call_target="tpu_custom_call" | custom-call | flops 100000000 | bytes 500000 | tf_op jit(solution)/shard_map/pallas_call | solution.py:67
  97.6 8.0 %all_to_all.16.packed_ref = bf16[4,64,128]{2,1,0:T(8,128)(2,1)S(1)} all-to-all(bf16[4,64,128]{2,1,0:T(8,128)(2,1)S(1)} %shard_map.77), channel_id=1, replica_groups={{0,128,256,384},{16,144,272,400},{32,160,288,416},{48,176,304,432},{64,..., dimensions={0} | all-to-all | bytes 131072 | tf_op jit(solution)/shard_map/all_to_all | solution.py:320
  105.6 0.7 shard_map.78
  (26 shorter events, 0.1 us)
Async XLA Ops:
  0.0 50.3 %copy-start = (bf16[256,128]{1,0:T(8,128)(2,1)S(1)}, bf16[256,128]{1,0:T(8,128)(2,1)}, u32[]{:S(2)}) copy-start(bf16[256,128]{1,0:T(8,128)(2,1)} %param.11) | copy-start | bytes 196612
  0.0 1.0 copy-start.5
  2.5 13.4 %copy-start.10 = (bf16[128,4096]{1,0:T(8,128)(2,1)S(1)}, bf16[128,4096]{1,0:T(8,128)(2,1)}, u32[]{:S(2)}) copy-start(bf16[128,4096]{1,0:T(8,128)(2,1)} %t0.3) | copy-start | bytes 3145732
  2.5 57.5 %copy-start.13 = (f32[256,16]{0,1:T(8,128)S(1)}, f32[256,16]{0,1:T(8,128)}, u32[]{:S(2)}) copy-start(f32[256,16]{0,1:T(8,128)} %param.9) | copy-start | bytes 49156
  2.5 57.7 %copy-start.14 = (f32[256,16]{0,1:T(8,128)S(1)}, f32[256,16]{0,1:T(8,128)}, u32[]{:S(2)}) copy-start(f32[256,16]{0,1:T(8,128)} %param.10) | copy-start | bytes 49156
  2.5 57.9 %copy-start.1 = (f32[256,256]{1,0:T(8,128)S(1)}, f32[256,256]{1,0:T(8,128)}, u32[]{:S(2)}) copy-start(f32[256,256]{1,0:T(8,128)} %constant.51.clone.fwd_ref) | copy-start | bytes 786436
  2.5 60.4 %all-to-all-start = ((bf16[32,192,128]{2,1,0:T(8,128)(2,1)}), bf16[32,192,128]{2,1,0:T(8,128)(2,1)S(1)}, u32[]{:S(2)}, u32[]{:S(2)}) async-start(bf16[32,192,128]{2,1,0:T(8,128)(2,1)} %shard_map.73), calls=%async_computation | async-start | bytes 3145728 | tf_op jit(solution)/shard_map/all_to_all | solution.py:278
  15.9 27.9 %collective-permute-start = (bf16[128,4096]{1,0:T(8,128)(2,1)S(1)}, bf16[128,4096]{1,0:T(8,128)(2,1)}, u32[]{:S(2)}, u32[]{:S(2)}) collective-permute-start(bf16[128,4096]{1,0:T(8,128)(2,1)S(1)} %copy-done.10), channel_id=1, source_target_pairs={{0,128},{1,385},{2,130},{3,387},{4,132},{5,389},{6,134},{7,391},{8... | collective-permute-start | bytes 3145736 | tf_op jit(solution)/shard_map/ppermute | solution.py:270
  44.8 13.3 %collective-permute-start.2 = (bf16[128,2048]{1,0:T(8,128)(2,1)S(1)}, bf16[128,2048]{1,0:T(8,128)(2,1)}, u32[]{:S(2)}, u32[]{:S(2)}) collective-permute-start(bf16[128,2048]{1,0:T(8,128)(2,1)S(1)} %constant_dynamic-slice_fusion.1), channel_id=1, source_target_pairs={{0,128},{1,385},{2,130},{3,387},{4,132},{5,389},{6,134},{7,391},{8... | collective-permute-start | bytes 1572872 | tf_op jit(solution)/shard_map/ppermute | solution.py:280
  47.0 15.9 %collective-permute-start.1 = (bf16[128,4096]{1,0:T(8,128)(2,1)}, bf16[128,4096]{1,0:T(8,128)(2,1)}, u32[]{:S(2)}, u32[]{:S(2)}) collective-permute-start(bf16[128,4096]{1,0:T(8,128)(2,1)} %collective-permute-done.t1), channel_id=1, source_target_pairs={{0,1},{1,0},{2,3},{3,2},{4,5},{5,4},{6,7},{7,6},{8,9},{9,8},{10,11... | collective-permute-start | bytes 3145736 | tf_op jit(solution)/shard_map/ppermute | solution.py:279
  58.1 4.0 %collective-permute-start.3 = (bf16[128,2048]{1,0:T(8,128)(2,1)}, bf16[128,2048]{1,0:T(8,128)(2,1)S(1)}, u32[]{:S(2)}, u32[]{:S(2)}) collective-permute-start(bf16[128,2048]{1,0:T(8,128)(2,1)} %collective-permute-done.2.t3), channel_id=1, source_target_pairs={{0,1},{1,0},{2,3},{3,2},{4,5},{5,4},{6,7},{7,6},{8,9},{9,8},{10,11... | collective-permute-start | bytes 1572872 | tf_op jit(solution)/shard_map/ppermute | solution.py:281
  60.2 2.7 %copy-start.7 = (f32[16,128]{1,0:T(8,128)}, f32[16,128]{1,0:T(8,128)S(1)}, u32[]{:S(2)}) copy-start(f32[16,128]{1,0:T(8,128)S(1)} %pad_maximum_fusion.a_ref) | copy-start | bytes 24580
  61.2 0.7 copy-start.6
  62.1 0.8 copy-start.11
  63.0 1.2 %copy-start.9 = (bf16[32,192,128]{2,1,0:T(8,128)(2,1)}, bf16[32,192,128]{2,1,0:T(8,128)(2,1)S(1)}, u32[]{:S(2)}) copy-start(bf16[32,192,128]{2,1,0:T(8,128)(2,1)S(1)} %all-to-all-done.blocks_ref) | copy-start | bytes 4718596
  69.6 11.3 %copy-start.12 = (f32[8,32,128]{2,1,0:T(8,128)S(1)}, f32[8,32,128]{2,1,0:T(8,128)}, u32[]{:S(2)}) copy-start(f32[8,32,128]{2,1,0:T(8,128)} %get-tuple-element.12) | copy-start | bytes 393220
  69.6 25.7 %copy-start.2 = (f32[256,256]{1,0:T(8,128)S(1)}, f32[256,256]{1,0:T(8,128)}, u32[]{:S(2)}) copy-start(f32[256,256]{1,0:T(8,128)} %constant.51.clone.fwd_ref) | copy-start | bytes 786436
  69.6 25.7 %copy-start.3 = (f32[256,256]{1,0:T(8,128)S(1)}, f32[256,256]{1,0:T(8,128)}, u32[]{:S(2)}) copy-start(f32[256,256]{1,0:T(8,128)} %constant.52.clone.inv_ref) | copy-start | bytes 786436
  69.6 25.7 %copy-start.8 = (f32[16,128]{1,0:T(8,128)S(1)}, f32[16,128]{1,0:T(8,128)}, u32[]{:S(2)}) copy-start(f32[16,128]{1,0:T(8,128)} %copy-done.7) | copy-start | bytes 24580
  76.1 19.2 %collective-permute-start.4 = (f32[128,512]{1,0:T(8,128)}, f32[128,512]{1,0:T(8,128)S(1)}, u32[]{:S(2)}, u32[]{:S(2)}) collective-permute-start(f32[128,512]{1,0:T(8,128)} %shard_map.76.both_ref), channel_id=1, source_target_pairs={{0,16},{16,32},{32,48},{48,64},{64,80},{80,96},{96,112},{112,0},{1... | collective-permute-start | bytes 786440 | tf_op jit(solution)/shard_map/ppermute | solution.py:316
  95.3 1.0 copy-start.4

commit v2 on v1

--- a/solution.py
+++ b/solution.py
@@ -114,76 +114,91 @@
     return lax.div(ctx, NZ), lax.rem(ctx, NZ), lax.rem(ch, NC)
 
 
-def token_copies(refs, bufs, sems):
-    return [pltpu.make_async_copy(r, b, sems.at[k]) for k, (r, b) in enumerate(zip(refs, bufs))]
-
-
-def fill_products(copies, bufs, weights_of, product_ref):
+PARTS = 4
+
+
+def project(t0, t1, t2, t3, t4, blocks_ref, a_ref, streams_ref, state_ref, tokens_ref, arrived_ref, wide_ref, into_ref, product_ref, sems, block_sems):
     x, _, core = positions()
     near = lax.rem(x + NX - 1 + 2 * core, NX)
     far = lax.rem(x + NX + 1 - 2 * core, NX)
-    whole = weights_of(0, NX * NZ)
-    for k, place in ((0, x), (1, near), (2, far)):
-        copies[k].wait()
-        product_ref[place] = jnp.dot(bufs[k][...], whole, preferred_element_type=f32)
-    count = NX * NZ // NC
-    copies[3].wait()
-    total = jnp.dot(bufs[3][...], weights_of(core * count, count), preferred_element_type=f32)
-    copies[4].wait()
-    total = total + jnp.dot(bufs[4][...], weights_of((1 - core) * count, count), preferred_element_type=f32)
-    product_ref[lax.rem(x + 2, NX)] = total
-
-
-def make_signal(t0, t1, t2, t3, t4, blocks_ref, a_ref, signal_ref, state_ref, b0, b1, b2, b3, b4, into_ref, product_ref, sems):
-    bufs = (b0, b1, b2, b3, b4)
-    copies = token_copies((t0, t1, t2, t3, t4), bufs, sems)
-    for copy in copies:
-        copy.start()
+    across = lax.rem(x + 2, NX)
+    part = t0.shape[1] // PARTS
+    share = NX * NZ // PARTS
+
+    def rows_of(k):
+        return pl.ds(pl.multiple_of(k * ROWS, ROWS), ROWS)
+
+    def block_copy(j):
+        at = pl.ds(j * share, share)
+        return pltpu.make_async_copy(blocks_ref.at[at], arrived_ref.at[at], block_sems.at[j])
+
+    def token_copies(j):
+        at = pl.ds(j * part, part)
+        found = [
+            pltpu.make_async_copy(ref.at[:, at], tokens_ref.at[rows_of(k), at], sems.at[i, j])
+            for i, (ref, k) in enumerate(((t0, x), (t1, near), (t2, far)))
+        ]
+        half = PARTS // NC
+        inner = pl.ds((j % half) * part, part)
+        mine = (j // half) == core
+        return found, mine, [
+            pltpu.make_async_copy(ref.at[:, inner], tokens_ref.at[rows_of(across), at], sems.at[3, j]) for ref in (t3, t4)
+        ]
+
+    plans = [token_copies(j) for j in range(PARTS)]
+    for j in range(PARTS):
+        block_copy(j).start()
+        found, mine, (first, second) = plans[j]
+        for copy in found:
+            copy.start()
+        pl.when(mine)(first.start)
+        pl.when(jnp.logical_not(mine))(second.start)
     back = ROWS - 1.0 - lax.broadcasted_iota(jnp.int32, (ROWS, LANES), 0).astype(f32)
     for m in range(MODES):
         into_ref[m] = jnp.exp(-a_ref[m : m + 1, :] * back)
-
-    def weights_of(first, count):
-        return blocks_ref[pl.ds(first, count), :ROWS, :].reshape(count * ROWS, LANES)
-
-    fill_products(copies, bufs, weights_of, product_ref)
+    low_half = lower_lanes((HALF, LANES))
+    for j in range(PARTS):
+        block_copy(j).wait()
+        for block in range(j * share, (j + 1) * share):
+            top, bottom = pl.ds(ROWS * block, HALF), pl.ds(ROWS * block + HALF, HALF)
+            wide_ref[pl.ds(ROWS * block, ROWS), :LANES] = arrived_ref[block, :ROWS]
+            packed = arrived_ref[block, ROWS:].astype(f32)
+            turned = swap_halves(packed)
+            wide_ref[top, LANES:] = jnp.where(low_half, packed, turned).astype(bf16)
+            wide_ref[bottom, LANES:] = jnp.where(low_half, turned, packed).astype(bf16)
+        found, _, (first, _) = plans[j]
+        for copy in found:
+            copy.wait()
+        first.wait()
+        at = slice(j * part, (j + 1) * part)
+        term = jnp.dot(tokens_ref[:, at], wide_ref[at, :], preferred_element_type=f32)
+        product_ref[...] = term if j == 0 else product_ref[...] + term
     low = lower_lanes((ROWS, LANES))
     for pair in range(NX // 2):
-        parts = []
-        for chunk in (2 * pair, 2 * pair + 1):
-            both = product_ref[chunk].astype(bf16).astype(f32)
-            parts.append(both * swap_halves(both))
-        signal = jnp.where(low, parts[0], parts[1])
-        signal_ref[:, LANES * pair : LANES * (pair + 1)] = signal
+        lanes = slice(LANES * pair, LANES * (pair + 1))
+        chunks = [slice(ROWS * k, ROWS * (k + 1)) for k in (2 * pair, 2 * pair + 1)]
+        a, b = (product_ref[k, :LANES].astype(bf16).astype(f32) for k in chunks)
+        turned_a, turned_b = swap_halves(a), swap_halves(b)
+        gate_in, values = jnp.where(low, a, turned_b), jnp.where(low, turned_a, b)
+        gate_out = jnp.where(low, product_ref[chunks[0], LANES:], product_ref[chunks[1], LANES:])
+        signal = gate_in * values
+        for k, value in enumerate((gate_in, values, gate_out)):
+            streams_ref[k, :, lanes] = value.astype(bf16)
         for m in range(MODES):
             state = jnp.sum(signal * into_ref[m], axis=0, keepdims=True)
             for z in range(NZ):
                 state_ref[z, pair * MODES + m : pair * MODES + m + 1, :] = state
 
 
-def make_gates(t0, t1, t2, t3, t4, blocks_ref, signal_ref, fwd_ref, inv_ref, long_ref, both_ref, b0, b1, b2, b3, b4, weight_ref, product_ref, sems):
-    bufs = (b0, b1, b2, b3, b4)
-    copies = token_copies((t0, t1, t2, t3, t4), bufs, sems)
-    for copy in copies:
-        copy.start()
-    low_half = lower_lanes((HALF, LANES))
-    for block in range(NX * NZ):
-        packed = blocks_ref[block, ROWS:].astype(f32)
-        turned = swap_halves(packed)
-        weight_ref[block, :HALF, :] = jnp.where(low_half, packed, turned).astype(bf16)
-        weight_ref[block, HALF:, :] = jnp.where(low_half, turned, packed).astype(bf16)
-
-    def weights_of(first, count):
-        return weight_ref[pl.ds(first, count)].reshape(count * ROWS, LANES)
-
-    fill_products(copies, bufs, weights_of, product_ref)
-    spectrum = dot32(fwd_ref[:, :ROWS], signal_ref[...])
+def filter_inside(streams_ref, fwd_ref, inv_ref, long_ref):
+    signal = streams_ref[0].astype(f32) * streams_ref[1].astype(f32)
+    spectrum = dot32(fwd_ref[:, :ROWS], signal)
     response = jnp.concatenate([long_ref[...]] * 2, axis=1)
-    both_ref[:, : 2 * LANES] = dot32(inv_ref[:ROWS, :], multiply_spectra(spectrum, response))
-    low = lower_lanes((ROWS, LANES))
-    for pair in range(NX // 2):
-        gate = jnp.where(low, product_ref[2 * pair], product_ref[2 * pair + 1])
-        both_ref[:, LANES * (2 + pair) : LANES * (3 + pair)] = gate.astype(bf16).astype(f32)
+    return dot32(inv_ref[:ROWS, :], multiply_spectra(spectrum, response))
+
+
+def filter_chunks(streams_ref, fwd_ref, inv_ref, long_ref, local_ref):
+    local_ref[...] = filter_inside(streams_ref, fwd_ref, inv_ref, long_ref)
 
 
 def carry_in(states_ref, a_ref, z):
@@ -212,22 +227,23 @@
     return [before[0] + decay_here * first, before[1] + decay_here * second]
 
 
-def gate_rows(both_ref, carries, out_ref):
+def gate_rows(streams_ref, local, carries, out_ref):
     parts = []
     for pair in range(NX // 2):
-        value = both_ref[:, LANES * pair : LANES * (pair + 1)]
+        lanes = slice(LANES * pair, LANES * (pair + 1))
+        value = local[:, lanes]
         for m in range(MODES):
             value = value + out_ref[m] * carries[pair][m : m + 1, :]
-        gate = both_ref[:, LANES * (2 + pair) : LANES * (3 + pair)]
-        parts.append((gate * value).astype(bf16).astype(f32))
+        parts.append((streams_ref[2, :, lanes].astype(f32) * value).astype(bf16).astype(f32))
     return parts
 
 
-def finish(both_ref, arrived_ref, states_ref, a_ref, out_ref, fwd_ref, inv_ref, short_ref, packed_ref):
+def finish(streams_ref, local_ref, arrived_ref, states_ref, a_ref, out_ref, fwd_ref, inv_ref, long_ref, short_ref, packed_ref):
     _, z, _ = positions()
     low = lower_lanes((ROWS, LANES))
-    own = gate_rows(both_ref, carry_in(states_ref, a_ref, z), out_ref)
-    arrived = gate_rows(arrived_ref, carry_in(states_ref, a_ref, lax.rem(z + NZ - 1, NZ)), out_ref)
+    before = filter_inside(arrived_ref, fwd_ref, inv_ref, long_ref)
+    own = gate_rows(streams_ref, local_ref[...], carry_in(states_ref, a_ref, z), out_ref)
+    arrived = gate_rows(arrived_ref, before, carry_in(states_ref, a_ref, lax.rem(z + NZ - 1, NZ)), out_ref)
     turned = [swap_halves(v) for v in arrived]
     shifted = [jnp.where(low, 0.0, turned[0]), jnp.where(low, turned[0], turned[1])]
     previous = jnp.concatenate([jnp.where(z == 0, s, a) for s, a in zip(shifted, arrived)], axis=1)
@@ -288,34 +304,44 @@
     table = sds((MODES, ROWS, LANES), f32)
     spectrum = sds((SPAN, LANES), f32)
     out, long_spectrum, short_spectrum = call(build_tables, (table, spectrum, spectrum), rates, weights, taps, forward)
-    buffers = [pltpu.VMEM((rows, features), bf16)] * 3 + [pltpu.VMEM((rows, width), bf16)] * 2
-    products = pltpu.VMEM((NX, ROWS, LANES), f32)
-    arrivals = pltpu.SemaphoreType.DMA((5,))
-    operands = (tokens, near, far, half, other, blocks)
-    signal, states = call(
-        make_signal,
-        (sds((ROWS, 2 * LANES), f32), sds((NZ, 2 * MODES, LANES), f32)),
-        *operands,
+    streams, states = call(
+        project,
+        (sds((3, ROWS, 2 * LANES), bf16), sds((NZ, 2 * MODES, LANES), f32)),
+        tokens,
+        near,
+        far,
+        half,
+        other,
+        blocks,
         rates,
-        scratch=[*buffers, pltpu.VMEM((MODES, ROWS, LANES), f32), products, arrivals],
-        far=5,
+        scratch=[
+            pltpu.VMEM((NX * rows, features), bf16),
+            pltpu.VMEM((count, ROWS + HALF, LANES), bf16),
+            pltpu.VMEM((features, 2 * LANES), bf16),
+            pltpu.VMEM((MODES, ROWS, LANES), f32),
+            pltpu.VMEM((NX * rows, 2 * LANES), f32),
+            pltpu.SemaphoreType.DMA((4, PARTS)),
+            pltpu.SemaphoreType.DMA((PARTS,)),
+        ],
+        far=6,
     )
     states = lax.all_to_all(states, "ctx", 0, 0, tiled=True, axis_index_groups=z_groups)
-    both = call(
-        make_gates,
-        sds((ROWS, 4 * LANES), f32),
-        *operands,
-        signal,
+    onward = [(a * NZ + b, a * NZ + (b + 1) % NZ) for a in range(NX) for b in range(NZ)]
+    arrived = lax.ppermute(streams, "ctx", onward)
+    local = call(filter_chunks, sds((ROWS, 2 * LANES), f32), streams, forward, inverse, long_spectrum)
+    packed = call(
+        finish,
+        sds((NX, HALF, LANES), bf16),
+        streams,
+        local,
+        arrived,
+        states,
+        rates,
+        out,
         forward,
         inverse,
         long_spectrum,
-        scratch=[*buffers, pltpu.VMEM((count, ROWS, LANES), bf16), products, arrivals],
-        far=5,
-    )
-    onward = [(a * NZ + b, a * NZ + (b + 1) % NZ) for a in range(NX) for b in range(NZ)]
-    arrived = lax.ppermute(both, "ctx", onward)
-    packed = call(
-        finish, sds((NX, HALF, LANES), bf16), both, arrived, states, rates, out, forward, inverse, short_spectrum
+        short_spectrum,
     )
     packed = lax.all_to_all(packed, "ctx", 0, 0, tiled=True, axis_index_groups=x_groups)
     return call(unpack_rows, sds((ROWS, 2 * LANES), bf16), packed)

time: 107 us -> 99.6 us (0.931)
  the two profiles are of different devices: /device:TPU:40 before, /device:TPU:48 now
where the time goes in v2:
time: 99.6 us; the launch traced here: 99 us
  waiting for transfers between devices  39.9 us (40%)
  starting transfers between devices  34 us (34%)
  Pallas kernels  13 us (13%)
  blocking collectives  7.99 us (8%)
  local copies, waits for them, and re-layouts  2.97 us (3%)
    ppermute x1, waiting for transfers between devices, per_device(): near = lax.ppermute(tokens, ('ctx', 'ch'), outward)  24.1 us
    all_to_all x1, starting transfers between devices, per_device(): blocks = lax.all_to_all(blocks, 'ctx', 0, 0, tiled=True)  13.4 us
    pallas_call x6, Pallas kernels, call(): pl.pallas_call(body, out_shape=outs, in_specs=[ANY] * far + [VMEM] * (len...  13 us
    ppermute x1, waiting for transfers between devices, per_device(): lax.ppermute(lax.dynamic_slice_in_dim(near, core * width, width, 1), ('ct...  8.5 us
    all_to_all x1, blocking collectives, per_device(): lax.all_to_all(packed, 'ctx', 0, 0, tiled=True, axis_index_groups=x_groups)  7.99 us
    all_to_all x1, waiting for transfers between devices, per_device(): lax.all_to_all(states, 'ctx', 0, 0, tiled=True, axis_index_groups=z_groups)  6.46 us
    all_to_all x1, starting transfers between devices, per_device(): lax.all_to_all(states, 'ctx', 0, 0, tiled=True, axis_index_groups=z_groups)  4.93 us
    ppermute x1, starting transfers between devices, per_device(): arrived = lax.ppermute(streams, 'ctx', onward)  4.5 us
  transfers between devices with their start and end apart: 7, of which 4 were waited for; matrix products, arithmetic and copies ran while one was open for 1% of the time, Pallas kernels for 2%

profile of v2, /device:TPU:48, one launch (start us, length us, event | category | flops | bytes accessed | tf_op | source)
XLA Modules:
  0.0 99.0 jit_solution(11778730982171250096)
XLA Ops:
  0.0 1.0 copy-done.5
  1.0 1.5 %shard_map.73 = bf16[32,192,128]{2,1,0:T(8,128)(2,1)} custom-call(bf16[3,128,256]{2,1,0:T(8,128)(2,1)S(1)} %copy-done.5), custom_call_target="tpu_custom_call" | custom-call | flops 100000000 | bytes 500000 | tf_op jit(solution)/shard_map/pallas_call | solution.py:67
  2.5 0.0 copy-start.8
  2.5 0.0 copy-start.11
  2.5 0.0 copy-start.12
  2.5 13.4 %all-to-all-start = ((bf16[32,192,128]{2,1,0:T(8,128)(2,1)}), bf16[32,192,128]{2,1,0:T(8,128)(2,1)}, u32[]{:S(2)}, u32[]{:S(2)}) async-start(bf16[32,192,128]{2,1,0:T(8,128)(2,1)} %shard_map.73), calls=%async_computation | async-start | bytes 3145728 | tf_op jit(solution)/shard_map/all_to_all | solution.py:294
  16.0 3.6 %collective-permute-start = (bf16[128,4096]{1,0:T(8,128)(2,1)S(1)}, bf16[128,4096]{1,0:T(8,128)(2,1)S(1)}, u32[]{:S(2)}, u32[]{:S(2)}) collective-permute-start(bf16[128,4096]{1,0:T(8,128)(2,1)S(1)} %copy-done.8), channel_id=1, source_target_pairs={{0,128},{1,385},{2,130},{3,387},{4,132},{5,389},{6,134},{7,391},{8... | collective-permute-start | bytes 3145736 | tf_op jit(solution)/shard_map/ppermute | solution.py:286
  19.6 24.1 %collective-permute-done.t1 = bf16[128,4096]{1,0:T(8,128)(2,1)S(1)} collective-permute-done((bf16[128,4096]{1,0:T(8,128)(2,1)S(1)}, bf16[128,4096]{1,0:T(8,128)(2,1)S(1)}, u32[]{:S(2)}, u32[]{:S(2)}) %collective-permute-start) | collective-permute-done | bytes 1048608 | tf_op jit(solution)/shard_map/ppermute | solution.py:286
  43.8 2.1 %collective-permute-start.2 = (bf16[128,2048]{1,0:T(8,128)(2,1)S(1)}, bf16[128,2048]{1,0:T(8,128)(2,1)S(1)}, u32[]{:S(2)}, u32[]{:S(2)}) collective-permute-start(bf16[128,2048]{1,0:T(8,128)(2,1)S(1)} %constant_dynamic-slice_fusion.1), channel_id=1, source_target_pairs={{0,128},{1,385},{2,130},{3,387},{4,132},{5,389},{6,134},{7,391},{8... | collective-permute-start | bytes 1572872 | tf_op jit(solution)/shard_map/ppermute | solution.py:296
  45.9 3.5 %collective-permute-start.1 = (bf16[128,4096]{1,0:T(8,128)(2,1)S(1)}, bf16[128,4096]{1,0:T(8,128)(2,1)}, u32[]{:S(2)}, u32[]{:S(2)}) collective-permute-start(bf16[128,4096]{1,0:T(8,128)(2,1)S(1)} %collective-permute-done.t1), channel_id=1, source_target_pairs={{0,1},{1,0},{2,3},{3,2},{4,5},{5,4},{6,7},{7,6},{8,9},{9,8},{10,11... | collective-permute-start | bytes 3145736 | tf_op jit(solution)/shard_map/ppermute | solution.py:295
  49.4 8.5 %collective-permute-done.2.t3 = bf16[128,2048]{1,0:T(8,128)(2,1)S(1)} collective-permute-done((bf16[128,2048]{1,0:T(8,128)(2,1)S(1)}, bf16[128,2048]{1,0:T(8,128)(2,1)S(1)}, u32[]{:S(2)}, u32[]{:S(2)}) %collective-permute-start.2) | collective-permute-done | bytes 524320 | tf_op jit(solution)/shard_map/ppermute | solution.py:296
  57.9 1.9 %collective-permute-start.3 = (bf16[128,2048]{1,0:T(8,128)(2,1)S(1)}, bf16[128,2048]{1,0:T(8,128)(2,1)S(1)}, u32[]{:S(2)}, u32[]{:S(2)}) collective-permute-start(bf16[128,2048]{1,0:T(8,128)(2,1)S(1)} %collective-permute-done.2.t3), channel_id=1, source_target_pairs={{0,1},{1,0},{2,3},{3,2},{4,5},{5,4},{6,7},{7,6},{8,9},{9,8},{10,11... | collective-permute-start | bytes 1572872 | tf_op jit(solution)/shard_map/ppermute | solution.py:297
  59.8 0.1 copy.9
  60.0 0.1 dynamic-slice_bitcast_fusion
  60.0 0.7 pad_maximum_fusion.a_ref
  60.7 0.1 bitcast_multiply_fusion
  60.8 0.0 copy-start.6
  60.8 0.0 copy-start.2
  60.9 0.8 collective-permute-done.3.t4
  61.7 0.8 copy-done.10
  62.5 7.1 %shard_map.74 = (bf16[3,128,256]{2,1,0:T(8,128)(2,1)}, f32[8,32,128]{2,1,0:T(8,128)}) custom-call(bf16[128,4096]{1,0:T(8,128)(2,1)} %t0.1, bf16[128,4096]{1,0:T(8,128)(2,1)} %copy-done.7, bf16[128,4096]{1,0:T(8,128)(2,1)} %collective-permute-done.1.t2, bf16[128,2048]{1,0:T(8,128)(2,1)} %copy-done.9, bf16[128,2048]{1,0:T(8,128)(2,1)} %copy-done.10, ...), custom_call_target="tpu_custom_call" | custom-call | flops 100000000 | bytes 500000 | tf_op jit(solution)/shard_map/pallas_call | solution.py:67
  69.6 4.5 %collective-permute-start.4 = (bf16[3,128,256]{2,1,0:T(8,128)(2,1)}, bf16[3,128,256]{2,1,0:T(8,128)(2,1)S(1)}, u32[]{:S(2)}, u32[]{:S(2)}) collective-permute-start(bf16[3,128,256]{2,1,0:T(8,128)(2,1)} %get-tuple-element.10.streams_ref), channel_id=1, source_target_pairs={{0,16},{16,32},{32,48},{48,64},{64,80},{80,96},{96,112},{112,0},{1... | collective-permute-start | bytes 589832 | tf_op jit(solution)/shard_map/ppermute | solution.py:330
  74.1 4.9 %all-to-all-start.1 = ((f32[8,32,128]{2,1,0:T(8,128)}), f32[8,32,128]{2,1,0:T(8,128)S(1)}, u32[]{:S(2)}, u32[]{:S(2)}) async-start(f32[8,32,128]{2,1,0:T(8,128)} %get-tuple-element.12), calls=%async_computation.1 | async-start | bytes 262144 | tf_op jit(solution)/shard_map/all_to_all | solution.py:328
  79.0 0.1 pad_maximum_fusion.1.w_ref
  79.1 0.1 maximum_convert_fusion.taps_ref
  79.2 0.7 shard_map.75
  80.0 0.9 copy-done.3
  80.9 0.8 shard_map.76.local_ref
  81.7 6.5 %all-to-all-done.1.states_ref = f32[8,32,128]{2,1,0:T(8,128)S(1)} async-done(((f32[8,32,128]{2,1,0:T(8,128)}), f32[8,32,128]{2,1,0:T(8,128)S(1)}, u32[]{:S(2)}, u32[]{:S(2)}) %all-to-all-start.1) | async-done | bytes 131104 | tf_op jit(solution)/shard_map/all_to_all | solution.py:328
  88.2 2.1 %shard_map.77 = bf16[4,64,128]{2,1,0:T(8,128)(2,1)S(1)} custom-call(bf16[3,128,256]{2,1,0:T(8,128)(2,1)S(1)} %copy-done.4, f32[128,256]{1,0:T(8,128)S(1)} %shard_map.76.local_ref, bf16[3,128,256]{2,1,0:T(8,128)(2,1)S(1)} %collective-permute-done.4.arrived_ref, f32[8,32,128]{2,1,0:T(8,128)S(1)} %all-to-all-done.1.states_ref, f32[16,128]{1,0:T(8,128)S(1)} %copy-done.6, ...), custom_call_target="tpu_custom_call" | custom-call | flops 100000000 | bytes 500000 | tf_op jit(solution)/shard_map/pallas_call | solution.py:67
  90.3 8.0 %all_to_all.15.packed_ref = bf16[4,64,128]{2,1,0:T(8,128)(2,1)S(1)} all-to-all(bf16[4,64,128]{2,1,0:T(8,128)(2,1)S(1)} %shard_map.77), channel_id=1, replica_groups={{0,128,256,384},{16,144,272,400},{32,160,288,416},{48,176,304,432},{64,..., dimensions={0} | all-to-all | bytes 131072 | tf_op jit(solution)/shard_map/all_to_all | solution.py:346
  98.3 0.7 shard_map.78
  (23 shorter events, 0.1 us)
Async XLA Ops:
  0.0 59.8 %copy-start = (bf16[256,128]{1,0:T(8,128)(2,1)S(1)}, bf16[256,128]{1,0:T(8,128)(2,1)}, u32[]{:S(2)}) copy-start(bf16[256,128]{1,0:T(8,128)(2,1)} %param.11) | copy-start | bytes 196612
  0.0 1.0 copy-start.5
  2.5 13.5 %copy-start.8 = (bf16[128,4096]{1,0:T(8,128)(2,1)S(1)}, bf16[128,4096]{1,0:T(8,128)(2,1)}, u32[]{:S(2)}) copy-start(bf16[128,4096]{1,0:T(8,128)(2,1)} %t0.1) | copy-start | bytes 3145732
  2.5 57.5 %copy-start.11 = (f32[256,16]{0,1:T(8,128)S(1)}, f32[256,16]{0,1:T(8,128)}, u32[]{:S(2)}) copy-start(f32[256,16]{0,1:T(8,128)} %param.9) | copy-start | bytes 49156
  2.5 58.2 %copy-start.12 = (f32[256,16]{0,1:T(8,128)S(1)}, f32[256,16]{0,1:T(8,128)}, u32[]{:S(2)}) copy-start(f32[256,16]{0,1:T(8,128)} %param.10) | copy-start | bytes 49156
  2.5 59.2 %all-to-all-start = ((bf16[32,192,128]{2,1,0:T(8,128)(2,1)}), bf16[32,192,128]{2,1,0:T(8,128)(2,1)}, u32[]{:S(2)}, u32[]{:S(2)}) async-start(bf16[32,192,128]{2,1,0:T(8,128)(2,1)} %shard_map.73), calls=%async_computation | async-start | bytes 3145728 | tf_op jit(solution)/shard_map/all_to_all | solution.py:294
  16.0 27.8 %collective-permute-start = (bf16[128,4096]{1,0:T(8,128)(2,1)S(1)}, bf16[128,4096]{1,0:T(8,128)(2,1)S(1)}, u32[]{:S(2)}, u32[]{:S(2)}) collective-permute-start(bf16[128,4096]{1,0:T(8,128)(2,1)S(1)} %copy-done.8), channel_id=1, source_target_pairs={{0,128},{1,385},{2,130},{3,387},{4,132},{5,389},{6,134},{7,391},{8... | collective-permute-start | bytes 3145736 | tf_op jit(solution)/shard_map/ppermute | solution.py:286
  43.8 17.9 %copy-start.7 = (bf16[128,4096]{1,0:T(8,128)(2,1)}, bf16[128,4096]{1,0:T(8,128)(2,1)S(1)}, u32[]{:S(2)}) copy-start(bf16[128,4096]{1,0:T(8,128)(2,1)S(1)} %collective-permute-done.t1) | copy-start | bytes 3145732
  43.8 14.1 %collective-permute-start.2 = (bf16[128,2048]{1,0:T(8,128)(2,1)S(1)}, bf16[128,2048]{1,0:T(8,128)(2,1)S(1)}, u32[]{:S(2)}, u32[]{:S(2)}) collective-permute-start(bf16[128,2048]{1,0:T(8,128)(2,1)S(1)} %constant_dynamic-slice_fusion.1), channel_id=1, source_target_pairs={{0,128},{1,385},{2,130},{3,387},{4,132},{5,389},{6,134},{7,391},{8... | collective-permute-start | bytes 1572872 | tf_op jit(solution)/shard_map/ppermute | solution.py:296
  45.9 15.0 %collective-permute-start.1 = (bf16[128,4096]{1,0:T(8,128)(2,1)S(1)}, bf16[128,4096]{1,0:T(8,128)(2,1)}, u32[]{:S(2)}, u32[]{:S(2)}) collective-permute-start(bf16[128,4096]{1,0:T(8,128)(2,1)S(1)} %collective-permute-done.t1), channel_id=1, source_target_pairs={{0,1},{1,0},{2,3},{3,2},{4,5},{5,4},{6,7},{7,6},{8,9},{9,8},{10,11... | collective-permute-start | bytes 3145736 | tf_op jit(solution)/shard_map/ppermute | solution.py:295
  57.9 3.8 %copy-start.9 = (bf16[128,2048]{1,0:T(8,128)(2,1)}, bf16[128,2048]{1,0:T(8,128)(2,1)S(1)}, u32[]{:S(2)}) copy-start(bf16[128,2048]{1,0:T(8,128)(2,1)S(1)} %collective-permute-done.2.t3) | copy-start | bytes 1572868
  57.9 3.8 %collective-permute-start.3 = (bf16[128,2048]{1,0:T(8,128)(2,1)S(1)}, bf16[128,2048]{1,0:T(8,128)(2,1)S(1)}, u32[]{:S(2)}, u32[]{:S(2)}) collective-permute-start(bf16[128,2048]{1,0:T(8,128)(2,1)S(1)} %collective-permute-done.2.t3), channel_id=1, source_target_pairs={{0,1},{1,0},{2,3},{3,2},{4,5},{5,4},{6,7},{7,6},{8,9},{9,8},{10,11... | collective-permute-start | bytes 1572872 | tf_op jit(solution)/shard_map/ppermute | solution.py:297
  60.8 18.4 %copy-start.1 = (f32[256,256]{1,0:T(8,128)S(1)}, f32[256,256]{1,0:T(8,128)}, u32[]{:S(2)}) copy-start(f32[256,256]{1,0:T(8,128)} %constant.51.clone.fwd_ref) | copy-start | bytes 786436
  60.8 18.4 %copy-start.6 = (f32[16,128]{1,0:T(8,128)S(1)}, f32[16,128]{1,0:T(8,128)}, u32[]{:S(2)}) copy-start(f32[16,128]{1,0:T(8,128)} %pad_maximum_fusion.a_ref) | copy-start | bytes 24580
  60.8 19.1 %copy-start.2 = (f32[256,256]{1,0:T(8,128)S(1)}, f32[256,256]{1,0:T(8,128)}, u32[]{:S(2)}) copy-start(f32[256,256]{1,0:T(8,128)} %constant.52.clone.inv_ref) | copy-start | bytes 786436
  61.7 0.8 copy-start.10
  69.6 18.6 %copy-start.4 = (bf16[3,128,256]{2,1,0:T(8,128)(2,1)S(1)}, bf16[3,128,256]{2,1,0:T(8,128)(2,1)}, u32[]{:S(2)}) copy-start(bf16[3,128,256]{2,1,0:T(8,128)(2,1)} %get-tuple-element.10.streams_ref) | copy-start | bytes 589828
  69.6 12.1 %collective-permute-start.4 = (bf16[3,128,256]{2,1,0:T(8,128)(2,1)}, bf16[3,128,256]{2,1,0:T(8,128)(2,1)S(1)}, u32[]{:S(2)}, u32[]{:S(2)}) collective-permute-start(bf16[3,128,256]{2,1,0:T(8,128)(2,1)} %get-tuple-element.10.streams_ref), channel_id=1, source_target_pairs={{0,16},{16,32},{32,48},{48,64},{64,80},{80,96},{96,112},{112,0},{1... | collective-permute-start | bytes 589832 | tf_op jit(solution)/shard_map/ppermute | solution.py:330
  74.1 14.1 %all-to-all-start.1 = ((f32[8,32,128]{2,1,0:T(8,128)}), f32[8,32,128]{2,1,0:T(8,128)S(1)}, u32[]{:S(2)}, u32[]{:S(2)}) async-start(f32[8,32,128]{2,1,0:T(8,128)} %get-tuple-element.12), calls=%async_computation.1 | async-start | bytes 262144 | tf_op jit(solution)/shard_map/all_to_all | solution.py:328
  80.0 0.9 copy-start.3

commit v3 on v2

--- a/solution.py
+++ b/solution.py
@@ -18,6 +18,7 @@
 SPAN = 2 * ROWS
 MODES = 16
 
+parity_groups = [[x * NZ + z for x in range(NX) for z in range(p, NZ, 2)] for p in range(2)]
 x_groups = [[x * NZ + z for x in range(NX)] for z in range(NZ)]
 z_groups = [[x * NZ + z for z in range(NZ)] for x in range(NX)]
 
@@ -60,7 +61,7 @@
     return pltpu.roll(v, HALF, v.ndim - 1)
 
 
-VMEM, ANY = pl.BlockSpec(memory_space=pltpu.VMEM), pl.BlockSpec(memory_space=pl.ANY)
+VMEM, ANY = pl.BlockSpec(memory_space=pltpu.VMEM), pl.BlockSpec(memory_space=pltpu.HBM)
 
 
 def call(body, outs, *args, scratch=(), flops=10**8, far=0, out_specs=None):
@@ -70,7 +71,7 @@
         in_specs=[ANY] * far + [VMEM] * (len(args) - far),
         out_specs=jax.tree.map(lambda _: VMEM, outs) if out_specs is None else out_specs,
         scratch_shapes=scratch,
-        compiler_params=pltpu.CompilerParams(vmem_limit_bytes=(60 if far else 16) << 20),
+        compiler_params=pltpu.CompilerParams(vmem_limit_bytes=16 << 20),
         cost_estimate=pl.CostEstimate(flops=flops, bytes_accessed=flops // 200, transcendentals=0),
     )(*args)
 
@@ -90,11 +91,13 @@
         both, packed = both.astype(bf16), packed.astype(bf16)
         block_ref[x, :ROWS] = both
         block_ref[x, ROWS:] = packed
-        for z in range(NZ):
-            pltpu.make_async_copy(block_ref.at[x], out_ref.at[x * NZ + z], sems.at[x * NZ + z]).start()
+        for z in range(NZ // 2):
+            at = x * (NZ // 2) + z
+            pltpu.make_async_copy(block_ref.at[x], out_ref.at[at], sems.at[at]).start()
     for x in range(NX):
-        for z in range(NZ):
-            pltpu.make_async_copy(block_ref.at[x], out_ref.at[x * NZ + z], sems.at[x * NZ + z]).wait()
+        for z in range(NZ // 2):
+            at = x * (NZ // 2) + z
+            pltpu.make_async_copy(block_ref.at[x], out_ref.at[at], sems.at[at]).wait()
 
 
 def build_tables(a_ref, w_ref, taps_ref, fwd_ref, out_ref, long_ref, short_ref):
@@ -114,73 +117,69 @@
     return lax.div(ctx, NZ), lax.rem(ctx, NZ), lax.rem(ch, NC)
 
 
-PARTS = 4
-
-
-def project(t0, t1, t2, t3, t4, blocks_ref, a_ref, streams_ref, state_ref, tokens_ref, arrived_ref, wide_ref, into_ref, product_ref, sems, block_sems):
-    x, _, core = positions()
+BLOCKS = NX * NZ // 2
+
+
+def widen(blocks_ref, wide_ref):
+    low_half = lower_lanes((HALF, LANES))
+    for block in range(BLOCKS):
+        top, bottom = slice(ROWS * block, ROWS * block + HALF), slice(ROWS * block + HALF, ROWS * (block + 1))
+        wide_ref[ROWS * block : ROWS * (block + 1), :LANES] = blocks_ref[block, :ROWS]
+        packed = blocks_ref[block, ROWS:].astype(f32)
+        turned = swap_halves(packed)
+        wide_ref[top, LANES:] = jnp.where(low_half, packed, turned).astype(bf16)
+        wide_ref[bottom, LANES:] = jnp.where(low_half, turned, packed).astype(bf16)
+
+
+def project_first(t0, t1, t2, t3, t4, blocks_ref, product_ref, rest_ref, tokens_ref, wide_ref, sems):
+    x, z, core = positions()
     near = lax.rem(x + NX - 1 + 2 * core, NX)
     far = lax.rem(x + NX + 1 - 2 * core, NX)
     across = lax.rem(x + 2, NX)
-    part = t0.shape[1] // PARTS
-    share = NX * NZ // PARTS
+    half = BLOCKS // NC
 
     def rows_of(k):
         return pl.ds(pl.multiple_of(k * ROWS, ROWS), ROWS)
 
-    def block_copy(j):
-        at = pl.ds(j * share, share)
-        return pltpu.make_async_copy(blocks_ref.at[at], arrived_ref.at[at], block_sems.at[j])
-
-    def token_copies(j):
-        at = pl.ds(j * part, part)
-        found = [
-            pltpu.make_async_copy(ref.at[:, at], tokens_ref.at[rows_of(k), at], sems.at[i, j])
-            for i, (ref, k) in enumerate(((t0, x), (t1, near), (t2, far)))
-        ]
-        half = PARTS // NC
-        inner = pl.ds((j % half) * part, part)
-        mine = (j // half) == core
-        return found, mine, [
-            pltpu.make_async_copy(ref.at[:, inner], tokens_ref.at[rows_of(across), at], sems.at[3, j]) for ref in (t3, t4)
-        ]
-
-    plans = [token_copies(j) for j in range(PARTS)]
-    for j in range(PARTS):
-        block_copy(j).start()
-        found, mine, (first, second) = plans[j]
-        for copy in found:
-            copy.start()
-        pl.when(mine)(first.start)
-        pl.when(jnp.logical_not(mine))(second.start)
+    for side, target in ((0, tokens_ref), (1, rest_ref)):
+        parity = lax.rem(z + side, 2)
+        for i in range(BLOCKS):
+            to = pl.ds(LANES * i, LANES)
+            at = pl.ds(pl.multiple_of((2 * i + parity) * LANES, LANES), LANES)
+            for k, (ref, place) in enumerate(((t0, x), (t1, near), (t2, far))):
+                pltpu.make_async_copy(ref.at[:, at], target.at[rows_of(place), to], sems.at[k, side]).start()
+            inner = pl.ds(pl.multiple_of((2 * (i % half) + parity) * LANES, LANES), LANES)
+            mine = (i // half) == core
+            first = pltpu.make_async_copy(t3.at[:, inner], target.at[rows_of(across), to], sems.at[3, side])
+            second = pltpu.make_async_copy(t4.at[:, inner], target.at[rows_of(across), to], sems.at[3, side])
+            pl.when(mine)(first.start)
+            pl.when(jnp.logical_not(mine))(second.start)
+    widen(blocks_ref, wide_ref)
+
+    def wait(target, side):
+        for k in range(4):
+            rows = target.at[slice(ROWS * k, ROWS * (k + 1))]
+            pltpu.make_async_copy(rows, rows, sems.at[k, side]).wait()
+
+    wait(tokens_ref, 0)
+    product_ref[...] = jnp.dot(tokens_ref[...], wide_ref[...], preferred_element_type=f32)
+    wait(rest_ref, 1)
+
+
+def project_rest(rest_ref, product_ref, blocks_ref, a_ref, streams_ref, state_ref, wide_ref, into_ref, total_ref):
+    widen(blocks_ref, wide_ref)
+    total_ref[...] = product_ref[...] + jnp.dot(rest_ref[...], wide_ref[...], preferred_element_type=f32)
     back = ROWS - 1.0 - lax.broadcasted_iota(jnp.int32, (ROWS, LANES), 0).astype(f32)
     for m in range(MODES):
         into_ref[m] = jnp.exp(-a_ref[m : m + 1, :] * back)
-    low_half = lower_lanes((HALF, LANES))
-    for j in range(PARTS):
-        block_copy(j).wait()
-        for block in range(j * share, (j + 1) * share):
-            top, bottom = pl.ds(ROWS * block, HALF), pl.ds(ROWS * block + HALF, HALF)
-            wide_ref[pl.ds(ROWS * block, ROWS), :LANES] = arrived_ref[block, :ROWS]
-            packed = arrived_ref[block, ROWS:].astype(f32)
-            turned = swap_halves(packed)
-            wide_ref[top, LANES:] = jnp.where(low_half, packed, turned).astype(bf16)
-            wide_ref[bottom, LANES:] = jnp.where(low_half, turned, packed).astype(bf16)
-        found, _, (first, _) = plans[j]
-        for copy in found:
-            copy.wait()
-        first.wait()
-        at = slice(j * part, (j + 1) * part)
-        term = jnp.dot(tokens_ref[:, at], wide_ref[at, :], preferred_element_type=f32)
-        product_ref[...] = term if j == 0 else product_ref[...] + term
     low = lower_lanes((ROWS, LANES))
     for pair in range(NX // 2):
         lanes = slice(LANES * pair, LANES * (pair + 1))
         chunks = [slice(ROWS * k, ROWS * (k + 1)) for k in (2 * pair, 2 * pair + 1)]
-        a, b = (product_ref[k, :LANES].astype(bf16).astype(f32) for k in chunks)
+        a, b = (total_ref[k, :LANES].astype(bf16).astype(f32) for k in chunks)
         turned_a, turned_b = swap_halves(a), swap_halves(b)
         gate_in, values = jnp.where(low, a, turned_b), jnp.where(low, turned_a, b)
-        gate_out = jnp.where(low, product_ref[chunks[0], LANES:], product_ref[chunks[1], LANES:])
+        gate_out = jnp.where(low, total_ref[chunks[0], LANES:], total_ref[chunks[1], LANES:])
         signal = gate_in * values
         for k, value in enumerate((gate_in, values, gate_out)):
             streams_ref[k, :, lanes] = value.astype(bf16)
@@ -273,7 +272,6 @@
     core = lax.axis_index("ch") % NC
     rows, features = tokens.shape
     width = features // NC
-    count = NX * NZ
     wide = lax.axis_size("ch")
 
     def place(a, b, k):
@@ -286,12 +284,16 @@
     near = lax.ppermute(tokens, ("ctx", "ch"), outward)
     blocks = call(
         spread_weights,
-        sds((count, ROWS + HALF, LANES), bf16),
+        sds((BLOCKS, ROWS + HALF, LANES), bf16),
         projections,
-        scratch=[pltpu.VMEM((NX, ROWS + HALF, LANES), bf16), pltpu.SemaphoreType.DMA((count,))],
+        scratch=[pltpu.VMEM((NX, ROWS + HALF, LANES), bf16), pltpu.SemaphoreType.DMA((BLOCKS,))],
         out_specs=ANY,
     )
-    blocks = lax.all_to_all(blocks, "ctx", 0, 0, tiled=True)
+    blocks = lax.all_to_all(blocks, "ctx", 0, 0, tiled=True, axis_index_groups=parity_groups)
+    across = [
+        (place(a, b, k), place(a, (b + 1 - 2 * (k % NC)) % NZ, k)) for a in range(NX) for b in range(NZ) for k in range(wide)
+    ]
+    rest_blocks = lax.ppermute(blocks, ("ctx", "ch"), across)
     far = lax.ppermute(near, "ch", swap)
     half = lax.ppermute(lax.dynamic_slice_in_dim(near, core * width, width, 1), ("ctx", "ch"), outward)
     other = lax.ppermute(half, "ch", swap)
@@ -304,26 +306,35 @@
     table = sds((MODES, ROWS, LANES), f32)
     spectrum = sds((SPAN, LANES), f32)
     out, long_spectrum, short_spectrum = call(build_tables, (table, spectrum, spectrum), rates, weights, taps, forward)
-    streams, states = call(
-        project,
-        (sds((3, ROWS, 2 * LANES), bf16), sds((NZ, 2 * MODES, LANES), f32)),
+    half_depth = BLOCKS * ROWS
+    product, rest = call(
+        project_first,
+        (sds((NX * rows, 2 * LANES), f32), sds((NX * rows, half_depth), bf16)),
         tokens,
         near,
         far,
         half,
         other,
         blocks,
+        scratch=[
+            pltpu.VMEM((NX * rows, half_depth), bf16),
+            pltpu.VMEM((half_depth, 2 * LANES), bf16),
+            pltpu.SemaphoreType.DMA((4, 2)),
+        ],
+        far=5,
+    )
+    streams, states = call(
+        project_rest,
+        (sds((3, ROWS, 2 * LANES), bf16), sds((NZ, 2 * MODES, LANES), f32)),
+        rest,
+        product,
+        rest_blocks,
         rates,
         scratch=[
-            pltpu.VMEM((NX * rows, features), bf16),
-            pltpu.VMEM((count, ROWS + HALF, LANES), bf16),
-            pltpu.VMEM((features, 2 * LANES), bf16),
+            pltpu.VMEM((half_depth, 2 * LANES), bf16),
             pltpu.VMEM((MODES, ROWS, LANES), f32),
             pltpu.VMEM((NX * rows, 2 * LANES), f32),
-            pltpu.SemaphoreType.DMA((4, PARTS)),
-            pltpu.SemaphoreType.DMA((PARTS,)),
         ],
-        far=6,
     )
     states = lax.all_to_all(states, "ctx", 0, 0, tiled=True, axis_index_groups=z_groups)
     onward = [(a * NZ + b, a * NZ + (b + 1) % NZ) for a in range(NX) for b in range(NZ)]

time: 99.6 us -> 85.7 us (0.86)
  the two profiles are of different devices: /device:TPU:48 before, /device:TPU:56 now
where the time goes in v3:
time: 85.7 us; the launch traced here: 85.1 us
  starting transfers between devices  38.1 us (44%)
  waiting for transfers between devices  25.1 us (29%)
  Pallas kernels  10.6 us (12%)
  blocking collectives  7.99 us (9%)
  local copies, waits for them, and re-layouts  1.98 us (2%)
  other arithmetic  1.01 us (1%)
    all_to_all x1, waiting for transfers between devices, per_device(): lax.all_to_all(blocks, 'ctx', 0, 0, tiled=True, axis_index_groups=parity_...  13.6 us
    all_to_all x1, starting transfers between devices, per_device(): lax.all_to_all(blocks, 'ctx', 0, 0, tiled=True, axis_index_groups=parity_...  12.6 us
    pallas_call x7, Pallas kernels, call(): pl.pallas_call(body, out_shape=outs, in_specs=[ANY] * far + [VMEM] * (len...  10.6 us
    all_to_all x1, blocking collectives, per_device(): lax.all_to_all(packed, 'ctx', 0, 0, tiled=True, axis_index_groups=x_groups)  7.99 us
    all_to_all x1, waiting for transfers between devices, per_device(): lax.all_to_all(states, 'ctx', 0, 0, tiled=True, axis_index_groups=z_groups)  7.26 us
    ppermute x1, starting transfers between devices, per_device(): rest_blocks = lax.ppermute(blocks, ('ctx', 'ch'), across)  6.47 us
    ppermute x1, starting transfers between devices, per_device(): arrived = lax.ppermute(streams, 'ctx', onward)  4.48 us
    ppermute x1, starting transfers between devices, per_device(): lax.ppermute(lax.dynamic_slice_in_dim(near, core * width, width, 1), ('ct...  3.8 us
  transfers between devices with their start and end apart: 8, of which 4 were waited for; matrix products, arithmetic and copies ran while one was open for 2% of the time, Pallas kernels for 6%

profile of v3, /device:TPU:56, one launch (start us, length us, event | category | flops | bytes accessed | tf_op | source)
XLA Modules:
  0.0 85.1 jit_solution(13012723678967924091)
XLA Ops:
  0.0 3.5 %collective-permute-start = (bf16[128,4096]{1,0:T(8,128)(2,1)}, bf16[128,4096]{1,0:T(8,128)(2,1)S(1)}, u32[]{:S(2)}, u32[]{:S(2)}) collective-permute-start(bf16[128,4096]{1,0:T(8,128)(2,1)} %t0.1), channel_id=1, source_target_pairs={{0,128},{1,385},{2,130},{3,387},{4,132},{5,389},{6,134},{7,391},{8... | collective-permute-start | bytes 3145736 | tf_op jit(solution)/shard_map/ppermute | solution.py:284
  3.5 0.9 %copy-done.4 = bf16[3,128,256]{2,1,0:T(8,128)(2,1)S(1)} copy-done((bf16[3,128,256]{2,1,0:T(8,128)(2,1)S(1)}, bf16[3,128,256]{2,1,0:T(8,128)(2,1)}, u32[]{:S(2)}) %copy-start.4) | copy-done | bytes 196632
  4.5 1.2 %shard_map.73 = bf16[16,192,128]{2,1,0:T(8,128)(2,1)} custom-call(bf16[3,128,256]{2,1,0:T(8,128)(2,1)S(1)} %copy-done.4), custom_call_target="tpu_custom_call" | custom-call | flops 100000000 | bytes 500000 | tf_op jit(solution)/shard_map/pallas_call | solution.py:68
  5.6 12.6 %all-to-all-start = ((bf16[16,192,128]{2,1,0:T(8,128)(2,1)}), bf16[16,192,128]{2,1,0:T(8,128)(2,1)S(1)}, u32[]{:S(2)}, u32[]{:S(2)}) async-start(bf16[16,192,128]{2,1,0:T(8,128)(2,1)} %shard_map.73), calls=%async_computation | async-start | bytes 1572864 | tf_op jit(solution)/shard_map/all_to_all | solution.py:292
  18.2 0.0 collective-permute-done.t1
  18.2 0.8 constant_dynamic-slice_fusion.1
  19.1 3.8 %collective-permute-start.2 = (bf16[128,2048]{1,0:T(8,128)(2,1)}, bf16[128,2048]{1,0:T(8,128)(2,1)S(1)}, u32[]{:S(2)}, u32[]{:S(2)}) collective-permute-start(bf16[128,2048]{1,0:T(8,128)(2,1)} %constant_dynamic-slice_fusion.1), channel_id=1, source_target_pairs={{0,128},{1,385},{2,130},{3,387},{4,132},{5,389},{6,134},{7,391},{8... | collective-permute-start | bytes 1572872 | tf_op jit(solution)/shard_map/ppermute | solution.py:298
  22.9 1.9 %collective-permute-start.1 = (bf16[128,4096]{1,0:T(8,128)(2,1)S(1)}, bf16[128,4096]{1,0:T(8,128)(2,1)}, u32[]{:S(2)}, u32[]{:S(2)}) collective-permute-start(bf16[128,4096]{1,0:T(8,128)(2,1)S(1)} %collective-permute-done.t1), channel_id=1, source_target_pairs={{0,1},{1,0},{2,3},{3,2},{4,5},{5,4},{6,7},{7,6},{8,9},{9,8},{10,11... | collective-permute-start | bytes 3145736 | tf_op jit(solution)/shard_map/ppermute | solution.py:297
  24.8 13.6 %all-to-all-done.blocks_ref = bf16[16,192,128]{2,1,0:T(8,128)(2,1)S(1)} async-done(((bf16[16,192,128]{2,1,0:T(8,128)(2,1)}), bf16[16,192,128]{2,1,0:T(8,128)(2,1)S(1)}, u32[]{:S(2)}, u32[]{:S(2)}) %all-to-all-start) | async-done | bytes 786464 | tf_op jit(solution)/shard_map/all_to_all | solution.py:292
  38.4 6.5 %collective-permute-start.4 = (bf16[16,192,128]{2,1,0:T(8,128)(2,1)S(1)}, bf16[16,192,128]{2,1,0:T(8,128)(2,1)}, u32[]{:S(2)}, u32[]{:S(2)}) collective-permute-start(bf16[16,192,128]{2,1,0:T(8,128)(2,1)S(1)} %all-to-all-done.blocks_ref), channel_id=1, source_target_pairs={{0,16},{1,113},{2,18},{3,115},{4,20},{5,117},{6,22},{7,119},{8,24}... | collective-permute-start | bytes 2359304 | tf_op jit(solution)/shard_map/ppermute | solution.py:296
  44.9 1.9 %collective-permute-start.3 = (bf16[128,2048]{1,0:T(8,128)(2,1)S(1)}, bf16[128,2048]{1,0:T(8,128)(2,1)}, u32[]{:S(2)}, u32[]{:S(2)}) collective-permute-start(bf16[128,2048]{1,0:T(8,128)(2,1)S(1)} %collective-permute-done.2.t3), channel_id=1, source_target_pairs={{0,1},{1,0},{2,3},{3,2},{4,5},{5,4},{6,7},{7,6},{8,9},{9,8},{10,11... | collective-permute-start | bytes 1572872 | tf_op jit(solution)/shard_map/ppermute | solution.py:299
  46.9 0.1 copy.9
  47.0 0.1 dynamic-slice_bitcast_fusion
  47.1 0.1 pad_maximum_fusion.a_ref
  47.2 0.8 bitcast_multiply_fusion
  47.9 0.9 %collective-permute-done.3.t4 = bf16[128,2048]{1,0:T(8,128)(2,1)} collective-permute-done((bf16[128,2048]{1,0:T(8,128)(2,1)S(1)}, bf16[128,2048]{1,0:T(8,128)(2,1)}, u32[]{:S(2)}, u32[]{:S(2)}) %collective-permute-start.3) | collective-permute-done | bytes 524320 | tf_op jit(solution)/shard_map/ppermute | solution.py:299
  48.9 0.0 collective-permute-done.1.t2
  48.9 2.1 %shard_map.74 = (f32[512,256]{1,0:T(8,128)S(1)}, bf16[512,2048]{1,0:T(8,128)(2,1)S(1)}) custom-call(bf16[128,4096]{1,0:T(8,128)(2,1)S(1)} %copy-done.1, bf16[128,4096]{1,0:T(8,128)(2,1)S(1)} %collective-permute-done.t1, bf16[128,4096]{1,0:T(8,128)(2,1)} %collective-permute-done.1.t2, bf16[128,2048]{1,0:T(8,128)(2,1)S(1)} %collective-permute-done.2.t3, ...), custom_call_target="tpu_custom_call" | custom-call | flops 100000000 | bytes 500000 | tf_op jit(solution)/shard_map/pallas_call | solution.py:68
  51.0 0.0 copy-start.2
  51.0 0.0 copy-start.3
  51.0 3.4 %collective-permute-done.4.blocks_ref = bf16[16,192,128]{2,1,0:T(8,128)(2,1)} collective-permute-done((bf16[16,192,128]{2,1,0:T(8,128)(2,1)S(1)}, bf16[16,192,128]{2,1,0:T(8,128)(2,1)}, u32[]{:S(2)}, u32[]{:S(2)}) %collective-permute-start.4) | collective-permute-done | bytes 786464 | tf_op jit(solution)/shard_map/ppermute | solution.py:296
  54.4 2.9 %shard_map.75 = (bf16[3,128,256]{2,1,0:T(8,128)(2,1)S(1)}, f32[8,32,128]{2,1,0:T(8,128)}) custom-call(bf16[512,2048]{1,0:T(8,128)(2,1)S(1)} %get-tuple-element.12.rest_ref, f32[512,256]{1,0:T(8,128)S(1)} %get-tuple-element.13.product_ref, bf16[16,192,128]{2,1,0:T(8,128)(2,1)} %collective-permute-done.4.blocks_ref, f32[16,128]{1,0:T(8,128)S(1)} %pad_maximum_fusion.a_ref), custom_call_target="tpu_custom_call" | custom-call | flops 100000000 | bytes 500000 | tf_op jit(solution)/shard_map/pallas_call | solution.py:68
  57.3 4.5 %collective-permute-start.5 = (bf16[3,128,256]{2,1,0:T(8,128)(2,1)S(1)}, bf16[3,128,256]{2,1,0:T(8,128)(2,1)S(1)}, u32[]{:S(2)}, u32[]{:S(2)}) collective-permute-start(bf16[3,128,256]{2,1,0:T(8,128)(2,1)S(1)} %get-tuple-element.14.streams_ref), channel_id=1, source_target_pairs={{0,16},{16,32},{32,48},{48,64},{64,80},{80,96},{96,112},{112,0},{1... | collective-permute-start | bytes 589832 | tf_op jit(solution)/shard_map/ppermute | solution.py:341
  61.8 3.4 %all-to-all-start.1 = ((f32[8,32,128]{2,1,0:T(8,128)}), f32[8,32,128]{2,1,0:T(8,128)S(1)}, u32[]{:S(2)}, u32[]{:S(2)}) async-start(f32[8,32,128]{2,1,0:T(8,128)} %get-tuple-element.16), calls=%async_computation.1 | async-start | bytes 262144 | tf_op jit(solution)/shard_map/all_to_all | solution.py:339
  65.2 0.1 pad_maximum_fusion.1.w_ref
  65.3 0.1 maximum_convert_fusion.taps_ref
  65.4 0.7 shard_map.76
  66.1 0.8 shard_map.77.local_ref
  66.9 7.3 %all-to-all-done.1.states_ref = f32[8,32,128]{2,1,0:T(8,128)S(1)} async-done(((f32[8,32,128]{2,1,0:T(8,128)}), f32[8,32,128]{2,1,0:T(8,128)S(1)}, u32[]{:S(2)}, u32[]{:S(2)}) %all-to-all-start.1) | async-done | bytes 131104 | tf_op jit(solution)/shard_map/all_to_all | solution.py:339
  74.2 2.1 %shard_map.78 = bf16[4,64,128]{2,1,0:T(8,128)(2,1)S(1)} custom-call(bf16[3,128,256]{2,1,0:T(8,128)(2,1)S(1)} %get-tuple-element.14.streams_ref, f32[128,256]{1,0:T(8,128)S(1)} %shard_map.77.local_ref, bf16[3,128,256]{2,1,0:T(8,128)(2,1)S(1)} %collective-permute-done.5.arrived_ref, f32[8,32,128]{2,1,0:T(8,128)S(1)} %all-to-all-done.1.states_ref, ...), custom_call_target="tpu_custom_call" | custom-call | flops 100000000 | bytes 500000 | tf_op jit(solution)/shard_map/pallas_call | solution.py:68
  76.3 8.0 %all_to_all.15.packed_ref = bf16[4,64,128]{2,1,0:T(8,128)(2,1)S(1)} all-to-all(bf16[4,64,128]{2,1,0:T(8,128)(2,1)S(1)} %shard_map.78), channel_id=1, replica_groups={{0,128,256,384},{16,144,272,400},{32,160,288,416},{48,176,304,432},{64,..., dimensions={0} | all-to-all | bytes 131072 | tf_op jit(solution)/shard_map/all_to_all | solution.py:357
  84.3 0.7 shard_map.79
  (12 shorter events, 0.0 us)
Async XLA Ops:
  0.0 46.9 %copy-start = (bf16[256,128]{1,0:T(8,128)(2,1)S(1)}, bf16[256,128]{1,0:T(8,128)(2,1)}, u32[]{:S(2)}) copy-start(bf16[256,128]{1,0:T(8,128)(2,1)} %param.11) | copy-start | bytes 196612
  0.0 48.9 %copy-start.1 = (bf16[128,4096]{1,0:T(8,128)(2,1)S(1)}, bf16[128,4096]{1,0:T(8,128)(2,1)}, u32[]{:S(2)}) copy-start(bf16[128,4096]{1,0:T(8,128)(2,1)} %t0.1) | copy-start | bytes 3145732
  0.0 18.2 %collective-permute-start = (bf16[128,4096]{1,0:T(8,128)(2,1)}, bf16[128,4096]{1,0:T(8,128)(2,1)S(1)}, u32[]{:S(2)}, u32[]{:S(2)}) collective-permute-start(bf16[128,4096]{1,0:T(8,128)(2,1)} %t0.1), channel_id=1, source_target_pairs={{0,128},{1,385},{2,130},{3,387},{4,132},{5,389},{6,134},{7,391},{8... | collective-permute-start | bytes 3145736 | tf_op jit(solution)/shard_map/ppermute | solution.py:284
  3.5 0.9 %copy-start.4 = (bf16[3,128,256]{2,1,0:T(8,128)(2,1)S(1)}, bf16[3,128,256]{2,1,0:T(8,128)(2,1)}, u32[]{:S(2)}) copy-start(bf16[3,128,256]{2,1,0:T(8,128)(2,1)} %w_ref.1) | copy-start | bytes 589828
  4.5 42.5 %copy-start.5 = (f32[256,16]{0,1:T(8,128)S(1)}, f32[256,16]{0,1:T(8,128)}, u32[]{:S(2)}) copy-start(f32[256,16]{0,1:T(8,128)} %param.9) | copy-start | bytes 49156
  5.6 32.8 %all-to-all-start = ((bf16[16,192,128]{2,1,0:T(8,128)(2,1)}), bf16[16,192,128]{2,1,0:T(8,128)(2,1)S(1)}, u32[]{:S(2)}, u32[]{:S(2)}) async-start(bf16[16,192,128]{2,1,0:T(8,128)(2,1)} %shard_map.73), calls=%async_computation | async-start | bytes 1572864 | tf_op jit(solution)/shard_map/all_to_all | solution.py:292
  19.1 25.8 %collective-permute-start.2 = (bf16[128,2048]{1,0:T(8,128)(2,1)}, bf16[128,2048]{1,0:T(8,128)(2,1)S(1)}, u32[]{:S(2)}, u32[]{:S(2)}) collective-permute-start(bf16[128,2048]{1,0:T(8,128)(2,1)} %constant_dynamic-slice_fusion.1), channel_id=1, source_target_pairs={{0,128},{1,385},{2,130},{3,387},{4,132},{5,389},{6,134},{7,391},{8... | collective-permute-start | bytes 1572872 | tf_op jit(solution)/shard_map/ppermute | solution.py:298
  22.9 26.0 %collective-permute-start.1 = (bf16[128,4096]{1,0:T(8,128)(2,1)S(1)}, bf16[128,4096]{1,0:T(8,128)(2,1)}, u32[]{:S(2)}, u32[]{:S(2)}) collective-permute-start(bf16[128,4096]{1,0:T(8,128)(2,1)S(1)} %collective-permute-done.t1), channel_id=1, source_target_pairs={{0,1},{1,0},{2,3},{3,2},{4,5},{5,4},{6,7},{7,6},{8,9},{9,8},{10,11... | collective-permute-start | bytes 3145736 | tf_op jit(solution)/shard_map/ppermute | solution.py:297
  38.4 16.0 %collective-permute-start.4 = (bf16[16,192,128]{2,1,0:T(8,128)(2,1)S(1)}, bf16[16,192,128]{2,1,0:T(8,128)(2,1)}, u32[]{:S(2)}, u32[]{:S(2)}) collective-permute-start(bf16[16,192,128]{2,1,0:T(8,128)(2,1)S(1)} %all-to-all-done.blocks_ref), channel_id=1, source_target_pairs={{0,16},{1,113},{2,18},{3,115},{4,20},{5,117},{6,22},{7,119},{8,24}... | collective-permute-start | bytes 2359304 | tf_op jit(solution)/shard_map/ppermute | solution.py:296
  44.9 3.9 %collective-permute-start.3 = (bf16[128,2048]{1,0:T(8,128)(2,1)S(1)}, bf16[128,2048]{1,0:T(8,128)(2,1)}, u32[]{:S(2)}, u32[]{:S(2)}) collective-permute-start(bf16[128,2048]{1,0:T(8,128)(2,1)S(1)} %collective-permute-done.2.t3), channel_id=1, source_target_pairs={{0,1},{1,0},{2,3},{3,2},{4,5},{5,4},{6,7},{7,6},{8,9},{9,8},{10,11... | collective-permute-start | bytes 1572872 | tf_op jit(solution)/shard_map/ppermute | solution.py:299
  51.0 14.4 %copy-start.2 = (f32[256,256]{1,0:T(8,128)S(1)}, f32[256,256]{1,0:T(8,128)}, u32[]{:S(2)}) copy-start(f32[256,256]{1,0:T(8,128)} %constant.51.clone.fwd_ref) | copy-start | bytes 786436
  51.0 15.1 %copy-start.3 = (f32[256,256]{1,0:T(8,128)S(1)}, f32[256,256]{1,0:T(8,128)}, u32[]{:S(2)}) copy-start(f32[256,256]{1,0:T(8,128)} %constant.52.clone.inv_ref) | copy-start | bytes 786436
  57.3 9.6 %collective-permute-start.5 = (bf16[3,128,256]{2,1,0:T(8,128)(2,1)S(1)}, bf16[3,128,256]{2,1,0:T(8,128)(2,1)S(1)}, u32[]{:S(2)}, u32[]{:S(2)}) collective-permute-start(bf16[3,128,256]{2,1,0:T(8,128)(2,1)S(1)} %get-tuple-element.14.streams_ref), channel_id=1, source_target_pairs={{0,16},{16,32},{32,48},{48,64},{64,80},{80,96},{96,112},{112,0},{1... | collective-permute-start | bytes 589832 | tf_op jit(solution)/shard_map/ppermute | solution.py:341
  61.8 12.4 %all-to-all-start.1 = ((f32[8,32,128]{2,1,0:T(8,128)}), f32[8,32,128]{2,1,0:T(8,128)S(1)}, u32[]{:S(2)}, u32[]{:S(2)}) async-start(f32[8,32,128]{2,1,0:T(8,128)} %get-tuple-element.16), calls=%async_computation.1 | async-start | bytes 262144 | tf_op jit(solution)/shard_map/all_to_all | solution.py:339

commit v4 on v3

--- a/solution.py
+++ b/solution.py
@@ -9,7 +9,6 @@
 from jax.sharding import PartitionSpec as P
 
 f32, bf16 = jnp.float32, jnp.bfloat16
-highest = lax.Precision.HIGHEST
 
 NX, NZ, NC = 4, 8, 2
 ROWS = 128
@@ -40,8 +39,21 @@
     return (np.concatenate([real, imag], axis=1) / SPAN).astype(np.float32)
 
 
-def dot32(a, b):
-    return jnp.dot(a, b, precision=highest, preferred_element_type=f32)
+def halves(v):
+    high = v.astype(bf16)
+    return high, (v - high.astype(f32)).astype(bf16)
+
+
+def dot_pair(a, b):
+    high, low = halves(a)
+    if b.dtype == bf16:
+        return dot(high, b) + dot(low, b)
+    b_high, b_low = halves(b)
+    return dot(high, b_high) + (dot(high, b_low) + dot(low, b_high))
+
+
+def dot(a, b):
+    return jnp.dot(a, b, preferred_element_type=f32)
 
 
 def multiply_spectra(u, h):
@@ -108,8 +120,8 @@
         out_ref[m] = weight * jnp.exp(-rate * (t + 1.0))
         impulse = impulse + weight * jnp.exp(-rate * t)
     transform = fwd_ref[:, :ROWS]
-    long_ref[...] = dot32(transform, impulse)
-    short_ref[...] = dot32(transform, taps_ref[...])
+    long_ref[...] = dot_pair(transform, impulse)
+    short_ref[...] = dot_pair(transform, taps_ref[...])
 
 
 def positions():
@@ -131,7 +143,7 @@
         wide_ref[bottom, LANES:] = jnp.where(low_half, turned, packed).astype(bf16)
 
 
-def project_first(t0, t1, t2, t3, t4, blocks_ref, product_ref, rest_ref, tokens_ref, wide_ref, sems):
+def project_first(t0, t1, t2, t3, t4, blocks_ref, a_ref, product_ref, rest_ref, into_ref, tokens_ref, wide_ref, sems):
     x, z, core = positions()
     near = lax.rem(x + NX - 1 + 2 * core, NX)
     far = lax.rem(x + NX + 1 - 2 * core, NX)
@@ -155,6 +167,9 @@
             pl.when(mine)(first.start)
             pl.when(jnp.logical_not(mine))(second.start)
     widen(blocks_ref, wide_ref)
+    back = ROWS - 1.0 - lax.broadcasted_iota(jnp.int32, (ROWS, LANES), 0).astype(f32)
+    for m in range(MODES):
+        into_ref[m] = jnp.exp(-a_ref[m : m + 1, :] * back)
 
     def wait(target, side):
         for k in range(4):
@@ -166,12 +181,9 @@
     wait(rest_ref, 1)
 
 
-def project_rest(rest_ref, product_ref, blocks_ref, a_ref, streams_ref, state_ref, wide_ref, into_ref, total_ref):
+def project_rest(rest_ref, product_ref, blocks_ref, into_ref, streams_ref, state_ref, wide_ref, total_ref):
     widen(blocks_ref, wide_ref)
     total_ref[...] = product_ref[...] + jnp.dot(rest_ref[...], wide_ref[...], preferred_element_type=f32)
-    back = ROWS - 1.0 - lax.broadcasted_iota(jnp.int32, (ROWS, LANES), 0).astype(f32)
-    for m in range(MODES):
-        into_ref[m] = jnp.exp(-a_ref[m : m + 1, :] * back)
     low = lower_lanes((ROWS, LANES))
     for pair in range(NX // 2):
         lanes = slice(LANES * pair, LANES * (pair + 1))
@@ -191,9 +203,9 @@
 
 def filter_inside(streams_ref, fwd_ref, inv_ref, long_ref):
     signal = streams_ref[0].astype(f32) * streams_ref[1].astype(f32)
-    spectrum = dot32(fwd_ref[:, :ROWS], signal)
+    spectrum = dot_pair(fwd_ref[:, :ROWS], signal)
     response = jnp.concatenate([long_ref[...]] * 2, axis=1)
-    return dot32(inv_ref[:ROWS, :], multiply_spectra(spectrum, response))
+    return dot_pair(inv_ref[:ROWS, :], multiply_spectra(spectrum, response))
 
 
 def filter_chunks(streams_ref, fwd_ref, inv_ref, long_ref, local_ref):
@@ -246,9 +258,9 @@
     turned = [swap_halves(v) for v in arrived]
     shifted = [jnp.where(low, 0.0, turned[0]), jnp.where(low, turned[0], turned[1])]
     previous = jnp.concatenate([jnp.where(z == 0, s, a) for s, a in zip(shifted, arrived)], axis=1)
-    window = jnp.concatenate([previous, jnp.concatenate(own, axis=1)], axis=0)
+    window = jnp.concatenate([previous, jnp.concatenate(own, axis=1)], axis=0).astype(bf16)
     response = jnp.concatenate([short_ref[...]] * 2, axis=1)
-    mixed = dot32(inv_ref[ROWS:, :], multiply_spectra(dot32(fwd_ref[...], window), response))
+    mixed = dot_pair(inv_ref[ROWS:, :], multiply_spectra(dot_pair(fwd_ref[...], window), response))
     low_half = lower_lanes((HALF, LANES))
     for pair in range(2):
         top = mixed[:HALF, LANES * pair : LANES * (pair + 1)]
@@ -307,15 +319,16 @@
     spectrum = sds((SPAN, LANES), f32)
     out, long_spectrum, short_spectrum = call(build_tables, (table, spectrum, spectrum), rates, weights, taps, forward)
     half_depth = BLOCKS * ROWS
-    product, rest = call(
+    product, rest, into = call(
         project_first,
-        (sds((NX * rows, 2 * LANES), f32), sds((NX * rows, half_depth), bf16)),
+        (sds((NX * rows, 2 * LANES), f32), sds((NX * rows, half_depth), bf16), table),
         tokens,
         near,
         far,
         half,
         other,
         blocks,
+        rates,
         scratch=[
             pltpu.VMEM((NX * rows, half_depth), bf16),
             pltpu.VMEM((half_depth, 2 * LANES), bf16),
@@ -329,10 +342,9 @@
         rest,
         product,
         rest_blocks,
-        rates,
+        into,
         scratch=[
             pltpu.VMEM((half_depth, 2 * LANES), bf16),
-            pltpu.VMEM((MODES, ROWS, LANES), f32),
             pltpu.VMEM((NX * rows, 2 * LANES), f32),
         ],
     )

time: 85.7 us -> 85 us (level)
  the two profiles are of different devices: /device:TPU:56 before, /device:TPU:32 now
where the time goes in v4:
time: 85 us; the launch traced here: 84.3 us
  starting transfers between devices  38.1 us (45%)
  waiting for transfers between devices  25.6 us (30%)
  Pallas kernels  9.47 us (11%)
  blocking collectives  7.99 us (9%)
  local copies, waits for them, and re-layouts  1.97 us (2%)
  other arithmetic  1.01 us (1%)
    all_to_all x1, waiting for transfers between devices, per_device(): lax.all_to_all(blocks, 'ctx', 0, 0, tiled=True, axis_index_groups=parity_...  13.6 us
    all_to_all x1, starting transfers between devices, per_device(): lax.all_to_all(blocks, 'ctx', 0, 0, tiled=True, axis_index_groups=parity_...  12.6 us
    pallas_call x7, Pallas kernels, call(): pl.pallas_call(body, out_shape=outs, in_specs=[ANY] * far + [VMEM] * (len...  9.47 us
    all_to_all x1, blocking collectives, per_device(): lax.all_to_all(packed, 'ctx', 0, 0, tiled=True, axis_index_groups=x_groups)  7.99 us
    all_to_all x1, waiting for transfers between devices, per_device(): lax.all_to_all(states, 'ctx', 0, 0, tiled=True, axis_index_groups=z_groups)  7.67 us
    ppermute x1, starting transfers between devices, per_device(): rest_blocks = lax.ppermute(blocks, ('ctx', 'ch'), across)  6.47 us
    ppermute x1, starting transfers between devices, per_device(): arrived = lax.ppermute(streams, 'ctx', onward)  4.48 us
    ppermute x1, starting transfers between devices, per_device(): lax.ppermute(lax.dynamic_slice_in_dim(near, core * width, width, 1), ('ct...  3.8 us
  transfers between devices with their start and end apart: 8, of which 4 were waited for; matrix products, arithmetic and copies ran while one was open for 2% of the time, Pallas kernels for 5%

profile of v4, /device:TPU:32, one launch (start us, length us, event | category | flops | bytes accessed | tf_op | source)
XLA Modules:
  0.0 84.3 jit_solution(15913866553411867560)
XLA Ops:
  0.0 3.5 %collective-permute-start = (bf16[128,4096]{1,0:T(8,128)(2,1)}, bf16[128,4096]{1,0:T(8,128)(2,1)S(1)}, u32[]{:S(2)}, u32[]{:S(2)}) collective-permute-start(bf16[128,4096]{1,0:T(8,128)(2,1)} %t0.1), channel_id=1, source_target_pairs={{0,128},{1,385},{2,130},{3,387},{4,132},{5,389},{6,134},{7,391},{8... | collective-permute-start | bytes 3145736 | tf_op jit(solution)/shard_map/ppermute | solution.py:296
  3.5 0.9 %copy-done.4 = bf16[3,128,256]{2,1,0:T(8,128)(2,1)S(1)} copy-done((bf16[3,128,256]{2,1,0:T(8,128)(2,1)S(1)}, bf16[3,128,256]{2,1,0:T(8,128)(2,1)}, u32[]{:S(2)}) %copy-start.4) | copy-done | bytes 196632
  4.5 1.2 %shard_map.73 = bf16[16,192,128]{2,1,0:T(8,128)(2,1)} custom-call(bf16[3,128,256]{2,1,0:T(8,128)(2,1)S(1)} %copy-done.4), custom_call_target="tpu_custom_call" | custom-call | flops 100000000 | bytes 500000 | tf_op jit(solution)/shard_map/pallas_call | solution.py:80
  5.6 12.6 %all-to-all-start = ((bf16[16,192,128]{2,1,0:T(8,128)(2,1)}), bf16[16,192,128]{2,1,0:T(8,128)(2,1)S(1)}, u32[]{:S(2)}, u32[]{:S(2)}) async-start(bf16[16,192,128]{2,1,0:T(8,128)(2,1)} %shard_map.73), calls=%async_computation | async-start | bytes 1572864 | tf_op jit(solution)/shard_map/all_to_all | solution.py:304
  18.2 0.0 collective-permute-done.t1
  18.2 0.8 constant_dynamic-slice_fusion.1
  19.1 3.8 %collective-permute-start.2 = (bf16[128,2048]{1,0:T(8,128)(2,1)}, bf16[128,2048]{1,0:T(8,128)(2,1)S(1)}, u32[]{:S(2)}, u32[]{:S(2)}) collective-permute-start(bf16[128,2048]{1,0:T(8,128)(2,1)} %constant_dynamic-slice_fusion.1), channel_id=1, source_target_pairs={{0,128},{1,385},{2,130},{3,387},{4,132},{5,389},{6,134},{7,391},{8... | collective-permute-start | bytes 1572872 | tf_op jit(solution)/shard_map/ppermute | solution.py:310
  22.9 1.9 %collective-permute-start.1 = (bf16[128,4096]{1,0:T(8,128)(2,1)S(1)}, bf16[128,4096]{1,0:T(8,128)(2,1)}, u32[]{:S(2)}, u32[]{:S(2)}) collective-permute-start(bf16[128,4096]{1,0:T(8,128)(2,1)S(1)} %collective-permute-done.t1), channel_id=1, source_target_pairs={{0,1},{1,0},{2,3},{3,2},{4,5},{5,4},{6,7},{7,6},{8,9},{9,8},{10,11... | collective-permute-start | bytes 3145736 | tf_op jit(solution)/shard_map/ppermute | solution.py:309
  24.8 13.6 %all-to-all-done.blocks_ref = bf16[16,192,128]{2,1,0:T(8,128)(2,1)S(1)} async-done(((bf16[16,192,128]{2,1,0:T(8,128)(2,1)}), bf16[16,192,128]{2,1,0:T(8,128)(2,1)S(1)}, u32[]{:S(2)}, u32[]{:S(2)}) %all-to-all-start) | async-done | bytes 786464 | tf_op jit(solution)/shard_map/all_to_all | solution.py:304
  38.4 6.5 %collective-permute-start.4 = (bf16[16,192,128]{2,1,0:T(8,128)(2,1)S(1)}, bf16[16,192,128]{2,1,0:T(8,128)(2,1)}, u32[]{:S(2)}, u32[]{:S(2)}) collective-permute-start(bf16[16,192,128]{2,1,0:T(8,128)(2,1)S(1)} %all-to-all-done.blocks_ref), channel_id=1, source_target_pairs={{0,16},{1,113},{2,18},{3,115},{4,20},{5,117},{6,22},{7,119},{8,24}... | collective-permute-start | bytes 2359304 | tf_op jit(solution)/shard_map/ppermute | solution.py:308
  44.9 0.0 collective-permute-done.2.t3
  44.9 1.9 %collective-permute-start.3 = (bf16[128,2048]{1,0:T(8,128)(2,1)S(1)}, bf16[128,2048]{1,0:T(8,128)(2,1)}, u32[]{:S(2)}, u32[]{:S(2)}) collective-permute-start(bf16[128,2048]{1,0:T(8,128)(2,1)S(1)} %collective-permute-done.2.t3), channel_id=1, source_target_pairs={{0,1},{1,0},{2,3},{3,2},{4,5},{5,4},{6,7},{7,6},{8,9},{9,8},{10,11... | collective-permute-start | bytes 1572872 | tf_op jit(solution)/shard_map/ppermute | solution.py:311
  46.9 0.1 copy.9
  47.0 0.1 dynamic-slice_bitcast_fusion
  47.1 0.1 pad_maximum_fusion.a_ref
  47.2 0.8 bitcast_multiply_fusion
  47.9 0.9 %collective-permute-done.3.t4 = bf16[128,2048]{1,0:T(8,128)(2,1)} collective-permute-done((bf16[128,2048]{1,0:T(8,128)(2,1)S(1)}, bf16[128,2048]{1,0:T(8,128)(2,1)}, u32[]{:S(2)}, u32[]{:S(2)}) %collective-permute-start.3) | collective-permute-done | bytes 524320 | tf_op jit(solution)/shard_map/ppermute | solution.py:311
  48.9 0.0 collective-permute-done.1.t2
  48.9 2.2 %shard_map.74 = (f32[512,256]{1,0:T(8,128)S(1)}, bf16[512,2048]{1,0:T(8,128)(2,1)S(1)}, f32[16,128,128]{2,1,0:T(8,128)S(1)}) custom-call(bf16[128,4096]{1,0:T(8,128)(2,1)S(1)} %copy-done.1, bf16[128,4096]{1,0:T(8,128)(2,1)S(1)} %collective-permute-done.t1, bf16[128,4096]{1,0:T(8,128)(2,1)} %collective-permute-done.1.t2, ...), custom_call_target="tpu_custom_call" | custom-call | flops 100000000 | bytes 500000 | tf_op jit(solution)/shard_map/pallas_call | solution.py:80
  51.0 3.4 %collective-permute-done.4.blocks_ref = bf16[16,192,128]{2,1,0:T(8,128)(2,1)} collective-permute-done((bf16[16,192,128]{2,1,0:T(8,128)(2,1)S(1)}, bf16[16,192,128]{2,1,0:T(8,128)(2,1)}, u32[]{:S(2)}, u32[]{:S(2)}) %collective-permute-start.4) | collective-permute-done | bytes 786464 | tf_op jit(solution)/shard_map/ppermute | solution.py:308
  54.4 3.0 %shard_map.75 = (bf16[3,128,256]{2,1,0:T(8,128)(2,1)S(1)}, f32[8,32,128]{2,1,0:T(8,128)}) custom-call(bf16[512,2048]{1,0:T(8,128)(2,1)S(1)} %get-tuple-element.13.rest_ref, f32[512,256]{1,0:T(8,128)S(1)} %get-tuple-element.14.product_ref, bf16[16,192,128]{2,1,0:T(8,128)(2,1)} %collective-permute-done.4.blocks_ref, f32[16,128,128]{2,1,0:T(8,128)S(1)} %get-tuple-element.15.into_ref), custom_call_target="tpu_custom_call" | custom-call | flops 100000000 | bytes 500000 | tf_op jit(solution)/shard_map/pallas_call | solution.py:80
  57.4 4.5 %collective-permute-start.5 = (bf16[3,128,256]{2,1,0:T(8,128)(2,1)S(1)}, bf16[3,128,256]{2,1,0:T(8,128)(2,1)S(1)}, u32[]{:S(2)}, u32[]{:S(2)}) collective-permute-start(bf16[3,128,256]{2,1,0:T(8,128)(2,1)S(1)} %get-tuple-element.16.streams_ref), channel_id=1, source_target_pairs={{0,16},{16,32},{32,48},{48,64},{64,80},{80,96},{96,112},{112,0},{1... | collective-permute-start | bytes 589832 | tf_op jit(solution)/shard_map/ppermute | solution.py:353
  61.8 3.4 %all-to-all-start.1 = ((f32[8,32,128]{2,1,0:T(8,128)}), f32[8,32,128]{2,1,0:T(8,128)S(1)}, u32[]{:S(2)}, u32[]{:S(2)}) async-start(f32[8,32,128]{2,1,0:T(8,128)} %get-tuple-element.18), calls=%async_computation.1 | async-start | bytes 262144 | tf_op jit(solution)/shard_map/all_to_all | solution.py:351
  65.2 0.1 pad_maximum_fusion.1.w_ref
  65.3 0.1 maximum_convert_fusion.taps_ref
  65.4 0.6 shard_map.76
  66.0 0.5 shard_map.77.local_ref
  66.5 0.0 collective-permute-done.5.arrived_ref
  66.5 7.7 %all-to-all-done.1.states_ref = f32[8,32,128]{2,1,0:T(8,128)S(1)} async-done(((f32[8,32,128]{2,1,0:T(8,128)}), f32[8,32,128]{2,1,0:T(8,128)S(1)}, u32[]{:S(2)}, u32[]{:S(2)}) %all-to-all-start.1) | async-done | bytes 131104 | tf_op jit(solution)/shard_map/all_to_all | solution.py:351
  74.2 1.4 %shard_map.78 = bf16[4,64,128]{2,1,0:T(8,128)(2,1)S(1)} custom-call(bf16[3,128,256]{2,1,0:T(8,128)(2,1)S(1)} %get-tuple-element.16.streams_ref, f32[128,256]{1,0:T(8,128)S(1)} %shard_map.77.local_ref, bf16[3,128,256]{2,1,0:T(8,128)(2,1)S(1)} %collective-permute-done.5.arrived_ref, f32[8,32,128]{2,1,0:T(8,128)S(1)} %all-to-all-done.1.states_ref, ...), custom_call_target="tpu_custom_call" | custom-call | flops 100000000 | bytes 500000 | tf_op jit(solution)/shard_map/pallas_call | solution.py:80
  75.6 8.0 %all_to_all.15.packed_ref = bf16[4,64,128]{2,1,0:T(8,128)(2,1)S(1)} all-to-all(bf16[4,64,128]{2,1,0:T(8,128)(2,1)S(1)} %shard_map.78), channel_id=1, replica_groups={{0,128,256,384},{16,144,272,400},{32,160,288,416},{48,176,304,432},{64,..., dimensions={0} | all-to-all | bytes 131072 | tf_op jit(solution)/shard_map/all_to_all | solution.py:369
  83.6 0.7 shard_map.79
  (12 shorter events, 0.0 us)
Async XLA Ops:
  0.0 46.9 %copy-start = (bf16[256,128]{1,0:T(8,128)(2,1)S(1)}, bf16[256,128]{1,0:T(8,128)(2,1)}, u32[]{:S(2)}) copy-start(bf16[256,128]{1,0:T(8,128)(2,1)} %param.11) | copy-start | bytes 196612
  0.0 48.9 %copy-start.1 = (bf16[128,4096]{1,0:T(8,128)(2,1)S(1)}, bf16[128,4096]{1,0:T(8,128)(2,1)}, u32[]{:S(2)}) copy-start(bf16[128,4096]{1,0:T(8,128)(2,1)} %t0.1) | copy-start | bytes 3145732
  0.0 18.2 %collective-permute-start = (bf16[128,4096]{1,0:T(8,128)(2,1)}, bf16[128,4096]{1,0:T(8,128)(2,1)S(1)}, u32[]{:S(2)}, u32[]{:S(2)}) collective-permute-start(bf16[128,4096]{1,0:T(8,128)(2,1)} %t0.1), channel_id=1, source_target_pairs={{0,128},{1,385},{2,130},{3,387},{4,132},{5,389},{6,134},{7,391},{8... | collective-permute-start | bytes 3145736 | tf_op jit(solution)/shard_map/ppermute | solution.py:296
  3.5 0.9 %copy-start.4 = (bf16[3,128,256]{2,1,0:T(8,128)(2,1)S(1)}, bf16[3,128,256]{2,1,0:T(8,128)(2,1)}, u32[]{:S(2)}) copy-start(bf16[3,128,256]{2,1,0:T(8,128)(2,1)} %w_ref.1) | copy-start | bytes 589828
  4.5 42.5 %copy-start.5 = (f32[256,16]{0,1:T(8,128)S(1)}, f32[256,16]{0,1:T(8,128)}, u32[]{:S(2)}) copy-start(f32[256,16]{0,1:T(8,128)} %param.9) | copy-start | bytes 49156
  5.6 32.8 %all-to-all-start = ((bf16[16,192,128]{2,1,0:T(8,128)(2,1)}), bf16[16,192,128]{2,1,0:T(8,128)(2,1)S(1)}, u32[]{:S(2)}, u32[]{:S(2)}) async-start(bf16[16,192,128]{2,1,0:T(8,128)(2,1)} %shard_map.73), calls=%async_computation | async-start | bytes 1572864 | tf_op jit(solution)/shard_map/all_to_all | solution.py:304
  19.1 25.8 %collective-permute-start.2 = (bf16[128,2048]{1,0:T(8,128)(2,1)}, bf16[128,2048]{1,0:T(8,128)(2,1)S(1)}, u32[]{:S(2)}, u32[]{:S(2)}) collective-permute-start(bf16[128,2048]{1,0:T(8,128)(2,1)} %constant_dynamic-slice_fusion.1), channel_id=1, source_target_pairs={{0,128},{1,385},{2,130},{3,387},{4,132},{5,389},{6,134},{7,391},{8... | collective-permute-start | bytes 1572872 | tf_op jit(solution)/shard_map/ppermute | solution.py:310
  22.9 26.0 %collective-permute-start.1 = (bf16[128,4096]{1,0:T(8,128)(2,1)S(1)}, bf16[128,4096]{1,0:T(8,128)(2,1)}, u32[]{:S(2)}, u32[]{:S(2)}) collective-permute-start(bf16[128,4096]{1,0:T(8,128)(2,1)S(1)} %collective-permute-done.t1), channel_id=1, source_target_pairs={{0,1},{1,0},{2,3},{3,2},{4,5},{5,4},{6,7},{7,6},{8,9},{9,8},{10,11... | collective-permute-start | bytes 3145736 | tf_op jit(solution)/shard_map/ppermute | solution.py:309
  38.4 16.0 %collective-permute-start.4 = (bf16[16,192,128]{2,1,0:T(8,128)(2,1)S(1)}, bf16[16,192,128]{2,1,0:T(8,128)(2,1)}, u32[]{:S(2)}, u32[]{:S(2)}) collective-permute-start(bf16[16,192,128]{2,1,0:T(8,128)(2,1)S(1)} %all-to-all-done.blocks_ref), channel_id=1, source_target_pairs={{0,16},{1,113},{2,18},{3,115},{4,20},{5,117},{6,22},{7,119},{8,24}... | collective-permute-start | bytes 2359304 | tf_op jit(solution)/shard_map/ppermute | solution.py:308
  44.9 3.9 %collective-permute-start.3 = (bf16[128,2048]{1,0:T(8,128)(2,1)S(1)}, bf16[128,2048]{1,0:T(8,128)(2,1)}, u32[]{:S(2)}, u32[]{:S(2)}) collective-permute-start(bf16[128,2048]{1,0:T(8,128)(2,1)S(1)} %collective-permute-done.2.t3), channel_id=1, source_target_pairs={{0,1},{1,0},{2,3},{3,2},{4,5},{5,4},{6,7},{7,6},{8,9},{9,8},{10,11... | collective-permute-start | bytes 1572872 | tf_op jit(solution)/shard_map/ppermute | solution.py:311
  54.4 11.0 %copy-start.2 = (f32[256,256]{1,0:T(8,128)S(1)}, f32[256,256]{1,0:T(8,128)}, u32[]{:S(2)}) copy-start(f32[256,256]{1,0:T(8,128)} %constant.51.clone.fwd_ref) | copy-start | bytes 786436
  54.4 11.6 %copy-start.3 = (f32[256,256]{1,0:T(8,128)S(1)}, f32[256,256]{1,0:T(8,128)}, u32[]{:S(2)}) copy-start(f32[256,256]{1,0:T(8,128)} %constant.52.clone.inv_ref) | copy-start | bytes 786436
  57.4 9.2 %collective-permute-start.5 = (bf16[3,128,256]{2,1,0:T(8,128)(2,1)S(1)}, bf16[3,128,256]{2,1,0:T(8,128)(2,1)S(1)}, u32[]{:S(2)}, u32[]{:S(2)}) collective-permute-start(bf16[3,128,256]{2,1,0:T(8,128)(2,1)S(1)} %get-tuple-element.16.streams_ref), channel_id=1, source_target_pairs={{0,16},{16,32},{32,48},{48,64},{64,80},{80,96},{96,112},{112,0},{1... | collective-permute-start | bytes 589832 | tf_op jit(solution)/shard_map/ppermute | solution.py:353
  61.8 12.4 %all-to-all-start.1 = ((f32[8,32,128]{2,1,0:T(8,128)}), f32[8,32,128]{2,1,0:T(8,128)S(1)}, u32[]{:S(2)}, u32[]{:S(2)}) async-start(f32[8,32,128]{2,1,0:T(8,128)} %get-tuple-element.18), calls=%async_computation.1 | async-start | bytes 262144 | tf_op jit(solution)/shard_map/all_to_all | solution.py:351

commit v5 on v4

--- a/solution.py
+++ b/solution.py
@@ -16,10 +16,9 @@
 HALF = 64
 SPAN = 2 * ROWS
 MODES = 16
+STEP = 8
 
 parity_groups = [[x * NZ + z for x in range(NX) for z in range(p, NZ, 2)] for p in range(2)]
-x_groups = [[x * NZ + z for x in range(NX)] for z in range(NZ)]
-z_groups = [[x * NZ + z for z in range(NZ)] for x in range(NX)]
 
 
 def real_transform():
@@ -112,12 +111,16 @@
             pltpu.make_async_copy(block_ref.at[x], out_ref.at[at], sems.at[at]).wait()
 
 
-def build_tables(a_ref, w_ref, taps_ref, fwd_ref, out_ref, long_ref, short_ref):
-    t = lax.broadcasted_iota(jnp.int32, (ROWS, LANES), 0).astype(f32)
-    impulse = jnp.zeros((ROWS, LANES), f32)
+def build_tables(a_ref, w_ref, taps_ref, fwd_ref, near_ref, far_ref, long_ref, short_ref):
+    channels = a_ref.shape[1]
+    t = lax.broadcasted_iota(jnp.int32, (ROWS, channels), 0).astype(f32)
+    step = lax.broadcasted_iota(jnp.int32, (STEP, channels), 0).astype(f32)
+    block = lax.broadcasted_iota(jnp.int32, (ROWS // STEP, channels), 0).astype(f32) * float(STEP)
+    impulse = jnp.zeros((ROWS, channels), f32)
     for m in range(MODES):
         rate, weight = a_ref[m : m + 1, :], w_ref[m : m + 1, :]
-        out_ref[m] = weight * jnp.exp(-rate * (t + 1.0))
+        near_ref[m] = weight * jnp.exp(-rate * (step + 1.0))
+        far_ref[m] = jnp.exp(-rate * block)
         impulse = impulse + weight * jnp.exp(-rate * t)
     transform = fwd_ref[:, :ROWS]
     long_ref[...] = dot_pair(transform, impulse)
@@ -181,7 +184,7 @@
     wait(rest_ref, 1)
 
 
-def project_rest(rest_ref, product_ref, blocks_ref, into_ref, streams_ref, state_ref, wide_ref, total_ref):
+def project_rest(rest_ref, product_ref, blocks_ref, into_ref, a_ref, streams_ref, carry_ref, wide_ref, total_ref, state_ref):
     widen(blocks_ref, wide_ref)
     total_ref[...] = product_ref[...] + jnp.dot(rest_ref[...], wide_ref[...], preferred_element_type=f32)
     low = lower_lanes((ROWS, LANES))
@@ -196,86 +199,99 @@
         for k, value in enumerate((gate_in, values, gate_out)):
             streams_ref[k, :, lanes] = value.astype(bf16)
         for m in range(MODES):
-            state = jnp.sum(signal * into_ref[m], axis=0, keepdims=True)
-            for z in range(NZ):
-                state_ref[z, pair * MODES + m : pair * MODES + m + 1, :] = state
-
-
-def filter_inside(streams_ref, fwd_ref, inv_ref, long_ref):
-    signal = streams_ref[0].astype(f32) * streams_ref[1].astype(f32)
-    spectrum = dot_pair(fwd_ref[:, :ROWS], signal)
+            state_ref[pair, m : m + 1, :] = jnp.sum(signal * into_ref[m], axis=0, keepdims=True)
+    share_states(state_ref, a_ref, carry_ref)
+
+
+def share_states(state_ref, a_ref, carry_ref):
+    _, here, _ = positions()
+    here = here.astype(f32)
+    rate = a_ref[...] * float(ROWS)
+    low = lower_lanes((MODES, LANES))
+    nothing = jnp.zeros((MODES, LANES), f32)
+    row = jnp.exp(-rate * float(NZ))
+    states, earlier = [], [nothing]
+    for x in range(NX):
+        state = state_ref[x // 2]
+        turned = swap_halves(state)
+        states.append(jnp.where(low, state, turned) if x % 2 == 0 else jnp.where(low, turned, state))
+        earlier.append(states[-1] + row * earlier[-1])
+    same, across = [], []
+    for z in range(NZ):
+        after = z - 1.0 - here
+        same.append(jnp.where(after >= 0.0, jnp.exp(-rate * jnp.maximum(after, 0.0)), 0.0))
+        across.append(jnp.exp(-rate * (z + NZ - 1.0 - here)))
+    last = nothing
+    for x in range(NX):
+        for z in range(NZ):
+            now = same[z] * states[x] + across[z] * earlier[x]
+            carry_ref[x * NZ + z] = jnp.where(low, now, last)
+            last = now
+
+
+def pack(streams_ref, arrived_ref, p0, p1, p2, p3, chunk_ref):
+    x, z, _ = positions()
+    low = lower_lanes((HALF, LANES))
+    chunk_ref[NX] = jnp.zeros(chunk_ref.shape[1:], bf16)
+    for first, ref in ((0, streams_ref), (NX + 1, arrived_ref)):
+        for k in range(3):
+            for pair in range(NX // 2):
+                lanes = slice(LANES * pair, LANES * (pair + 1))
+                top, bottom = ref[k, :HALF, lanes].astype(f32), ref[k, HALF:, lanes].astype(f32)
+                chunk_ref[first + 2 * pair, k] = jnp.where(low, top, swap_halves(bottom)).astype(bf16)
+                chunk_ref[first + 2 * pair + 1, k] = jnp.where(low, swap_halves(top), bottom).astype(bf16)
+    back = jnp.where(z == 0, 1, 0)
+    for k, ref in enumerate((p0, p1, p2, p3)):
+        chunk = lax.rem(x + k, NX)
+        ref[0] = chunk_ref[chunk]
+        ref[1] = chunk_ref[NX + 1 + chunk - back]
+
+
+def finish(p0, p1, p2, p3, carry_ref, near_ref, far_ref, fwd_ref, inv_ref, long_ref, short_ref, out_ref, part_ref):
+    x, _, _ = positions()
+    for k, ref in enumerate((p0, p1, p2, p3)):
+        part_ref[lax.rem(x + NX - k, NX)] = ref[...]
+    low, low_modes = lower_lanes((HALF, LANES)), lower_lanes((MODES, LANES))
+
+    def whole(side, k):
+        columns = []
+        for pair in range(NX // 2):
+            a, b = (part_ref[2 * pair + h, side, k].astype(f32) for h in range(2))
+            top, bottom = jnp.where(low, a, swap_halves(b)), jnp.where(low, swap_halves(a), b)
+            columns.append(jnp.concatenate([top, bottom], axis=0))
+        return jnp.concatenate(columns, axis=1)
+
+    signal = jnp.concatenate([whole(side, 0) * whole(side, 1) for side in range(2)], axis=1)
     response = jnp.concatenate([long_ref[...]] * 2, axis=1)
-    return dot_pair(inv_ref[:ROWS, :], multiply_spectra(spectrum, response))
-
-
-def filter_chunks(streams_ref, fwd_ref, inv_ref, long_ref, local_ref):
-    local_ref[...] = filter_inside(streams_ref, fwd_ref, inv_ref, long_ref)
-
-
-def carry_in(states_ref, a_ref, z):
-    low = lower_lanes((MODES, LANES))
-    rate = a_ref[...] * float(ROWS)
-    decay = jnp.exp(-rate)
-    decay_row = jnp.exp(-rate * float(NZ))
-    decay_here = jnp.exp(-rate * z.astype(f32))
-    before, whole = [], []
-    for pair in range(NX // 2):
-        upto = jnp.zeros((MODES, LANES), f32)
-        total = jnp.zeros((MODES, LANES), f32)
-        for k in range(NZ):
-            step = states_ref[k, pair * MODES : (pair + 1) * MODES, :]
-            upto = jnp.where(k < z, upto * decay + step, upto)
-            total = total * decay + step
-        before.append(upto)
-        whole.append(total)
-    swapped = [swap_halves(v) for v in whole]
-    first = jnp.where(low, 0.0, swapped[0])
-    second = jnp.where(
-        low,
-        swapped[0] + decay_row * whole[0],
-        swapped[1] + decay_row * (whole[0] + decay_row * swapped[0]),
-    )
-    return [before[0] + decay_here * first, before[1] + decay_here * second]
-
-
-def gate_rows(streams_ref, local, carries, out_ref):
-    parts = []
-    for pair in range(NX // 2):
-        lanes = slice(LANES * pair, LANES * (pair + 1))
-        value = local[:, lanes]
-        for m in range(MODES):
-            value = value + out_ref[m] * carries[pair][m : m + 1, :]
-        parts.append((streams_ref[2, :, lanes].astype(f32) * value).astype(bf16).astype(f32))
-    return parts
-
-
-def finish(streams_ref, local_ref, arrived_ref, states_ref, a_ref, out_ref, fwd_ref, inv_ref, long_ref, short_ref, packed_ref):
-    _, z, _ = positions()
-    low = lower_lanes((ROWS, LANES))
-    before = filter_inside(arrived_ref, fwd_ref, inv_ref, long_ref)
-    own = gate_rows(streams_ref, local_ref[...], carry_in(states_ref, a_ref, z), out_ref)
-    arrived = gate_rows(arrived_ref, before, carry_in(states_ref, a_ref, lax.rem(z + NZ - 1, NZ)), out_ref)
-    turned = [swap_halves(v) for v in arrived]
-    shifted = [jnp.where(low, 0.0, turned[0]), jnp.where(low, turned[0], turned[1])]
-    previous = jnp.concatenate([jnp.where(z == 0, s, a) for s, a in zip(shifted, arrived)], axis=1)
-    window = jnp.concatenate([previous, jnp.concatenate(own, axis=1)], axis=0).astype(bf16)
-    response = jnp.concatenate([short_ref[...]] * 2, axis=1)
-    mixed = dot_pair(inv_ref[ROWS:, :], multiply_spectra(dot_pair(fwd_ref[...], window), response))
-    low_half = lower_lanes((HALF, LANES))
-    for pair in range(2):
-        top = mixed[:HALF, LANES * pair : LANES * (pair + 1)]
-        bottom = mixed[HALF:, LANES * pair : LANES * (pair + 1)]
-        packed_ref[2 * pair] = jnp.where(low_half, top, swap_halves(bottom)).astype(bf16)
-        packed_ref[2 * pair + 1] = jnp.where(low_half, swap_halves(top), bottom).astype(bf16)
-
-
-def unpack_rows(packed_ref, out_ref):
-    low = lower_lanes((HALF, LANES))
-    for pair in range(2):
-        a, b = (packed_ref[2 * pair + h].astype(f32) for h in range(2))
-        lanes = slice(LANES * pair, LANES * (pair + 1))
-        out_ref[:HALF, lanes] = jnp.where(low, a, swap_halves(b)).astype(bf16)
-        out_ref[HALF:, lanes] = jnp.where(low, swap_halves(a), b).astype(bf16)
+    local = dot_pair(inv_ref[:ROWS, :], multiply_spectra(dot_pair(fwd_ref[:, :ROWS], signal), response))
+    carries = []
+    for group in range(NX):
+        total = carry_ref[group * NZ]
+        for z in range(1, NZ):
+            total = total + carry_ref[group * NZ + z]
+        carries.append(total)
+    gated = []
+    for side in range(2):
+        columns = []
+        for pair in range(NX // 2):
+            a, b = carries[2 * pair], carries[2 * pair + 1]
+            if side == 0:
+                carry = jnp.where(low_modes, a, swap_halves(b))
+            else:
+                carry = jnp.where(low_modes, swap_halves(a), b)
+            lanes = slice(LANES * pair, LANES * (pair + 1))
+            heads = [near_ref[m, :, lanes] * carry[m : m + 1, :] for m in range(MODES)]
+            blocks = []
+            for i in range(ROWS // STEP):
+                value = local[STEP * i : STEP * (i + 1), 2 * LANES * side + LANES * pair : 2 * LANES * side + LANES * (pair + 1)]
+                for m in range(MODES):
+                    value = value + heads[m] * far_ref[m, i : i + 1, lanes]
+                blocks.append(value)
+            columns.append(jnp.concatenate(blocks, axis=0))
+        gated.append((whole(side, 2) * jnp.concatenate(columns, axis=1)).astype(bf16))
+    window = jnp.concatenate([gated[1], gated[0]], axis=0)
+    mixed = dot_pair(inv_ref[ROWS:, :], multiply_spectra(dot_pair(fwd_ref[...], window), short_ref[...]))
+    out_ref[...] = mixed.astype(bf16)
 
 
 def per_device(tokens, projections, decay_rates, residues, short_filter):
@@ -284,6 +300,7 @@
     core = lax.axis_index("ch") % NC
     rows, features = tokens.shape
     width = features // NC
+    count = NX * NZ
     wide = lax.axis_size("ch")
 
     def place(a, b, k):
@@ -311,13 +328,22 @@
     other = lax.ppermute(half, "ch", swap)
 
     rates = lax.dynamic_slice_in_dim(decay_rates, x * HALF, HALF, 0).T
-    weights = lax.dynamic_slice_in_dim(residues, x * HALF, HALF, 0).T * jnp.sqrt(2.0 * rates)
-    taps = lax.dynamic_slice_in_dim(short_filter, x * HALF, HALF, 0).T.astype(f32)
-    rates, weights, taps = (jnp.concatenate([v, v], axis=1) for v in (rates, weights, taps))
+    rates = jnp.concatenate([rates, rates], axis=1)
+    all_rates = decay_rates.T
+    all_weights = residues.T * jnp.sqrt(2.0 * all_rates)
+    taps = short_filter.T.astype(f32)
+    channels = all_rates.shape[1]
     forward, inverse = jnp.asarray(real_transform()), jnp.asarray(inverse_transform())
     table = sds((MODES, ROWS, LANES), f32)
-    spectrum = sds((SPAN, LANES), f32)
-    out, long_spectrum, short_spectrum = call(build_tables, (table, spectrum, spectrum), rates, weights, taps, forward)
+    spectrum = sds((SPAN, channels), f32)
+    steps, jumps, long_spectrum, short_spectrum = call(
+        build_tables,
+        (sds((MODES, STEP, channels), f32), sds((MODES, ROWS // STEP, channels), f32), spectrum, spectrum),
+        all_rates,
+        all_weights,
+        taps,
+        forward,
+    )
     half_depth = BLOCKS * ROWS
     product, rest, into = call(
         project_first,
@@ -336,38 +362,42 @@
         ],
         far=5,
     )
-    streams, states = call(
+    streams, carries = call(
         project_rest,
-        (sds((3, ROWS, 2 * LANES), bf16), sds((NZ, 2 * MODES, LANES), f32)),
+        (sds((3, ROWS, 2 * LANES), bf16), sds((count, MODES, LANES), f32)),
         rest,
         product,
         rest_blocks,
         into,
+        rates,
         scratch=[
             pltpu.VMEM((half_depth, 2 * LANES), bf16),
             pltpu.VMEM((NX * rows, 2 * LANES), f32),
+            pltpu.VMEM((NX // 2, MODES, LANES), f32),
         ],
     )
-    states = lax.all_to_all(states, "ctx", 0, 0, tiled=True, axis_index_groups=z_groups)
     onward = [(a * NZ + b, a * NZ + (b + 1) % NZ) for a in range(NX) for b in range(NZ)]
     arrived = lax.ppermute(streams, "ctx", onward)
-    local = call(filter_chunks, sds((ROWS, 2 * LANES), f32), streams, forward, inverse, long_spectrum)
-    packed = call(
+    carries = lax.all_to_all(carries, "ctx", 0, 0, tiled=True)
+    piece = sds((2, 3, HALF, LANES), bf16)
+    pieces = call(pack, (piece,) * NX, streams, arrived, scratch=[pltpu.VMEM((2 * NX + 1, 3, HALF, LANES), bf16)])
+    moved = [pieces[0]] + [None] * (NX - 1)
+    for k in (2, 1, 3):
+        turn = [(a * NZ + b, (a + k) % NX * NZ + b) for a in range(NX) for b in range(NZ)]
+        moved[k] = lax.ppermute(pieces[k], "ctx", turn)
+    return call(
         finish,
-        sds((NX, HALF, LANES), bf16),
-        streams,
-        local,
-        arrived,
-        states,
-        rates,
-        out,
+        sds((ROWS, 2 * LANES), bf16),
+        *moved,
+        carries,
+        steps,
+        jumps,
         forward,
         inverse,
         long_spectrum,
         short_spectrum,
+        scratch=[pltpu.VMEM((NX, 2, 3, HALF, LANES), bf16)],
     )
-    packed = lax.all_to_all(packed, "ctx", 0, 0, tiled=True, axis_index_groups=x_groups)
-    return call(unpack_rows, sds((ROWS, 2 * LANES), bf16), packed)
 
 
 def solution(mesh):

time: 85 us -> 93.5 us (1.10)
  the two profiles are of different devices: /device:TPU:32 before, /device:TPU:48 now
where the time goes in v5:
time: 93.5 us; the launch traced here: 92.8 us
  starting transfers between devices  50.4 us (54%)
  waiting for transfers between devices  30.6 us (33%)
  Pallas kernels  9.45 us (10%)
  local copies, waits for them, and re-layouts  1.96 us (2%)
    all_to_all x1, waiting for transfers between devices, per_device(): lax.all_to_all(blocks, 'ctx', 0, 0, tiled=True, axis_index_groups=parity_...  13.6 us
    all_to_all x1, starting transfers between devices, per_device(): lax.all_to_all(blocks, 'ctx', 0, 0, tiled=True, axis_index_groups=parity_...  12.6 us
    ppermute x3, starting transfers between devices, per_device(): moved[k] = lax.ppermute(pieces[k], 'ctx', turn)  11.4 us
    pallas_call x6, Pallas kernels, call(): pl.pallas_call(body, out_shape=outs, in_specs=[ANY] * far + [VMEM] * (len...  9.45 us
    ppermute x1, waiting for transfers between devices, per_device(): arrived = lax.ppermute(streams, 'ctx', onward)  9.45 us
    ppermute x1, starting transfers between devices, per_device(): rest_blocks = lax.ppermute(blocks, ('ctx', 'ch'), across)  6.47 us
    all_to_all x1, starting transfers between devices, per_device(): carries = lax.all_to_all(carries, 'ctx', 0, 0, tiled=True)  5.16 us
    ppermute x1, starting transfers between devices, per_device(): lax.ppermute(lax.dynamic_slice_in_dim(near, core * width, width, 1), ('ct...  3.8 us
  transfers between devices with their start and end apart: 11, of which 5 were waited for; matrix products, arithmetic and copies ran while one was open for 1% of the time, Pallas kernels for 5%

profile of v5, /device:TPU:48, one launch (start us, length us, event | category | flops | bytes accessed | tf_op | source)
XLA Modules:
  0.0 92.8 jit_solution(12006398714830546016)
XLA Ops:
  0.0 3.5 %collective-permute-start = (bf16[128,4096]{1,0:T(8,128)(2,1)}, bf16[128,4096]{1,0:T(8,128)(2,1)S(1)}, u32[]{:S(2)}, u32[]{:S(2)}) collective-permute-start(bf16[128,4096]{1,0:T(8,128)(2,1)} %t0.1), channel_id=1, source_target_pairs={{0,128},{1,385},{2,130},{3,387},{4,132},{5,389},{6,134},{7,391},{8... | collective-permute-start | bytes 3145736 | tf_op jit(solution)/shard_map/ppermute | solution.py:313
  3.5 0.9 copy-done.3
  4.5 1.1 %shard_map.73 = bf16[16,192,128]{2,1,0:T(8,128)(2,1)} custom-call(bf16[3,128,256]{2,1,0:T(8,128)(2,1)S(1)} %copy-done.3), custom_call_target="tpu_custom_call" | custom-call | flops 100000000 | bytes 500000 | tf_op jit(solution)/shard_map/pallas_call | solution.py:79
  5.6 12.6 %all-to-all-start = ((bf16[16,192,128]{2,1,0:T(8,128)(2,1)}), bf16[16,192,128]{2,1,0:T(8,128)(2,1)S(1)}, u32[]{:S(2)}, u32[]{:S(2)}) async-start(bf16[16,192,128]{2,1,0:T(8,128)(2,1)} %shard_map.73), calls=%async_computation | async-start | bytes 1572864 | tf_op jit(solution)/shard_map/all_to_all | solution.py:321
  18.2 0.0 collective-permute-done.t1
  18.2 0.8 constant_dynamic-slice_fusion
  19.1 3.8 %collective-permute-start.2 = (bf16[128,2048]{1,0:T(8,128)(2,1)}, bf16[128,2048]{1,0:T(8,128)(2,1)S(1)}, u32[]{:S(2)}, u32[]{:S(2)}) collective-permute-start(bf16[128,2048]{1,0:T(8,128)(2,1)} %constant_dynamic-slice_fusion), channel_id=1, source_target_pairs={{0,128},{1,385},{2,130},{3,387},{4,132},{5,389},{6,134},{7,391},{8... | collective-permute-start | bytes 1572872 | tf_op jit(solution)/shard_map/ppermute | solution.py:327
  22.9 1.9 %collective-permute-start.1 = (bf16[128,4096]{1,0:T(8,128)(2,1)S(1)}, bf16[128,4096]{1,0:T(8,128)(2,1)}, u32[]{:S(2)}, u32[]{:S(2)}) collective-permute-start(bf16[128,4096]{1,0:T(8,128)(2,1)S(1)} %collective-permute-done.t1), channel_id=1, source_target_pairs={{0,1},{1,0},{2,3},{3,2},{4,5},{5,4},{6,7},{7,6},{8,9},{9,8},{10,11... | collective-permute-start | bytes 3145736 | tf_op jit(solution)/shard_map/ppermute | solution.py:326
  24.8 13.6 %all-to-all-done.blocks_ref = bf16[16,192,128]{2,1,0:T(8,128)(2,1)S(1)} async-done(((bf16[16,192,128]{2,1,0:T(8,128)(2,1)}), bf16[16,192,128]{2,1,0:T(8,128)(2,1)S(1)}, u32[]{:S(2)}, u32[]{:S(2)}) %all-to-all-start) | async-done | bytes 786464 | tf_op jit(solution)/shard_map/all_to_all | solution.py:321
  38.4 6.5 %collective-permute-start.4 = (bf16[16,192,128]{2,1,0:T(8,128)(2,1)S(1)}, bf16[16,192,128]{2,1,0:T(8,128)(2,1)}, u32[]{:S(2)}, u32[]{:S(2)}) collective-permute-start(bf16[16,192,128]{2,1,0:T(8,128)(2,1)S(1)} %all-to-all-done.blocks_ref), channel_id=1, source_target_pairs={{0,16},{1,113},{2,18},{3,115},{4,20},{5,117},{6,22},{7,119},{8,24}... | collective-permute-start | bytes 2359304 | tf_op jit(solution)/shard_map/ppermute | solution.py:325
  44.9 0.0 collective-permute-done.2.t3
  44.9 1.9 %collective-permute-start.3 = (bf16[128,2048]{1,0:T(8,128)(2,1)S(1)}, bf16[128,2048]{1,0:T(8,128)(2,1)}, u32[]{:S(2)}, u32[]{:S(2)}) collective-permute-start(bf16[128,2048]{1,0:T(8,128)(2,1)S(1)} %collective-permute-done.2.t3), channel_id=1, source_target_pairs={{0,1},{1,0},{2,3},{3,2},{4,5},{5,4},{6,7},{7,6},{8,9},{9,8},{10,11... | collective-permute-start | bytes 1572872 | tf_op jit(solution)/shard_map/ppermute | solution.py:328
  46.9 0.1 dynamic-slice_bitcast_fusion
  46.9 0.1 pad_maximum_fusion.a_ref
  47.0 1.8 %collective-permute-done.3.t4 = bf16[128,2048]{1,0:T(8,128)(2,1)} collective-permute-done((bf16[128,2048]{1,0:T(8,128)(2,1)S(1)}, bf16[128,2048]{1,0:T(8,128)(2,1)}, u32[]{:S(2)}, u32[]{:S(2)}) %collective-permute-start.3) | collective-permute-done | bytes 524320 | tf_op jit(solution)/shard_map/ppermute | solution.py:328
  48.8 0.0 collective-permute-done.1.t2
  48.8 2.1 %shard_map.74 = (f32[512,256]{1,0:T(8,128)S(1)}, bf16[512,2048]{1,0:T(8,128)(2,1)S(1)}, f32[16,128,128]{2,1,0:T(8,128)S(1)}) custom-call(bf16[128,4096]{1,0:T(8,128)(2,1)S(1)} %copy-done, bf16[128,4096]{1,0:T(8,128)(2,1)S(1)} %collective-permute-done.t1, bf16[128,4096]{1,0:T(8,128)(2,1)} %collective-permute-done.1.t2, ...), custom_call_target="tpu_custom_call" | custom-call | flops 100000000 | bytes 500000 | tf_op jit(solution)/shard_map/pallas_call | solution.py:79
  51.0 3.4 %collective-permute-done.4.blocks_ref = bf16[16,192,128]{2,1,0:T(8,128)(2,1)} collective-permute-done((bf16[16,192,128]{2,1,0:T(8,128)(2,1)S(1)}, bf16[16,192,128]{2,1,0:T(8,128)(2,1)}, u32[]{:S(2)}, u32[]{:S(2)}) %collective-permute-start.4) | collective-permute-done | bytes 786464 | tf_op jit(solution)/shard_map/ppermute | solution.py:325
  54.4 3.0 %shard_map.75 = (bf16[3,128,256]{2,1,0:T(8,128)(2,1)S(1)}, f32[32,16,128]{2,1,0:T(8,128)}) custom-call(bf16[512,2048]{1,0:T(8,128)(2,1)S(1)} %get-tuple-element.18.rest_ref, f32[512,256]{1,0:T(8,128)S(1)} %get-tuple-element.19.product_ref, bf16[16,192,128]{2,1,0:T(8,128)(2,1)} %collective-permute-done.4.blocks_ref, ...), custom_call_target="tpu_custom_call" | custom-call | flops 100000000 | bytes 500000 | tf_op jit(solution)/shard_map/pallas_call | solution.py:79
  57.4 5.2 %all-to-all-start.1 = ((f32[32,16,128]{2,1,0:T(8,128)}), f32[32,16,128]{2,1,0:T(8,128)S(1)}, u32[]{:S(2)}, u32[]{:S(2)}) async-start(f32[32,16,128]{2,1,0:T(8,128)} %get-tuple-element.26), calls=%async_computation.1 | async-start | bytes 524288 | tf_op jit(solution)/shard_map/all_to_all | solution.py:381
  62.6 0.1 copy.8
  62.7 3.7 %collective-permute-start.5 = (bf16[3,128,256]{2,1,0:T(8,128)(2,1)S(1)}, bf16[3,128,256]{2,1,0:T(8,128)(2,1)S(1)}, u32[]{:S(2)}, u32[]{:S(2)}) collective-permute-start(bf16[3,128,256]{2,1,0:T(8,128)(2,1)S(1)} %get-tuple-element.21.streams_ref), channel_id=1, source_target_pairs={{0,16},{16,32},{32,48},{48,64},{64,80},{80,96},{96,112},{112,0},{1... | collective-permute-start | bytes 589832 | tf_op jit(solution)/shard_map/ppermute | solution.py:380
  66.4 9.4 %collective-permute-done.5.arrived_ref = bf16[3,128,256]{2,1,0:T(8,128)(2,1)S(1)} collective-permute-done((bf16[3,128,256]{2,1,0:T(8,128)(2,1)S(1)}, bf16[3,128,256]{2,1,0:T(8,128)(2,1)S(1)}, u32[]{:S(2)}, u32[]{:S(2)}) %collective-permute-start.5) | collective-permute-done | bytes 196640 | tf_op jit(solution)/shard_map/ppermute | solution.py:380
  75.9 0.2 shard_map.76
  76.1 3.4 %collective-permute-start.6 = (bf16[2,3,64,128]{3,2,1,0:T(8,128)(2,1)S(1)}, bf16[2,3,64,128]{3,2,1,0:T(8,128)(2,1)S(1)}, u32[]{:S(2)}, u32[]{:S(2)}) collective-permute-start(bf16[2,3,64,128]{3,2,1,0:T(8,128)(2,1)S(1)} %get-tuple-element.23), channel_id=1, source_target_pairs={{0,128},{16,144},{32,160},{48,176},{64,192},{80,208},{96,224},{112... | collective-permute-start | bytes 294920 | tf_op jit(solution)/shard_map/ppermute | solution.py:387
  79.5 4.7 %collective-permute-start.7 = (bf16[2,3,64,128]{3,2,1,0:T(8,128)(2,1)S(1)}, bf16[2,3,64,128]{3,2,1,0:T(8,128)(2,1)S(1)}, u32[]{:S(2)}, u32[]{:S(2)}) collective-permute-start(bf16[2,3,64,128]{3,2,1,0:T(8,128)(2,1)S(1)} %get-tuple-element.24), channel_id=1, source_target_pairs={{0,256},{16,272},{32,288},{48,304},{64,320},{80,336},{96,352},{112... | collective-permute-start | bytes 294920 | tf_op jit(solution)/shard_map/ppermute | solution.py:387
  84.2 3.3 %collective-permute-start.8 = (bf16[2,3,64,128]{3,2,1,0:T(8,128)(2,1)S(1)}, bf16[2,3,64,128]{3,2,1,0:T(8,128)(2,1)S(1)}, u32[]{:S(2)}, u32[]{:S(2)}) collective-permute-start(bf16[2,3,64,128]{3,2,1,0:T(8,128)(2,1)S(1)} %get-tuple-element.25), channel_id=1, source_target_pairs={{0,384},{16,400},{32,416},{48,432},{64,448},{80,464},{96,480},{112... | collective-permute-start | bytes 294920 | tf_op jit(solution)/shard_map/ppermute | solution.py:387
  87.5 0.8 shard_map.77
  88.3 0.0 collective-permute-done.6.p1
  88.3 0.0 collective-permute-done.7.p2
  88.3 2.4 %collective-permute-done.8.p3 = bf16[2,3,64,128]{3,2,1,0:T(8,128)(2,1)S(1)} collective-permute-done((bf16[2,3,64,128]{3,2,1,0:T(8,128)(2,1)S(1)}, bf16[2,3,64,128]{3,2,1,0:T(8,128)(2,1)S(1)}, u32[]{:S(2)}, u32[]{:S(2)}) %collective-permute-start.8) | collective-permute-done | bytes 98336 | tf_op jit(solution)/shard_map/ppermute | solution.py:387
  90.7 2.2 %shard_map.78 = bf16[128,256]{1,0:T(8,128)(2,1)} custom-call(bf16[2,3,64,128]{3,2,1,0:T(8,128)(2,1)S(1)} %get-tuple-element.22.p0, bf16[2,3,64,128]{3,2,1,0:T(8,128)(2,1)S(1)} %collective-permute-done.6.p1, bf16[2,3,64,128]{3,2,1,0:T(8,128)(2,1)S(1)} %collective-permute-done.7.p2, bf16[2,3,64,128]{3,2,1,0:T(8,128)(2,1)S(1)} %collective-permute-done.8.p3, ...), custom_call_target="tpu_custom_call" | custom-call | flops 100000000 | bytes 500000 | tf_op jit(solution)/shard_map/pallas_call | solution.py:79
  (16 shorter events, 0.1 us)
Async XLA Ops:
  0.0 48.8 %copy-start = (bf16[128,4096]{1,0:T(8,128)(2,1)S(1)}, bf16[128,4096]{1,0:T(8,128)(2,1)}, u32[]{:S(2)}) copy-start(bf16[128,4096]{1,0:T(8,128)(2,1)} %t0.1) | copy-start | bytes 3145732
  0.0 18.2 %collective-permute-start = (bf16[128,4096]{1,0:T(8,128)(2,1)}, bf16[128,4096]{1,0:T(8,128)(2,1)S(1)}, u32[]{:S(2)}, u32[]{:S(2)}) collective-permute-start(bf16[128,4096]{1,0:T(8,128)(2,1)} %t0.1), channel_id=1, source_target_pairs={{0,128},{1,385},{2,130},{3,387},{4,132},{5,389},{6,134},{7,391},{8... | collective-permute-start | bytes 3145736 | tf_op jit(solution)/shard_map/ppermute | solution.py:313
  3.5 0.9 copy-start.3
  4.5 42.4 %copy-start.4 = (f32[256,16]{0,1:T(8,128)S(1)}, f32[256,16]{0,1:T(8,128)}, u32[]{:S(2)}) copy-start(f32[256,16]{0,1:T(8,128)} %param.9) | copy-start | bytes 49156
  5.6 32.8 %all-to-all-start = ((bf16[16,192,128]{2,1,0:T(8,128)(2,1)}), bf16[16,192,128]{2,1,0:T(8,128)(2,1)S(1)}, u32[]{:S(2)}, u32[]{:S(2)}) async-start(bf16[16,192,128]{2,1,0:T(8,128)(2,1)} %shard_map.73), calls=%async_computation | async-start | bytes 1572864 | tf_op jit(solution)/shard_map/all_to_all | solution.py:321
  19.1 25.8 %collective-permute-start.2 = (bf16[128,2048]{1,0:T(8,128)(2,1)}, bf16[128,2048]{1,0:T(8,128)(2,1)S(1)}, u32[]{:S(2)}, u32[]{:S(2)}) collective-permute-start(bf16[128,2048]{1,0:T(8,128)(2,1)} %constant_dynamic-slice_fusion), channel_id=1, source_target_pairs={{0,128},{1,385},{2,130},{3,387},{4,132},{5,389},{6,134},{7,391},{8... | collective-permute-start | bytes 1572872 | tf_op jit(solution)/shard_map/ppermute | solution.py:327
  22.9 26.0 %collective-permute-start.1 = (bf16[128,4096]{1,0:T(8,128)(2,1)S(1)}, bf16[128,4096]{1,0:T(8,128)(2,1)}, u32[]{:S(2)}, u32[]{:S(2)}) collective-permute-start(bf16[128,4096]{1,0:T(8,128)(2,1)S(1)} %collective-permute-done.t1), channel_id=1, source_target_pairs={{0,1},{1,0},{2,3},{3,2},{4,5},{5,4},{6,7},{7,6},{8,9},{9,8},{10,11... | collective-permute-start | bytes 3145736 | tf_op jit(solution)/shard_map/ppermute | solution.py:326
  38.4 16.0 %collective-permute-start.4 = (bf16[16,192,128]{2,1,0:T(8,128)(2,1)S(1)}, bf16[16,192,128]{2,1,0:T(8,128)(2,1)}, u32[]{:S(2)}, u32[]{:S(2)}) collective-permute-start(bf16[16,192,128]{2,1,0:T(8,128)(2,1)S(1)} %all-to-all-done.blocks_ref), channel_id=1, source_target_pairs={{0,16},{1,113},{2,18},{3,115},{4,20},{5,117},{6,22},{7,119},{8,24}... | collective-permute-start | bytes 2359304 | tf_op jit(solution)/shard_map/ppermute | solution.py:325
  44.9 3.9 %collective-permute-start.3 = (bf16[128,2048]{1,0:T(8,128)(2,1)S(1)}, bf16[128,2048]{1,0:T(8,128)(2,1)}, u32[]{:S(2)}, u32[]{:S(2)}) collective-permute-start(bf16[128,2048]{1,0:T(8,128)(2,1)S(1)} %collective-permute-done.2.t3), channel_id=1, source_target_pairs={{0,1},{1,0},{2,3},{3,2},{4,5},{5,4},{6,7},{7,6},{8,9},{9,8},{10,11... | collective-permute-start | bytes 1572872 | tf_op jit(solution)/shard_map/ppermute | solution.py:328
  54.4 8.2 %copy-start.5 = (bf16[256,128]{1,0:T(8,128)(2,1)S(1)}, bf16[256,128]{1,0:T(8,128)(2,1)}, u32[]{:S(2)}) copy-start(bf16[256,128]{1,0:T(8,128)(2,1)} %param.11) | copy-start | bytes 196612
  54.4 33.1 %copy-start.6 = (f32[256,16]{0,1:T(8,128)S(1)}, f32[256,16]{0,1:T(8,128)}, u32[]{:S(2)}) copy-start(f32[256,16]{0,1:T(8,128)} %param.10) | copy-start | bytes 49156
  54.4 33.1 %copy-start.1 = (f32[256,256]{1,0:T(8,128)S(1)}, f32[256,256]{1,0:T(8,128)}, u32[]{:S(2)}) copy-start(f32[256,256]{1,0:T(8,128)} %constant.51.clone.fwd_ref) | copy-start | bytes 786436
  54.4 36.3 %copy-start.2 = (f32[256,256]{1,0:T(8,128)S(1)}, f32[256,256]{1,0:T(8,128)}, u32[]{:S(2)}) copy-start(f32[256,256]{1,0:T(8,128)} %constant.52.clone.inv_ref) | copy-start | bytes 786436
  57.4 33.3 %all-to-all-start.1 = ((f32[32,16,128]{2,1,0:T(8,128)}), f32[32,16,128]{2,1,0:T(8,128)S(1)}, u32[]{:S(2)}, u32[]{:S(2)}) async-start(f32[32,16,128]{2,1,0:T(8,128)} %get-tuple-element.26), calls=%async_computation.1 | async-start | bytes 524288 | tf_op jit(solution)/shard_map/all_to_all | solution.py:381
  62.7 13.2 %collective-permute-start.5 = (bf16[3,128,256]{2,1,0:T(8,128)(2,1)S(1)}, bf16[3,128,256]{2,1,0:T(8,128)(2,1)S(1)}, u32[]{:S(2)}, u32[]{:S(2)}) collective-permute-start(bf16[3,128,256]{2,1,0:T(8,128)(2,1)S(1)} %get-tuple-element.21.streams_ref), channel_id=1, source_target_pairs={{0,16},{16,32},{32,48},{48,64},{64,80},{80,96},{96,112},{112,0},{1... | collective-permute-start | bytes 589832 | tf_op jit(solution)/shard_map/ppermute | solution.py:380
  76.1 12.2 %collective-permute-start.6 = (bf16[2,3,64,128]{3,2,1,0:T(8,128)(2,1)S(1)}, bf16[2,3,64,128]{3,2,1,0:T(8,128)(2,1)S(1)}, u32[]{:S(2)}, u32[]{:S(2)}) collective-permute-start(bf16[2,3,64,128]{3,2,1,0:T(8,128)(2,1)S(1)} %get-tuple-element.23), channel_id=1, source_target_pairs={{0,128},{16,144},{32,160},{48,176},{64,192},{80,208},{96,224},{112... | collective-permute-start | bytes 294920 | tf_op jit(solution)/shard_map/ppermute | solution.py:387
  79.5 8.8 %collective-permute-start.7 = (bf16[2,3,64,128]{3,2,1,0:T(8,128)(2,1)S(1)}, bf16[2,3,64,128]{3,2,1,0:T(8,128)(2,1)S(1)}, u32[]{:S(2)}, u32[]{:S(2)}) collective-permute-start(bf16[2,3,64,128]{3,2,1,0:T(8,128)(2,1)S(1)} %get-tuple-element.24), channel_id=1, source_target_pairs={{0,256},{16,272},{32,288},{48,304},{64,320},{80,336},{96,352},{112... | collective-permute-start | bytes 294920 | tf_op jit(solution)/shard_map/ppermute | solution.py:387
  84.2 6.5 %collective-permute-start.8 = (bf16[2,3,64,128]{3,2,1,0:T(8,128)(2,1)S(1)}, bf16[2,3,64,128]{3,2,1,0:T(8,128)(2,1)S(1)}, u32[]{:S(2)}, u32[]{:S(2)}) collective-permute-start(bf16[2,3,64,128]{3,2,1,0:T(8,128)(2,1)S(1)} %get-tuple-element.25), channel_id=1, source_target_pairs={{0,384},{16,400},{32,416},{48,432},{64,448},{80,464},{96,480},{112... | collective-permute-start | bytes 294920 | tf_op jit(solution)/shard_map/ppermute | solution.py:387

commit v6 on v4

--- a/solution.py
+++ b/solution.py
@@ -112,16 +112,30 @@
             pltpu.make_async_copy(block_ref.at[x], out_ref.at[at], sems.at[at]).wait()
 
 
-def build_tables(a_ref, w_ref, taps_ref, fwd_ref, out_ref, long_ref, short_ref):
+def own_channels(ref):
+    x, _, _ = positions()
+    found = ref[:, pl.ds(pl.multiple_of(lax.div(x, 2) * LANES, LANES), LANES)]
+    upper = lax.rem(x, 2) == 1
+    low = lower_lanes(found.shape)
+    turned = swap_halves(found)
+    return jnp.where(low, jnp.where(upper, turned, found), jnp.where(upper, found, turned))
+
+
+def build_tables(rates_ref, residues_ref, taps_ref, fwd_ref, out_ref, long_ref, short_ref):
+    x, _, _ = positions()
+    rates = own_channels(rates_ref)
+    weights = own_channels(residues_ref) * jnp.sqrt(2.0 * rates)
     t = lax.broadcasted_iota(jnp.int32, (ROWS, LANES), 0).astype(f32)
     impulse = jnp.zeros((ROWS, LANES), f32)
     for m in range(MODES):
-        rate, weight = a_ref[m : m + 1, :], w_ref[m : m + 1, :]
+        rate, weight = rates[m : m + 1, :], weights[m : m + 1, :]
         out_ref[m] = weight * jnp.exp(-rate * (t + 1.0))
         impulse = impulse + weight * jnp.exp(-rate * t)
+    own = taps_ref[pl.ds(pl.multiple_of(x * HALF, HALF), HALF), :].astype(f32)
+    taps = jnp.concatenate([own, own], axis=0).T
     transform = fwd_ref[:, :ROWS]
     long_ref[...] = dot_pair(transform, impulse)
-    short_ref[...] = dot_pair(transform, taps_ref[...])
+    short_ref[...] = dot_pair(transform, taps)
 
 
 def positions():
@@ -168,8 +182,9 @@
             pl.when(jnp.logical_not(mine))(second.start)
     widen(blocks_ref, wide_ref)
     back = ROWS - 1.0 - lax.broadcasted_iota(jnp.int32, (ROWS, LANES), 0).astype(f32)
+    rates = own_channels(a_ref)
     for m in range(MODES):
-        into_ref[m] = jnp.exp(-a_ref[m : m + 1, :] * back)
+        into_ref[m] = jnp.exp(-rates[m : m + 1, :] * back)
 
     def wait(target, side):
         for k in range(4):
@@ -181,7 +196,7 @@
     wait(rest_ref, 1)
 
 
-def project_rest(rest_ref, product_ref, blocks_ref, into_ref, streams_ref, state_ref, wide_ref, total_ref):
+def project_rest(blocks_ref, rest_ref, product_ref, into_ref, signal_ref, streams_ref, state_ref, wide_ref, total_ref):
     widen(blocks_ref, wide_ref)
     total_ref[...] = product_ref[...] + jnp.dot(rest_ref[...], wide_ref[...], preferred_element_type=f32)
     low = lower_lanes((ROWS, LANES))
@@ -193,7 +208,8 @@
         gate_in, values = jnp.where(low, a, turned_b), jnp.where(low, turned_a, b)
         gate_out = jnp.where(low, total_ref[chunks[0], LANES:], total_ref[chunks[1], LANES:])
         signal = gate_in * values
-        for k, value in enumerate((gate_in, values, gate_out)):
+        signal_ref[:, lanes] = signal
+        for k, value in enumerate((signal, gate_out)):
             streams_ref[k, :, lanes] = value.astype(bf16)
         for m in range(MODES):
             state = jnp.sum(signal * into_ref[m], axis=0, keepdims=True)
@@ -201,20 +217,19 @@
                 state_ref[z, pair * MODES + m : pair * MODES + m + 1, :] = state
 
 
-def filter_inside(streams_ref, fwd_ref, inv_ref, long_ref):
-    signal = streams_ref[0].astype(f32) * streams_ref[1].astype(f32)
+def filter_inside(signal, fwd_ref, inv_ref, long_ref):
     spectrum = dot_pair(fwd_ref[:, :ROWS], signal)
     response = jnp.concatenate([long_ref[...]] * 2, axis=1)
     return dot_pair(inv_ref[:ROWS, :], multiply_spectra(spectrum, response))
 
 
-def filter_chunks(streams_ref, fwd_ref, inv_ref, long_ref, local_ref):
-    local_ref[...] = filter_inside(streams_ref, fwd_ref, inv_ref, long_ref)
+def filter_chunks(signal_ref, fwd_ref, inv_ref, long_ref, local_ref):
+    local_ref[...] = filter_inside(signal_ref[...], fwd_ref, inv_ref, long_ref)
 
 
 def carry_in(states_ref, a_ref, z):
     low = lower_lanes((MODES, LANES))
-    rate = a_ref[...] * float(ROWS)
+    rate = own_channels(a_ref) * float(ROWS)
     decay = jnp.exp(-rate)
     decay_row = jnp.exp(-rate * float(NZ))
     decay_here = jnp.exp(-rate * z.astype(f32))
@@ -245,14 +260,14 @@
         value = local[:, lanes]
         for m in range(MODES):
             value = value + out_ref[m] * carries[pair][m : m + 1, :]
-        parts.append((streams_ref[2, :, lanes].astype(f32) * value).astype(bf16).astype(f32))
+        parts.append((streams_ref[1, :, lanes].astype(f32) * value).astype(bf16).astype(f32))
     return parts
 
 
 def finish(streams_ref, local_ref, arrived_ref, states_ref, a_ref, out_ref, fwd_ref, inv_ref, long_ref, short_ref, packed_ref):
     _, z, _ = positions()
     low = lower_lanes((ROWS, LANES))
-    before = filter_inside(arrived_ref, fwd_ref, inv_ref, long_ref)
+    before = filter_inside(arrived_ref[0], fwd_ref, inv_ref, long_ref)
     own = gate_rows(streams_ref, local_ref[...], carry_in(states_ref, a_ref, z), out_ref)
     arrived = gate_rows(arrived_ref, before, carry_in(states_ref, a_ref, lax.rem(z + NZ - 1, NZ)), out_ref)
     turned = [swap_halves(v) for v in arrived]
@@ -280,7 +295,6 @@
 
 def per_device(tokens, projections, decay_rates, residues, short_filter):
     sds = jax.ShapeDtypeStruct
-    x = lax.axis_index("ctx") // NZ
     core = lax.axis_index("ch") % NC
     rows, features = tokens.shape
     width = features // NC
@@ -310,14 +324,13 @@
     half = lax.ppermute(lax.dynamic_slice_in_dim(near, core * width, width, 1), ("ctx", "ch"), outward)
     other = lax.ppermute(half, "ch", swap)
 
-    rates = lax.dynamic_slice_in_dim(decay_rates, x * HALF, HALF, 0).T
-    weights = lax.dynamic_slice_in_dim(residues, x * HALF, HALF, 0).T * jnp.sqrt(2.0 * rates)
-    taps = lax.dynamic_slice_in_dim(short_filter, x * HALF, HALF, 0).T.astype(f32)
-    rates, weights, taps = (jnp.concatenate([v, v], axis=1) for v in (rates, weights, taps))
+    rates = decay_rates.T
     forward, inverse = jnp.asarray(real_transform()), jnp.asarray(inverse_transform())
     table = sds((MODES, ROWS, LANES), f32)
     spectrum = sds((SPAN, LANES), f32)
-    out, long_spectrum, short_spectrum = call(build_tables, (table, spectrum, spectrum), rates, weights, taps, forward)
+    out, long_spectrum, short_spectrum = call(
+        build_tables, (table, spectrum, spectrum), rates, residues.T, short_filter, forward
+    )
     half_depth = BLOCKS * ROWS
     product, rest, into = call(
         project_first,
@@ -336,12 +349,12 @@
         ],
         far=5,
     )
-    streams, states = call(
+    signal, streams, states = call(
         project_rest,
-        (sds((3, ROWS, 2 * LANES), bf16), sds((NZ, 2 * MODES, LANES), f32)),
+        (sds((ROWS, 2 * LANES), f32), sds((2, ROWS, 2 * LANES), bf16), sds((NZ, 2 * MODES, LANES), f32)),
+        rest_blocks,
         rest,
         product,
-        rest_blocks,
         into,
         scratch=[
             pltpu.VMEM((half_depth, 2 * LANES), bf16),
@@ -351,7 +364,7 @@
     states = lax.all_to_all(states, "ctx", 0, 0, tiled=True, axis_index_groups=z_groups)
     onward = [(a * NZ + b, a * NZ + (b + 1) % NZ) for a in range(NX) for b in range(NZ)]
     arrived = lax.ppermute(streams, "ctx", onward)
-    local = call(filter_chunks, sds((ROWS, 2 * LANES), f32), streams, forward, inverse, long_spectrum)
+    local = call(filter_chunks, sds((ROWS, 2 * LANES), f32), signal, forward, inverse, long_spectrum)
     packed = call(
         finish,
         sds((NX, HALF, LANES), bf16),

time: 85 us -> 80.6 us (0.948)
  the two profiles are of different devices: /device:TPU:32 before, /device:TPU:40 now
where the time goes in v6:
time: 80.6 us; the launch traced here: 80.1 us
  starting transfers between devices  38.2 us (47%)
  waiting for transfers between devices  23.4 us (29%)
  Pallas kernels  8.5 us (11%)
  blocking collectives  8.12 us (10%)
  local copies, waits for them, and re-layouts  1.77 us (2%)
    all_to_all x1, waiting for transfers between devices, per_device(): lax.all_to_all(blocks, 'ctx', 0, 0, tiled=True, axis_index_groups=parity_...  13.6 us
    all_to_all x1, starting transfers between devices, per_device(): lax.all_to_all(blocks, 'ctx', 0, 0, tiled=True, axis_index_groups=parity_...  12.6 us
    pallas_call x7, Pallas kernels, call(): pl.pallas_call(body, out_shape=outs, in_specs=[ANY] * far + [VMEM] * (len...  8.5 us
    all_to_all x1, blocking collectives, per_device(): lax.all_to_all(packed, 'ctx', 0, 0, tiled=True, axis_index_groups=x_groups)  8.12 us
    ppermute x1, starting transfers between devices, per_device(): rest_blocks = lax.ppermute(blocks, ('ctx', 'ch'), across)  6.47 us
    all_to_all x1, starting transfers between devices, per_device(): lax.all_to_all(states, 'ctx', 0, 0, tiled=True, axis_index_groups=z_groups)  4.03 us
    ppermute x1, starting transfers between devices, per_device(): arrived = lax.ppermute(streams, 'ctx', onward)  3.92 us
    ppermute x1, starting transfers between devices, per_device(): lax.ppermute(lax.dynamic_slice_in_dim(near, core * width, width, 1), ('ct...  3.8 us
  transfers between devices with their start and end apart: 8, of which 5 were waited for; matrix products, arithmetic and copies ran while one was open for 1% of the time, Pallas kernels for 6%

profile of v6, /device:TPU:40, one launch (start us, length us, event | category | flops | bytes accessed | tf_op | source)
XLA Modules:
  0.0 80.1 jit_solution(10709381725960513158)
XLA Ops:
  0.0 3.5 %collective-permute-start.1 = (bf16[128,4096]{1,0:T(8,128)(2,1)}, bf16[128,4096]{1,0:T(8,128)(2,1)S(1)}, u32[]{:S(2)}, u32[]{:S(2)}) collective-permute-start(bf16[128,4096]{1,0:T(8,128)(2,1)} %t0.1), channel_id=1, source_target_pairs={{0,128},{1,385},{2,130},{3,387},{4,132},{5,389},{6,134},{7,391},{8... | collective-permute-start | bytes 3145736 | tf_op jit(solution)/shard_map/ppermute | solution.py:310
  3.5 0.0 copy-start.3
  3.5 0.9 %copy-done.3 = bf16[3,128,256]{2,1,0:T(8,128)(2,1)S(1)} copy-done((bf16[3,128,256]{2,1,0:T(8,128)(2,1)S(1)}, bf16[3,128,256]{2,1,0:T(8,128)(2,1)}, u32[]{:S(2)}) %copy-start.3) | copy-done | bytes 196632
  4.5 1.1 %shard_map.73 = bf16[16,192,128]{2,1,0:T(8,128)(2,1)} custom-call(bf16[3,128,256]{2,1,0:T(8,128)(2,1)S(1)} %copy-done.3), custom_call_target="tpu_custom_call" | custom-call | flops 100000000 | bytes 500000 | tf_op jit(solution)/shard_map/pallas_call | solution.py:80
  5.6 12.6 %all-to-all-start = ((bf16[16,192,128]{2,1,0:T(8,128)(2,1)}), bf16[16,192,128]{2,1,0:T(8,128)(2,1)S(1)}, u32[]{:S(2)}, u32[]{:S(2)}) async-start(bf16[16,192,128]{2,1,0:T(8,128)(2,1)} %shard_map.73), calls=%async_computation | async-start | bytes 1572864 | tf_op jit(solution)/shard_map/all_to_all | solution.py:318
  18.2 0.0 collective-permute-done.1.t1
  18.2 0.8 %constant_dynamic-slice_fusion = bf16[128,2048]{1,0:T(8,128)(2,1)} fusion(bf16[128,4096]{1,0:T(8,128)(2,1)S(1)} %collective-permute-done.1.t1, s32[]{:T(128)S(6)} %select_n.11), kind=kLoop, calls=%fused_computation | loop fusion | bytes 1048580 | tf_op jit(solution)/shard_map/dynamic_slice | solution.py:324
  19.1 3.8 %collective-permute-start.3 = (bf16[128,2048]{1,0:T(8,128)(2,1)}, bf16[128,2048]{1,0:T(8,128)(2,1)S(1)}, u32[]{:S(2)}, u32[]{:S(2)}) collective-permute-start(bf16[128,2048]{1,0:T(8,128)(2,1)} %constant_dynamic-slice_fusion), channel_id=1, source_target_pairs={{0,128},{1,385},{2,130},{3,387},{4,132},{5,389},{6,134},{7,391},{8... | collective-permute-start | bytes 1572872 | tf_op jit(solution)/shard_map/ppermute | solution.py:324
  22.9 1.9 %collective-permute-start.2 = (bf16[128,4096]{1,0:T(8,128)(2,1)S(1)}, bf16[128,4096]{1,0:T(8,128)(2,1)}, u32[]{:S(2)}, u32[]{:S(2)}) collective-permute-start(bf16[128,4096]{1,0:T(8,128)(2,1)S(1)} %collective-permute-done.1.t1), channel_id=1, source_target_pairs={{0,1},{1,0},{2,3},{3,2},{4,5},{5,4},{6,7},{7,6},{8,9},{9,8},{10,11... | collective-permute-start | bytes 3145736 | tf_op jit(solution)/shard_map/ppermute | solution.py:323
  24.8 13.6 %all-to-all-done.blocks_ref = bf16[16,192,128]{2,1,0:T(8,128)(2,1)S(1)} async-done(((bf16[16,192,128]{2,1,0:T(8,128)(2,1)}), bf16[16,192,128]{2,1,0:T(8,128)(2,1)S(1)}, u32[]{:S(2)}, u32[]{:S(2)}) %all-to-all-start) | async-done | bytes 786464 | tf_op jit(solution)/shard_map/all_to_all | solution.py:318
  38.4 6.5 %collective-permute-start = (bf16[16,192,128]{2,1,0:T(8,128)(2,1)S(1)}, bf16[16,192,128]{2,1,0:T(8,128)(2,1)S(1)}, u32[]{:S(2)}, u32[]{:S(2)}) collective-permute-start(bf16[16,192,128]{2,1,0:T(8,128)(2,1)S(1)} %all-to-all-done.blocks_ref), channel_id=1, source_target_pairs={{0,16},{1,113},{2,18},{3,115},{4,20},{5,117},{6,22},{7,119},{8,24}... | collective-permute-start | bytes 2359304 | tf_op jit(solution)/shard_map/ppermute | solution.py:322
  44.9 0.0 collective-permute-done.3.t3
  44.9 1.9 %collective-permute-start.4 = (bf16[128,2048]{1,0:T(8,128)(2,1)S(1)}, bf16[128,2048]{1,0:T(8,128)(2,1)S(1)}, u32[]{:S(2)}, u32[]{:S(2)}) collective-permute-start(bf16[128,2048]{1,0:T(8,128)(2,1)S(1)} %collective-permute-done.3.t3), channel_id=1, source_target_pairs={{0,1},{1,0},{2,3},{3,2},{4,5},{5,4},{6,7},{7,6},{8,9},{9,8},{10,11... | collective-permute-start | bytes 1572872 | tf_op jit(solution)/shard_map/ppermute | solution.py:325
  46.8 1.9 %collective-permute-done.4.t4 = bf16[128,2048]{1,0:T(8,128)(2,1)S(1)} collective-permute-done((bf16[128,2048]{1,0:T(8,128)(2,1)S(1)}, bf16[128,2048]{1,0:T(8,128)(2,1)S(1)}, u32[]{:S(2)}, u32[]{:S(2)}) %collective-permute-start.4) | collective-permute-done | bytes 524320 | tf_op jit(solution)/shard_map/ppermute | solution.py:325
  48.7 0.0 collective-permute-done.2.t2
  48.7 0.0 copy-done
  48.7 0.0 copy-done.4
  48.7 2.4 %shard_map.74 = (f32[512,256]{1,0:T(8,128)S(1)}, bf16[512,2048]{1,0:T(8,128)(2,1)S(1)}, f32[16,128,128]{2,1,0:T(8,128)S(1)}) custom-call(bf16[128,4096]{1,0:T(8,128)(2,1)S(1)} %copy-done, bf16[128,4096]{1,0:T(8,128)(2,1)S(1)} %collective-permute-done.1.t1, bf16[128,4096]{1,0:T(8,128)(2,1)} %collective-permute-done.2.t2, ...), custom_call_target="tpu_custom_call" | custom-call | flops 100000000 | bytes 500000 | tf_op jit(solution)/shard_map/pallas_call | solution.py:80
  51.1 3.3 %collective-permute-done.blocks_ref = bf16[16,192,128]{2,1,0:T(8,128)(2,1)S(1)} collective-permute-done((bf16[16,192,128]{2,1,0:T(8,128)(2,1)S(1)}, bf16[16,192,128]{2,1,0:T(8,128)(2,1)S(1)}, u32[]{:S(2)}, u32[]{:S(2)}) %collective-permute-start) | collective-permute-done | bytes 786464 | tf_op jit(solution)/shard_map/ppermute | solution.py:322
  54.4 1.8 %shard_map.75 = (f32[128,256]{1,0:T(8,128)S(1)}, bf16[2,128,256]{2,1,0:T(8,128)(2,1)S(1)}, f32[8,32,128]{2,1,0:T(8,128)}) custom-call(bf16[16,192,128]{2,1,0:T(8,128)(2,1)S(1)} %collective-permute-done.blocks_ref, bf16[512,2048]{1,0:T(8,128)(2,1)S(1)} %get-tuple-element.14.rest_ref, f32[512,256]{1,0:T(8,128)S(1)} %get-tuple-element.15.product_ref, ...), custom_call_target="tpu_custom_call" | custom-call | flops 100000000 | bytes 500000 | tf_op jit(solution)/shard_map/pallas_call | solution.py:80
  56.1 4.0 %all-to-all-start.1 = ((f32[8,32,128]{2,1,0:T(8,128)}), f32[8,32,128]{2,1,0:T(8,128)S(1)}, u32[]{:S(2)}, u32[]{:S(2)}) async-start(f32[8,32,128]{2,1,0:T(8,128)} %get-tuple-element.20), calls=%async_computation.1 | async-start | bytes 262144 | tf_op jit(solution)/shard_map/all_to_all | solution.py:364
  60.2 3.9 %collective-permute-start.5 = (bf16[2,128,256]{2,1,0:T(8,128)(2,1)S(1)}, bf16[2,128,256]{2,1,0:T(8,128)(2,1)S(1)}, u32[]{:S(2)}, u32[]{:S(2)}) collective-permute-start(bf16[2,128,256]{2,1,0:T(8,128)(2,1)S(1)} %get-tuple-element.17.streams_ref), channel_id=1, source_target_pairs={{0,16},{16,32},{32,48},{48,64},{64,80},{80,96},{96,112},{112,0},{1... | collective-permute-start | bytes 393224 | tf_op jit(solution)/shard_map/ppermute | solution.py:366
  64.1 0.0 copy-done.1
  64.1 0.0 copy-done.5
  64.1 0.7 shard_map.76
  64.8 0.0 copy-done.2
  64.8 0.5 shard_map.77.local_ref
  65.4 3.8 %collective-permute-done.5.arrived_ref = bf16[2,128,256]{2,1,0:T(8,128)(2,1)S(1)} collective-permute-done((bf16[2,128,256]{2,1,0:T(8,128)(2,1)S(1)}, bf16[2,128,256]{2,1,0:T(8,128)(2,1)S(1)}, u32[]{:S(2)}, u32[]{:S(2)}) %collective-permute-start.5) | collective-permute-done | bytes 131104 | tf_op jit(solution)/shard_map/ppermute | solution.py:366
  69.2 0.8 all-to-all-done.1.states_ref
  70.0 1.3 %shard_map.78 = bf16[4,64,128]{2,1,0:T(8,128)(2,1)S(1)} custom-call(bf16[2,128,256]{2,1,0:T(8,128)(2,1)S(1)} %get-tuple-element.17.streams_ref, f32[128,256]{1,0:T(8,128)S(1)} %shard_map.77.local_ref, bf16[2,128,256]{2,1,0:T(8,128)(2,1)S(1)} %collective-permute-done.5.arrived_ref, f32[8,32,128]{2,1,0:T(8,128)S(1)} %all-to-all-done.1.states_ref, ...), custom_call_target="tpu_custom_call" | custom-call | flops 100000000 | bytes 500000 | tf_op jit(solution)/shard_map/pallas_call | solution.py:80
  71.3 8.1 %all_to_all.15.packed_ref = bf16[4,64,128]{2,1,0:T(8,128)(2,1)S(1)} all-to-all(bf16[4,64,128]{2,1,0:T(8,128)(2,1)S(1)} %shard_map.78), channel_id=1, replica_groups={{0,128,256,384},{16,144,272,400},{32,160,288,416},{48,176,304,432},{64,..., dimensions={0} | all-to-all | bytes 131072 | tf_op jit(solution)/shard_map/all_to_all | solution.py:382
  79.4 0.7 shard_map.79
  (7 shorter events, 0.0 us)
Async XLA Ops:
  0.0 48.7 %copy-start = (bf16[128,4096]{1,0:T(8,128)(2,1)S(1)}, bf16[128,4096]{1,0:T(8,128)(2,1)}, u32[]{:S(2)}) copy-start(bf16[128,4096]{1,0:T(8,128)(2,1)} %t0.1) | copy-start | bytes 3145732
  0.0 18.2 %collective-permute-start.1 = (bf16[128,4096]{1,0:T(8,128)(2,1)}, bf16[128,4096]{1,0:T(8,128)(2,1)S(1)}, u32[]{:S(2)}, u32[]{:S(2)}) collective-permute-start(bf16[128,4096]{1,0:T(8,128)(2,1)} %t0.1), channel_id=1, source_target_pairs={{0,128},{1,385},{2,130},{3,387},{4,132},{5,389},{6,134},{7,391},{8... | collective-permute-start | bytes 3145736 | tf_op jit(solution)/shard_map/ppermute | solution.py:310
  3.5 0.9 %copy-start.3 = (bf16[3,128,256]{2,1,0:T(8,128)(2,1)S(1)}, bf16[3,128,256]{2,1,0:T(8,128)(2,1)}, u32[]{:S(2)}) copy-start(bf16[3,128,256]{2,1,0:T(8,128)(2,1)} %w_ref.1) | copy-start | bytes 589828
  4.5 44.3 %copy-start.4 = (f32[256,16]{0,1:T(8,128)S(1)}, f32[256,16]{0,1:T(8,128)}, u32[]{:S(2)}) copy-start(f32[256,16]{0,1:T(8,128)} %param.9) | copy-start | bytes 49156
  5.6 32.8 %all-to-all-start = ((bf16[16,192,128]{2,1,0:T(8,128)(2,1)}), bf16[16,192,128]{2,1,0:T(8,128)(2,1)S(1)}, u32[]{:S(2)}, u32[]{:S(2)}) async-start(bf16[16,192,128]{2,1,0:T(8,128)(2,1)} %shard_map.73), calls=%async_computation | async-start | bytes 1572864 | tf_op jit(solution)/shard_map/all_to_all | solution.py:318
  19.1 25.8 %collective-permute-start.3 = (bf16[128,2048]{1,0:T(8,128)(2,1)}, bf16[128,2048]{1,0:T(8,128)(2,1)S(1)}, u32[]{:S(2)}, u32[]{:S(2)}) collective-permute-start(bf16[128,2048]{1,0:T(8,128)(2,1)} %constant_dynamic-slice_fusion), channel_id=1, source_target_pairs={{0,128},{1,385},{2,130},{3,387},{4,132},{5,389},{6,134},{7,391},{8... | collective-permute-start | bytes 1572872 | tf_op jit(solution)/shard_map/ppermute | solution.py:324
  22.9 25.8 %collective-permute-start.2 = (bf16[128,4096]{1,0:T(8,128)(2,1)S(1)}, bf16[128,4096]{1,0:T(8,128)(2,1)}, u32[]{:S(2)}, u32[]{:S(2)}) collective-permute-start(bf16[128,4096]{1,0:T(8,128)(2,1)S(1)} %collective-permute-done.1.t1), channel_id=1, source_target_pairs={{0,1},{1,0},{2,3},{3,2},{4,5},{5,4},{6,7},{7,6},{8,9},{9,8},{10,11... | collective-permute-start | bytes 3145736 | tf_op jit(solution)/shard_map/ppermute | solution.py:323
  38.4 16.0 %collective-permute-start = (bf16[16,192,128]{2,1,0:T(8,128)(2,1)S(1)}, bf16[16,192,128]{2,1,0:T(8,128)(2,1)S(1)}, u32[]{:S(2)}, u32[]{:S(2)}) collective-permute-start(bf16[16,192,128]{2,1,0:T(8,128)(2,1)S(1)} %all-to-all-done.blocks_ref), channel_id=1, source_target_pairs={{0,16},{1,113},{2,18},{3,115},{4,20},{5,117},{6,22},{7,119},{8,24}... | collective-permute-start | bytes 2359304 | tf_op jit(solution)/shard_map/ppermute | solution.py:322
  44.9 3.8 %collective-permute-start.4 = (bf16[128,2048]{1,0:T(8,128)(2,1)S(1)}, bf16[128,2048]{1,0:T(8,128)(2,1)S(1)}, u32[]{:S(2)}, u32[]{:S(2)}) collective-permute-start(bf16[128,2048]{1,0:T(8,128)(2,1)S(1)} %collective-permute-done.3.t3), channel_id=1, source_target_pairs={{0,1},{1,0},{2,3},{3,2},{4,5},{5,4},{6,7},{7,6},{8,9},{9,8},{10,11... | collective-permute-start | bytes 1572872 | tf_op jit(solution)/shard_map/ppermute | solution.py:325
  54.4 9.7 %copy-start.1 = (f32[256,256]{1,0:T(8,128)S(1)}, f32[256,256]{1,0:T(8,128)}, u32[]{:S(2)}) copy-start(f32[256,256]{1,0:T(8,128)} %constant.26.clone.fwd_ref) | copy-start | bytes 786436
  54.4 9.7 %copy-start.5 = (bf16[256,128]{1,0:T(8,128)(2,1)S(1)}, bf16[256,128]{1,0:T(8,128)(2,1)}, u32[]{:S(2)}) copy-start(bf16[256,128]{1,0:T(8,128)(2,1)} %taps_ref.1) | copy-start | bytes 196612
  54.4 9.7 %copy-start.6 = (f32[256,16]{0,1:T(8,128)S(1)}, f32[256,16]{0,1:T(8,128)}, u32[]{:S(2)}) copy-start(f32[256,16]{0,1:T(8,128)} %param.10) | copy-start | bytes 49156
  54.4 10.4 %copy-start.2 = (f32[256,256]{1,0:T(8,128)S(1)}, f32[256,256]{1,0:T(8,128)}, u32[]{:S(2)}) copy-start(f32[256,256]{1,0:T(8,128)} %constant.27.clone.inv_ref) | copy-start | bytes 786436
  56.1 13.8 %all-to-all-start.1 = ((f32[8,32,128]{2,1,0:T(8,128)}), f32[8,32,128]{2,1,0:T(8,128)S(1)}, u32[]{:S(2)}, u32[]{:S(2)}) async-start(f32[8,32,128]{2,1,0:T(8,128)} %get-tuple-element.20), calls=%async_computation.1 | async-start | bytes 262144 | tf_op jit(solution)/shard_map/all_to_all | solution.py:364
  60.2 9.0 %collective-permute-start.5 = (bf16[2,128,256]{2,1,0:T(8,128)(2,1)S(1)}, bf16[2,128,256]{2,1,0:T(8,128)(2,1)S(1)}, u32[]{:S(2)}, u32[]{:S(2)}) collective-permute-start(bf16[2,128,256]{2,1,0:T(8,128)(2,1)S(1)} %get-tuple-element.17.streams_ref), channel_id=1, source_target_pairs={{0,16},{16,32},{32,48},{48,64},{64,80},{80,96},{96,112},{112,0},{1... | collective-permute-start | bytes 393224 | tf_op jit(solution)/shard_map/ppermute | solution.py:366

commit v7 on v6

--- a/solution.py
+++ b/solution.py
@@ -88,7 +88,7 @@
     )(*args)
 
 
-def spread_weights(w_ref, out_ref, block_ref, sems):
+def spread_weights(w_ref, out_ref):
     low = lower_lanes((ROWS, LANES))
     low_half = lower_lanes((HALF, LANES))
     for x in range(NX):
@@ -101,15 +101,10 @@
             both = jnp.where(low, swap_halves(a), v)
             packed = jnp.where(low_half, swap_halves(o[:HALF]), o[HALF:])
         both, packed = both.astype(bf16), packed.astype(bf16)
-        block_ref[x, :ROWS] = both
-        block_ref[x, ROWS:] = packed
         for z in range(NZ // 2):
             at = x * (NZ // 2) + z
-            pltpu.make_async_copy(block_ref.at[x], out_ref.at[at], sems.at[at]).start()
-    for x in range(NX):
-        for z in range(NZ // 2):
-            at = x * (NZ // 2) + z
-            pltpu.make_async_copy(block_ref.at[x], out_ref.at[at], sems.at[at]).wait()
+            out_ref[at, :ROWS] = both
+            out_ref[at, ROWS:] = packed
 
 
 def own_channels(ref):
@@ -307,14 +302,8 @@
         (place(a, b, k), place(a + 1 - 2 * (k % NC), b, k)) for a in range(NX) for b in range(NZ) for k in range(wide)
     ]
     swap = [(k, k ^ 1) for k in range(wide)]
+    blocks = call(spread_weights, sds((BLOCKS, ROWS + HALF, LANES), bf16), projections)
     near = lax.ppermute(tokens, ("ctx", "ch"), outward)
-    blocks = call(
-        spread_weights,
-        sds((BLOCKS, ROWS + HALF, LANES), bf16),
-        projections,
-        scratch=[pltpu.VMEM((NX, ROWS + HALF, LANES), bf16), pltpu.SemaphoreType.DMA((BLOCKS,))],
-        out_specs=ANY,
-    )
     blocks = lax.all_to_all(blocks, "ctx", 0, 0, tiled=True, axis_index_groups=parity_groups)
     across = [
         (place(a, b, k), place(a, (b + 1 - 2 * (k % NC)) % NZ, k)) for a in range(NX) for b in range(NZ) for k in range(wide)

time: 80.6 us -> 80.5 us (level)
  transfers between devices with their start and end apart: 8 -> 8, of which waited for: 5 -> 6; matrix products, arithmetic and copies ran while one was open for 1% -> 1% of each run, Pallas kernels for 6% -> 6%
where the time goes in v7:
time: 80.5 us; the launch traced here: 80 us
  starting transfers between devices  38 us (47%)
  waiting for transfers between devices  23.5 us (29%)
  Pallas kernels  8.4 us (10%)
  blocking collectives  8.12 us (10%)
  local copies, waits for them, and re-layouts  1.77 us (2%)
    all_to_all x1, waiting for transfers between devices, per_device(): lax.all_to_all(blocks, 'ctx', 0, 0, tiled=True, axis_index_groups=parity_...  13.6 us
    all_to_all x1, starting transfers between devices, per_device(): lax.all_to_all(blocks, 'ctx', 0, 0, tiled=True, axis_index_groups=parity_...  12.6 us
    pallas_call x7, Pallas kernels, call(): pl.pallas_call(body, out_shape=outs, in_specs=[ANY] * far + [VMEM] * (len...  8.4 us
    all_to_all x1, blocking collectives, per_device(): lax.all_to_all(packed, 'ctx', 0, 0, tiled=True, axis_index_groups=x_groups)  8.12 us
    ppermute x1, starting transfers between devices, per_device(): rest_blocks = lax.ppermute(blocks, ('ctx', 'ch'), across)  6.47 us
    all_to_all x1, starting transfers between devices, per_device(): lax.all_to_all(states, 'ctx', 0, 0, tiled=True, axis_index_groups=z_groups)  4.03 us
    ppermute x1, starting transfers between devices, per_device(): arrived = lax.ppermute(streams, 'ctx', onward)  3.92 us
    ppermute x1, waiting for transfers between devices, per_device(): arrived = lax.ppermute(streams, 'ctx', onward)  3.78 us
  transfers between devices with their start and end apart: 8, of which 6 were waited for; matrix products, arithmetic and copies ran while one was open for 1% of the time, Pallas kernels for 6%

profile of v7, /device:TPU:40, one launch (start us, length us, event | category | flops | bytes accessed | tf_op | source)
XLA Modules:
  0.0 80.0 jit_solution(4615162612675147398)
XLA Ops:
  0.0 3.5 %collective-permute-start.1 = (bf16[128,4096]{1,0:T(8,128)(2,1)}, bf16[128,4096]{1,0:T(8,128)(2,1)S(1)}, u32[]{:S(2)}, u32[]{:S(2)}) collective-permute-start(bf16[128,4096]{1,0:T(8,128)(2,1)} %t0.1), channel_id=1, source_target_pairs={{0,128},{1,385},{2,130},{3,387},{4,132},{5,389},{6,134},{7,391},{8... | collective-permute-start | bytes 3145736 | tf_op jit(solution)/shard_map/ppermute | solution.py:306
  3.5 0.0 copy-start.3
  3.5 0.9 %copy-done.3 = bf16[3,128,256]{2,1,0:T(8,128)(2,1)S(1)} copy-done((bf16[3,128,256]{2,1,0:T(8,128)(2,1)S(1)}, bf16[3,128,256]{2,1,0:T(8,128)(2,1)}, u32[]{:S(2)}) %copy-start.3) | copy-done | bytes 196632
  4.5 1.0 %shard_map.73 = bf16[16,192,128]{2,1,0:T(8,128)(2,1)} custom-call(bf16[3,128,256]{2,1,0:T(8,128)(2,1)S(1)} %copy-done.3), custom_call_target="tpu_custom_call" | custom-call | flops 100000000 | bytes 500000 | tf_op jit(solution)/shard_map/pallas_call | solution.py:80
  5.5 12.6 %all-to-all-start = ((bf16[16,192,128]{2,1,0:T(8,128)(2,1)}), bf16[16,192,128]{2,1,0:T(8,128)(2,1)S(1)}, u32[]{:S(2)}, u32[]{:S(2)}) async-start(bf16[16,192,128]{2,1,0:T(8,128)(2,1)} %shard_map.73), calls=%async_computation | async-start | bytes 1572864 | tf_op jit(solution)/shard_map/all_to_all | solution.py:307
  18.1 0.1 collective-permute-done.1.t1
  18.2 0.8 %constant_dynamic-slice_fusion = bf16[128,2048]{1,0:T(8,128)(2,1)} fusion(bf16[128,4096]{1,0:T(8,128)(2,1)S(1)} %collective-permute-done.1.t1, s32[]{:T(128)S(6)} %select_n.11), kind=kLoop, calls=%fused_computation | loop fusion | bytes 1048580 | tf_op jit(solution)/shard_map/dynamic_slice | solution.py:313
  19.1 3.7 %collective-permute-start.3 = (bf16[128,2048]{1,0:T(8,128)(2,1)}, bf16[128,2048]{1,0:T(8,128)(2,1)S(1)}, u32[]{:S(2)}, u32[]{:S(2)}) collective-permute-start(bf16[128,2048]{1,0:T(8,128)(2,1)} %constant_dynamic-slice_fusion), channel_id=1, source_target_pairs={{0,128},{1,385},{2,130},{3,387},{4,132},{5,389},{6,134},{7,391},{8... | collective-permute-start | bytes 1572872 | tf_op jit(solution)/shard_map/ppermute | solution.py:313
  22.8 1.9 %collective-permute-start.2 = (bf16[128,4096]{1,0:T(8,128)(2,1)S(1)}, bf16[128,4096]{1,0:T(8,128)(2,1)}, u32[]{:S(2)}, u32[]{:S(2)}) collective-permute-start(bf16[128,4096]{1,0:T(8,128)(2,1)S(1)} %collective-permute-done.1.t1), channel_id=1, source_target_pairs={{0,1},{1,0},{2,3},{3,2},{4,5},{5,4},{6,7},{7,6},{8,9},{9,8},{10,11... | collective-permute-start | bytes 3145736 | tf_op jit(solution)/shard_map/ppermute | solution.py:312
  24.7 13.6 %all-to-all-done.blocks_ref = bf16[16,192,128]{2,1,0:T(8,128)(2,1)S(1)} async-done(((bf16[16,192,128]{2,1,0:T(8,128)(2,1)}), bf16[16,192,128]{2,1,0:T(8,128)(2,1)S(1)}, u32[]{:S(2)}, u32[]{:S(2)}) %all-to-all-start) | async-done | bytes 786464 | tf_op jit(solution)/shard_map/all_to_all | solution.py:307
  38.3 6.5 %collective-permute-start = (bf16[16,192,128]{2,1,0:T(8,128)(2,1)S(1)}, bf16[16,192,128]{2,1,0:T(8,128)(2,1)S(1)}, u32[]{:S(2)}, u32[]{:S(2)}) collective-permute-start(bf16[16,192,128]{2,1,0:T(8,128)(2,1)S(1)} %all-to-all-done.blocks_ref), channel_id=1, source_target_pairs={{0,16},{1,113},{2,18},{3,115},{4,20},{5,117},{6,22},{7,119},{8,24}... | collective-permute-start | bytes 2359304 | tf_op jit(solution)/shard_map/ppermute | solution.py:311
  44.8 0.0 collective-permute-done.3.t3
  44.8 1.9 %collective-permute-start.4 = (bf16[128,2048]{1,0:T(8,128)(2,1)S(1)}, bf16[128,2048]{1,0:T(8,128)(2,1)S(1)}, u32[]{:S(2)}, u32[]{:S(2)}) collective-permute-start(bf16[128,2048]{1,0:T(8,128)(2,1)S(1)} %collective-permute-done.3.t3), channel_id=1, source_target_pairs={{0,1},{1,0},{2,3},{3,2},{4,5},{5,4},{6,7},{7,6},{8,9},{9,8},{10,11... | collective-permute-start | bytes 1572872 | tf_op jit(solution)/shard_map/ppermute | solution.py:314
  46.7 1.9 %collective-permute-done.4.t4 = bf16[128,2048]{1,0:T(8,128)(2,1)S(1)} collective-permute-done((bf16[128,2048]{1,0:T(8,128)(2,1)S(1)}, bf16[128,2048]{1,0:T(8,128)(2,1)S(1)}, u32[]{:S(2)}, u32[]{:S(2)}) %collective-permute-start.4) | collective-permute-done | bytes 524320 | tf_op jit(solution)/shard_map/ppermute | solution.py:314
  48.6 0.0 collective-permute-done.2.t2
  48.6 0.0 copy-done
  48.6 0.0 copy-done.4
  48.6 2.4 %shard_map.74 = (f32[512,256]{1,0:T(8,128)S(1)}, bf16[512,2048]{1,0:T(8,128)(2,1)S(1)}, f32[16,128,128]{2,1,0:T(8,128)S(1)}) custom-call(bf16[128,4096]{1,0:T(8,128)(2,1)S(1)} %copy-done, bf16[128,4096]{1,0:T(8,128)(2,1)S(1)} %collective-permute-done.1.t1, bf16[128,4096]{1,0:T(8,128)(2,1)} %collective-permute-done.2.t2, ...), custom_call_target="tpu_custom_call" | custom-call | flops 100000000 | bytes 500000 | tf_op jit(solution)/shard_map/pallas_call | solution.py:80
  51.0 3.3 %collective-permute-done.blocks_ref = bf16[16,192,128]{2,1,0:T(8,128)(2,1)S(1)} collective-permute-done((bf16[16,192,128]{2,1,0:T(8,128)(2,1)S(1)}, bf16[16,192,128]{2,1,0:T(8,128)(2,1)S(1)}, u32[]{:S(2)}, u32[]{:S(2)}) %collective-permute-start) | collective-permute-done | bytes 786464 | tf_op jit(solution)/shard_map/ppermute | solution.py:311
  54.3 1.7 %shard_map.75 = (f32[128,256]{1,0:T(8,128)S(1)}, bf16[2,128,256]{2,1,0:T(8,128)(2,1)S(1)}, f32[8,32,128]{2,1,0:T(8,128)}) custom-call(bf16[16,192,128]{2,1,0:T(8,128)(2,1)S(1)} %collective-permute-done.blocks_ref, bf16[512,2048]{1,0:T(8,128)(2,1)S(1)} %get-tuple-element.14.rest_ref, f32[512,256]{1,0:T(8,128)S(1)} %get-tuple-element.15.product_ref, ...), custom_call_target="tpu_custom_call" | custom-call | flops 100000000 | bytes 500000 | tf_op jit(solution)/shard_map/pallas_call | solution.py:80
  56.0 4.0 %all-to-all-start.1 = ((f32[8,32,128]{2,1,0:T(8,128)}), f32[8,32,128]{2,1,0:T(8,128)S(1)}, u32[]{:S(2)}, u32[]{:S(2)}) async-start(f32[8,32,128]{2,1,0:T(8,128)} %get-tuple-element.20), calls=%async_computation.1 | async-start | bytes 262144 | tf_op jit(solution)/shard_map/all_to_all | solution.py:353
  60.0 3.9 %collective-permute-start.5 = (bf16[2,128,256]{2,1,0:T(8,128)(2,1)S(1)}, bf16[2,128,256]{2,1,0:T(8,128)(2,1)S(1)}, u32[]{:S(2)}, u32[]{:S(2)}) collective-permute-start(bf16[2,128,256]{2,1,0:T(8,128)(2,1)S(1)} %get-tuple-element.17.streams_ref), channel_id=1, source_target_pairs={{0,16},{16,32},{32,48},{48,64},{64,80},{80,96},{96,112},{112,0},{1... | collective-permute-start | bytes 393224 | tf_op jit(solution)/shard_map/ppermute | solution.py:355
  64.0 0.0 copy-done.1
  64.0 0.0 copy-done.5
  64.0 0.0 copy-done.6
  64.0 0.7 shard_map.76
  64.7 0.5 shard_map.77.local_ref
  65.2 3.8 %collective-permute-done.5.arrived_ref = bf16[2,128,256]{2,1,0:T(8,128)(2,1)S(1)} collective-permute-done((bf16[2,128,256]{2,1,0:T(8,128)(2,1)S(1)}, bf16[2,128,256]{2,1,0:T(8,128)(2,1)S(1)}, u32[]{:S(2)}, u32[]{:S(2)}) %collective-permute-start.5) | collective-permute-done | bytes 131104 | tf_op jit(solution)/shard_map/ppermute | solution.py:355
  69.0 0.8 all-to-all-done.1.states_ref
  69.8 1.3 %shard_map.78 = bf16[4,64,128]{2,1,0:T(8,128)(2,1)S(1)} custom-call(bf16[2,128,256]{2,1,0:T(8,128)(2,1)S(1)} %get-tuple-element.17.streams_ref, f32[128,256]{1,0:T(8,128)S(1)} %shard_map.77.local_ref, bf16[2,128,256]{2,1,0:T(8,128)(2,1)S(1)} %collective-permute-done.5.arrived_ref, f32[8,32,128]{2,1,0:T(8,128)S(1)} %all-to-all-done.1.states_ref, ...), custom_call_target="tpu_custom_call" | custom-call | flops 100000000 | bytes 500000 | tf_op jit(solution)/shard_map/pallas_call | solution.py:80
  71.1 8.1 %all_to_all.15.packed_ref = bf16[4,64,128]{2,1,0:T(8,128)(2,1)S(1)} all-to-all(bf16[4,64,128]{2,1,0:T(8,128)(2,1)S(1)} %shard_map.78), channel_id=1, replica_groups={{0,128,256,384},{16,144,272,400},{32,160,288,416},{48,176,304,432},{64,..., dimensions={0} | all-to-all | bytes 131072 | tf_op jit(solution)/shard_map/all_to_all | solution.py:371
  79.3 0.7 shard_map.79
  (7 shorter events, 0.0 us)
Async XLA Ops:
  0.0 48.6 %copy-start = (bf16[128,4096]{1,0:T(8,128)(2,1)S(1)}, bf16[128,4096]{1,0:T(8,128)(2,1)}, u32[]{:S(2)}) copy-start(bf16[128,4096]{1,0:T(8,128)(2,1)} %t0.1) | copy-start | bytes 3145732
  0.0 18.2 %collective-permute-start.1 = (bf16[128,4096]{1,0:T(8,128)(2,1)}, bf16[128,4096]{1,0:T(8,128)(2,1)S(1)}, u32[]{:S(2)}, u32[]{:S(2)}) collective-permute-start(bf16[128,4096]{1,0:T(8,128)(2,1)} %t0.1), channel_id=1, source_target_pairs={{0,128},{1,385},{2,130},{3,387},{4,132},{5,389},{6,134},{7,391},{8... | collective-permute-start | bytes 3145736 | tf_op jit(solution)/shard_map/ppermute | solution.py:306
  3.5 0.9 %copy-start.3 = (bf16[3,128,256]{2,1,0:T(8,128)(2,1)S(1)}, bf16[3,128,256]{2,1,0:T(8,128)(2,1)}, u32[]{:S(2)}) copy-start(bf16[3,128,256]{2,1,0:T(8,128)(2,1)} %w_ref.1) | copy-start | bytes 589828
  4.5 44.1 %copy-start.4 = (f32[256,16]{0,1:T(8,128)S(1)}, f32[256,16]{0,1:T(8,128)}, u32[]{:S(2)}) copy-start(f32[256,16]{0,1:T(8,128)} %param.9) | copy-start | bytes 49156
  5.5 32.8 %all-to-all-start = ((bf16[16,192,128]{2,1,0:T(8,128)(2,1)}), bf16[16,192,128]{2,1,0:T(8,128)(2,1)S(1)}, u32[]{:S(2)}, u32[]{:S(2)}) async-start(bf16[16,192,128]{2,1,0:T(8,128)(2,1)} %shard_map.73), calls=%async_computation | async-start | bytes 1572864 | tf_op jit(solution)/shard_map/all_to_all | solution.py:307
  19.1 25.7 %collective-permute-start.3 = (bf16[128,2048]{1,0:T(8,128)(2,1)}, bf16[128,2048]{1,0:T(8,128)(2,1)S(1)}, u32[]{:S(2)}, u32[]{:S(2)}) collective-permute-start(bf16[128,2048]{1,0:T(8,128)(2,1)} %constant_dynamic-slice_fusion), channel_id=1, source_target_pairs={{0,128},{1,385},{2,130},{3,387},{4,132},{5,389},{6,134},{7,391},{8... | collective-permute-start | bytes 1572872 | tf_op jit(solution)/shard_map/ppermute | solution.py:313
  22.8 25.8 %collective-permute-start.2 = (bf16[128,4096]{1,0:T(8,128)(2,1)S(1)}, bf16[128,4096]{1,0:T(8,128)(2,1)}, u32[]{:S(2)}, u32[]{:S(2)}) collective-permute-start(bf16[128,4096]{1,0:T(8,128)(2,1)S(1)} %collective-permute-done.1.t1), channel_id=1, source_target_pairs={{0,1},{1,0},{2,3},{3,2},{4,5},{5,4},{6,7},{7,6},{8,9},{9,8},{10,11... | collective-permute-start | bytes 3145736 | tf_op jit(solution)/shard_map/ppermute | solution.py:312
  38.3 16.0 %collective-permute-start = (bf16[16,192,128]{2,1,0:T(8,128)(2,1)S(1)}, bf16[16,192,128]{2,1,0:T(8,128)(2,1)S(1)}, u32[]{:S(2)}, u32[]{:S(2)}) collective-permute-start(bf16[16,192,128]{2,1,0:T(8,128)(2,1)S(1)} %all-to-all-done.blocks_ref), channel_id=1, source_target_pairs={{0,16},{1,113},{2,18},{3,115},{4,20},{5,117},{6,22},{7,119},{8,24}... | collective-permute-start | bytes 2359304 | tf_op jit(solution)/shard_map/ppermute | solution.py:311
  44.8 3.8 %collective-permute-start.4 = (bf16[128,2048]{1,0:T(8,128)(2,1)S(1)}, bf16[128,2048]{1,0:T(8,128)(2,1)S(1)}, u32[]{:S(2)}, u32[]{:S(2)}) collective-permute-start(bf16[128,2048]{1,0:T(8,128)(2,1)S(1)} %collective-permute-done.3.t3), channel_id=1, source_target_pairs={{0,1},{1,0},{2,3},{3,2},{4,5},{5,4},{6,7},{7,6},{8,9},{9,8},{10,11... | collective-permute-start | bytes 1572872 | tf_op jit(solution)/shard_map/ppermute | solution.py:314
  54.3 9.7 %copy-start.1 = (f32[256,256]{1,0:T(8,128)S(1)}, f32[256,256]{1,0:T(8,128)}, u32[]{:S(2)}) copy-start(f32[256,256]{1,0:T(8,128)} %constant.26.clone.fwd_ref) | copy-start | bytes 786436
  54.3 9.7 %copy-start.5 = (bf16[256,128]{1,0:T(8,128)(2,1)S(1)}, bf16[256,128]{1,0:T(8,128)(2,1)}, u32[]{:S(2)}) copy-start(bf16[256,128]{1,0:T(8,128)(2,1)} %taps_ref.1) | copy-start | bytes 196612
  54.3 9.7 %copy-start.6 = (f32[256,16]{0,1:T(8,128)S(1)}, f32[256,16]{0,1:T(8,128)}, u32[]{:S(2)}) copy-start(f32[256,16]{0,1:T(8,128)} %param.10) | copy-start | bytes 49156
  54.3 10.4 %copy-start.2 = (f32[256,256]{1,0:T(8,128)S(1)}, f32[256,256]{1,0:T(8,128)}, u32[]{:S(2)}) copy-start(f32[256,256]{1,0:T(8,128)} %constant.27.clone.inv_ref) | copy-start | bytes 786436
  56.0 13.8 %all-to-all-start.1 = ((f32[8,32,128]{2,1,0:T(8,128)}), f32[8,32,128]{2,1,0:T(8,128)S(1)}, u32[]{:S(2)}, u32[]{:S(2)}) async-start(f32[8,32,128]{2,1,0:T(8,128)} %get-tuple-element.20), calls=%async_computation.1 | async-start | bytes 262144 | tf_op jit(solution)/shard_map/all_to_all | solution.py:353
  60.0 9.0 %collective-permute-start.5 = (bf16[2,128,256]{2,1,0:T(8,128)(2,1)S(1)}, bf16[2,128,256]{2,1,0:T(8,128)(2,1)S(1)}, u32[]{:S(2)}, u32[]{:S(2)}) collective-permute-start(bf16[2,128,256]{2,1,0:T(8,128)(2,1)S(1)} %get-tuple-element.17.streams_ref), channel_id=1, source_target_pairs={{0,16},{16,32},{32,48},{48,64},{64,80},{80,96},{96,112},{112,0},{1... | collective-permute-start | bytes 393224 | tf_op jit(solution)/shard_map/ppermute | solution.py:355

commit v8 on v6

--- a/solution.py
+++ b/solution.py
@@ -146,15 +146,14 @@
 BLOCKS = NX * NZ // 2
 
 
-def widen(blocks_ref, wide_ref):
+def widen_gates(blocks_ref, first, wide_ref, lanes):
     low_half = lower_lanes((HALF, LANES))
     for block in range(BLOCKS):
         top, bottom = slice(ROWS * block, ROWS * block + HALF), slice(ROWS * block + HALF, ROWS * (block + 1))
-        wide_ref[ROWS * block : ROWS * (block + 1), :LANES] = blocks_ref[block, :ROWS]
-        packed = blocks_ref[block, ROWS:].astype(f32)
+        packed = blocks_ref[block, first:].astype(f32)
         turned = swap_halves(packed)
-        wide_ref[top, LANES:] = jnp.where(low_half, packed, turned).astype(bf16)
-        wide_ref[bottom, LANES:] = jnp.where(low_half, turned, packed).astype(bf16)
+        wide_ref[top, lanes] = jnp.where(low_half, packed, turned).astype(bf16)
+        wide_ref[bottom, lanes] = jnp.where(low_half, turned, packed).astype(bf16)
 
 
 def project_first(t0, t1, t2, t3, t4, blocks_ref, a_ref, product_ref, rest_ref, into_ref, tokens_ref, wide_ref, sems):
@@ -180,7 +179,9 @@
             second = pltpu.make_async_copy(t4.at[:, inner], target.at[rows_of(across), to], sems.at[3, side])
             pl.when(mine)(first.start)
             pl.when(jnp.logical_not(mine))(second.start)
-    widen(blocks_ref, wide_ref)
+    for block in range(BLOCKS):
+        wide_ref[ROWS * block : ROWS * (block + 1), :LANES] = blocks_ref[block, :ROWS]
+    widen_gates(blocks_ref, ROWS, wide_ref, slice(LANES, 2 * LANES))
     back = ROWS - 1.0 - lax.broadcasted_iota(jnp.int32, (ROWS, LANES), 0).astype(f32)
     rates = own_channels(a_ref)
     for m in range(MODES):
@@ -196,25 +197,30 @@
     wait(rest_ref, 1)
 
 
-def project_rest(blocks_ref, rest_ref, product_ref, into_ref, signal_ref, streams_ref, state_ref, wide_ref, total_ref):
-    widen(blocks_ref, wide_ref)
-    total_ref[...] = product_ref[...] + jnp.dot(rest_ref[...], wide_ref[...], preferred_element_type=f32)
+def project_signal(blocks_ref, rest_ref, product_ref, into_ref, signal_ref, state_ref, total_ref):
+    weights = blocks_ref[...].reshape(BLOCKS * ROWS, LANES)
+    total_ref[...] = product_ref[:, :LANES] + jnp.dot(rest_ref[...], weights, preferred_element_type=f32)
     low = lower_lanes((ROWS, LANES))
     for pair in range(NX // 2):
-        lanes = slice(LANES * pair, LANES * (pair + 1))
         chunks = [slice(ROWS * k, ROWS * (k + 1)) for k in (2 * pair, 2 * pair + 1)]
-        a, b = (total_ref[k, :LANES].astype(bf16).astype(f32) for k in chunks)
-        turned_a, turned_b = swap_halves(a), swap_halves(b)
-        gate_in, values = jnp.where(low, a, turned_b), jnp.where(low, turned_a, b)
-        gate_out = jnp.where(low, total_ref[chunks[0], LANES:], total_ref[chunks[1], LANES:])
-        signal = gate_in * values
-        signal_ref[:, lanes] = signal
-        for k, value in enumerate((signal, gate_out)):
-            streams_ref[k, :, lanes] = value.astype(bf16)
+        a, b = (total_ref[k, :].astype(bf16).astype(f32) for k in chunks)
+        signal = jnp.where(low, a, swap_halves(b)) * jnp.where(low, swap_halves(a), b)
+        signal_ref[:, LANES * pair : LANES * (pair + 1)] = signal
         for m in range(MODES):
             state = jnp.sum(signal * into_ref[m], axis=0, keepdims=True)
             for z in range(NZ):
                 state_ref[z, pair * MODES + m : pair * MODES + m + 1, :] = state
+
+
+def project_gates(blocks_ref, rest_ref, product_ref, signal_ref, streams_ref, wide_ref, total_ref):
+    widen_gates(blocks_ref, 0, wide_ref, slice(0, LANES))
+    total_ref[...] = product_ref[:, LANES:] + jnp.dot(rest_ref[...], wide_ref[...], preferred_element_type=f32)
+    streams_ref[0] = signal_ref[...].astype(bf16)
+    low = lower_lanes((ROWS, LANES))
+    for pair in range(NX // 2):
+        chunks = [slice(ROWS * k, ROWS * (k + 1)) for k in (2 * pair, 2 * pair + 1)]
+        gate = jnp.where(low, total_ref[chunks[0], :], total_ref[chunks[1], :])
+        streams_ref[1, :, LANES * pair : LANES * (pair + 1)] = gate.astype(bf16)
 
 
 def filter_inside(signal, fwd_ref, inv_ref, long_ref):
@@ -319,7 +325,8 @@
     across = [
         (place(a, b, k), place(a, (b + 1 - 2 * (k % NC)) % NZ, k)) for a in range(NX) for b in range(NZ) for k in range(wide)
     ]
-    rest_blocks = lax.ppermute(blocks, ("ctx", "ch"), across)
+    rest_pairs = lax.ppermute(blocks[:, :ROWS], ("ctx", "ch"), across)
+    rest_gates = lax.ppermute(blocks[:, ROWS:], ("ctx", "ch"), across)
     far = lax.ppermute(near, "ch", swap)
     half = lax.ppermute(lax.dynamic_slice_in_dim(near, core * width, width, 1), ("ctx", "ch"), outward)
     other = lax.ppermute(half, "ch", swap)
@@ -349,20 +356,27 @@
         ],
         far=5,
     )
-    signal, streams, states = call(
-        project_rest,
-        (sds((ROWS, 2 * LANES), f32), sds((2, ROWS, 2 * LANES), bf16), sds((NZ, 2 * MODES, LANES), f32)),
-        rest_blocks,
+    total = pltpu.VMEM((NX * rows, LANES), f32)
+    signal, states = call(
+        project_signal,
+        (sds((ROWS, 2 * LANES), f32), sds((NZ, 2 * MODES, LANES), f32)),
+        rest_pairs,
         rest,
         product,
         into,
-        scratch=[
-            pltpu.VMEM((half_depth, 2 * LANES), bf16),
-            pltpu.VMEM((NX * rows, 2 * LANES), f32),
-        ],
+        scratch=[total],
     )
     states = lax.all_to_all(states, "ctx", 0, 0, tiled=True, axis_index_groups=z_groups)
     onward = [(a * NZ + b, a * NZ + (b + 1) % NZ) for a in range(NX) for b in range(NZ)]
+    streams = call(
+        project_gates,
+        sds((2, ROWS, 2 * LANES), bf16),
+        rest_gates,
+        rest,
+        product,
+        signal,
+        scratch=[pltpu.VMEM((half_depth, LANES), bf16), total],
+    )
     arrived = lax.ppermute(streams, "ctx", onward)
     local = call(filter_chunks, sds((ROWS, 2 * LANES), f32), signal, forward, inverse, long_spectrum)
     packed = call(

time: 80.6 us -> 87.2 us (1.082)
  waiting for transfers between devices: 23.4 us -> 14.9 us
  local copies, waits for them, and re-layouts: 1.77 us -> 8.96 us
  starting transfers between devices: 38.2 us -> 44 us
  Pallas kernels: 8.5 us -> 10.2 us
    all_to_all x1, waiting for transfers between devices: 13.6 us -> 1.37 us  [per_device(): lax.all_to_all(blocks, 'ctx', 0, 0, tiled=True, axis_index_groups=parity_...]
    ppermute x1, waiting for transfers between devices: 0.01 us -> 11.1 us  [per_device(): lax.ppermute(lax.dynamic_slice_in_dim(near, core * width, width, 1), ('ct...]
    unnamed x14 -> x26, local copies, waits for them, and re-layouts: 0.94 us -> 8.16 us
    all_to_all x1, starting transfers between devices: 4.03 us -> 8.08 us  [per_device(): lax.all_to_all(states, 'ctx', 0, 0, tiled=True, axis_index_groups=z_groups)]
    ppermute x1 -> x2, waiting for transfers between devices: 3.28 us -> 0.61 us  [the longest x1 0.61 us: per_device(): rest_pairs = lax.ppermute(blocks[:, :ROWS], ('ctx', 'ch'), across)]
    ppermute x1, waiting for transfers between devices: 3.78 us -> 1.82 us  [per_device(): arrived = lax.ppermute(streams, 'ctx', onward)]
    ppermute x1 -> x2, starting transfers between devices: 6.47 us -> 8.39 us  [the longest x1 6.48 us: per_device(): rest_pairs = lax.ppermute(blocks[:, :ROWS], ('ctx', 'ch'), across)]
    ppermute x1, waiting for transfers between devices: 1.88 us -> 0.01 us  [per_device(): other = lax.ppermute(half, 'ch', swap)]
  transfers between devices with their start and end apart: 8 -> 9, of which waited for: 5 -> 4; matrix products, arithmetic and copies ran while one was open for 1% -> 1% of each run, Pallas kernels for 6% -> 9%
where the time goes in v8:
time: 87.2 us; the launch traced here: 86.3 us
  starting transfers between devices  44 us (50%)
  waiting for transfers between devices  14.9 us (17%)
  Pallas kernels  10.2 us (12%)
  local copies, waits for them, and re-layouts  8.96 us (10%)
  blocking collectives  7.99 us (9%)
    all_to_all x1, starting transfers between devices, per_device(): lax.all_to_all(blocks, 'ctx', 0, 0, tiled=True, axis_index_groups=parity_...  12.6 us
    ppermute x1, waiting for transfers between devices, per_device(): lax.ppermute(lax.dynamic_slice_in_dim(near, core * width, width, 1), ('ct...  11.1 us
    pallas_call x8, Pallas kernels, call(): pl.pallas_call(body, out_shape=outs, in_specs=[ANY] * far + [VMEM] * (len...  10.2 us
    unnamed x26, local copies, waits for them, and re-layouts  8.16 us
    all_to_all x1, starting transfers between devices, per_device(): lax.all_to_all(states, 'ctx', 0, 0, tiled=True, axis_index_groups=z_groups)  8.08 us
    all_to_all x1, blocking collectives, per_device(): lax.all_to_all(packed, 'ctx', 0, 0, tiled=True, axis_index_groups=x_groups)  7.99 us
    ppermute x1, starting transfers between devices, per_device(): rest_pairs = lax.ppermute(blocks[:, :ROWS], ('ctx', 'ch'), across)  6.48 us
    ppermute x1, starting transfers between devices, per_device(): arrived = lax.ppermute(streams, 'ctx', onward)  3.92 us
  transfers between devices with their start and end apart: 9, of which 4 were waited for; matrix products, arithmetic and copies ran while one was open for 1% of the time, Pallas kernels for 9%

profile of v8, /device:TPU:40, one launch (start us, length us, event | category | flops | bytes accessed | tf_op | source)
XLA Modules:
  0.0 86.3 jit_solution(9173498193578170543)
XLA Ops:
  0.0 3.4 %collective-permute-start.1 = (bf16[128,4096]{1,0:T(8,128)(2,1)}, bf16[128,4096]{1,0:T(8,128)(2,1)S(1)}, u32[]{:S(2)}, u32[]{:S(2)}) collective-permute-start(bf16[128,4096]{1,0:T(8,128)(2,1)} %t0.1), channel_id=1, source_target_pairs={{0,128},{1,385},{2,130},{3,387},{4,132},{5,389},{6,134},{7,391},{8... | collective-permute-start | bytes 3145736 | tf_op jit(solution)/shard_map/ppermute | solution.py:316
  3.4 0.9 %copy-done.9 = bf16[3,128,256]{2,1,0:T(8,128)(2,1)S(1)} copy-done((bf16[3,128,256]{2,1,0:T(8,128)(2,1)S(1)}, bf16[3,128,256]{2,1,0:T(8,128)(2,1)}, u32[]{:S(2)}) %copy-start.9) | copy-done | bytes 196632
  4.3 1.1 %shard_map.73 = bf16[16,192,128]{2,1,0:T(8,128)(2,1)} custom-call(bf16[3,128,256]{2,1,0:T(8,128)(2,1)S(1)} %copy-done.9), custom_call_target="tpu_custom_call" | custom-call | flops 100000000 | bytes 500000 | tf_op jit(solution)/shard_map/pallas_call | solution.py:80
  5.5 12.6 %all-to-all-start = ((bf16[16,192,128]{2,1,0:T(8,128)(2,1)}), bf16[16,192,128]{2,1,0:T(8,128)(2,1)S(1)}, u32[]{:S(2)}, u32[]{:S(2)}) async-start(bf16[16,192,128]{2,1,0:T(8,128)(2,1)} %shard_map.73), calls=%async_computation | async-start | bytes 1572864 | tf_op jit(solution)/shard_map/all_to_all | solution.py:324
  18.1 0.0 collective-permute-done.1.t1
  18.2 3.8 %collective-permute-start.3 = (bf16[128,2048]{1,0:T(8,128)(2,1)S(1)}, bf16[128,2048]{1,0:T(8,128)(2,1)S(1)}, u32[]{:S(2)}, u32[]{:S(2)}) collective-permute-start(bf16[128,2048]{1,0:T(8,128)(2,1)S(1)} %constant_dynamic-slice_fusion), channel_id=1, source_target_pairs={{0,128},{1,385},{2,130},{3,387},{4,132},{5,389},{6,134},{7,391},{8... | collective-permute-start | bytes 1572872 | tf_op jit(solution)/shard_map/ppermute | solution.py:331
  22.0 1.9 %collective-permute-start.2 = (bf16[128,4096]{1,0:T(8,128)(2,1)S(1)}, bf16[128,4096]{1,0:T(8,128)(2,1)S(1)}, u32[]{:S(2)}, u32[]{:S(2)}) collective-permute-start(bf16[128,4096]{1,0:T(8,128)(2,1)S(1)} %collective-permute-done.1.t1), channel_id=1, source_target_pairs={{0,1},{1,0},{2,3},{3,2},{4,5},{5,4},{6,7},{7,6},{8,9},{9,8},{10,11... | collective-permute-start | bytes 3145736 | tf_op jit(solution)/shard_map/ppermute | solution.py:330
  23.9 11.1 %collective-permute-done.3.t3 = bf16[128,2048]{1,0:T(8,128)(2,1)S(1)} collective-permute-done((bf16[128,2048]{1,0:T(8,128)(2,1)S(1)}, bf16[128,2048]{1,0:T(8,128)(2,1)S(1)}, u32[]{:S(2)}, u32[]{:S(2)}) %collective-permute-start.3) | collective-permute-done | bytes 524320 | tf_op jit(solution)/shard_map/ppermute | solution.py:331
  35.0 1.9 %collective-permute-start.4 = (bf16[128,2048]{1,0:T(8,128)(2,1)S(1)}, bf16[128,2048]{1,0:T(8,128)(2,1)}, u32[]{:S(2)}, u32[]{:S(2)}) collective-permute-start(bf16[128,2048]{1,0:T(8,128)(2,1)S(1)} %collective-permute-done.3.t3), channel_id=1, source_target_pairs={{0,1},{1,0},{2,3},{3,2},{4,5},{5,4},{6,7},{7,6},{8,9},{9,8},{10,11... | collective-permute-start | bytes 1572872 | tf_op jit(solution)/shard_map/ppermute | solution.py:332
  36.9 1.4 %all-to-all-done.blocks_ref = bf16[16,192,128]{2,1,0:T(8,128)(2,1)S(1)} async-done(((bf16[16,192,128]{2,1,0:T(8,128)(2,1)}), bf16[16,192,128]{2,1,0:T(8,128)(2,1)S(1)}, u32[]{:S(2)}, u32[]{:S(2)}) %all-to-all-start) | async-done | bytes 786464 | tf_op jit(solution)/shard_map/all_to_all | solution.py:324
  38.3 6.5 %collective-permute-start.5 = (bf16[16,128,128]{2,1,0:T(8,128)(2,1)S(1)}, bf16[16,128,128]{2,1,0:T(8,128)(2,1)S(1)}, u32[]{:S(2)}, u32[]{:S(2)}) collective-permute-start(bf16[16,128,128]{2,1,0:T(8,128)(2,1)S(1)} %slice.9), channel_id=1, source_target_pairs={{0,16},{1,113},{2,18},{3,115},{4,20},{5,117},{6,22},{7,119},{8,24}... | collective-permute-start | bytes 1572872 | tf_op jit(solution)/shard_map/ppermute | solution.py:328
  44.8 0.7 slice.8
  45.5 1.9 %collective-permute-start = (bf16[16,64,128]{2,1,0:T(8,128)(2,1)}, bf16[16,64,128]{2,1,0:T(8,128)(2,1)}, u32[]{:S(2)}, u32[]{:S(2)}) collective-permute-start(bf16[16,64,128]{2,1,0:T(8,128)(2,1)} %slice.8), channel_id=1, source_target_pairs={{0,16},{1,113},{2,18},{3,115},{4,20},{5,117},{6,22},{7,119},{8,24}... | collective-permute-start | bytes 786440 | tf_op jit(solution)/shard_map/ppermute | solution.py:329
  47.5 1.0 %copy-done.3 = bf16[128,4096]{1,0:T(8,128)(2,1)} copy-done((bf16[128,4096]{1,0:T(8,128)(2,1)}, bf16[128,4096]{1,0:T(8,128)(2,1)S(1)}, u32[]{:S(2)}) %copy-start.3) | copy-done | bytes 1048600
  48.5 1.2 %copy-done.1 = bf16[128,4096]{1,0:T(8,128)(2,1)S(1)} copy-done((bf16[128,4096]{1,0:T(8,128)(2,1)S(1)}, bf16[128,4096]{1,0:T(8,128)(2,1)}, u32[]{:S(2)}) %copy-start.1) | copy-done | bytes 1048600
  49.7 1.2 %copy-done.2 = bf16[128,4096]{1,0:T(8,128)(2,1)S(1)} copy-done((bf16[128,4096]{1,0:T(8,128)(2,1)S(1)}, bf16[128,4096]{1,0:T(8,128)(2,1)}, u32[]{:S(2)}) %copy-start.2) | copy-done | bytes 1048600
  50.9 1.2 %copy-done.4 = bf16[128,4096]{1,0:T(8,128)(2,1)S(1)} copy-done((bf16[128,4096]{1,0:T(8,128)(2,1)S(1)}, bf16[128,4096]{1,0:T(8,128)(2,1)}, u32[]{:S(2)}) %copy-start.4) | copy-done | bytes 1048600
  52.1 1.0 %copy-done.8 = bf16[128,2048]{1,0:T(8,128)(2,1)S(1)} copy-done((bf16[128,2048]{1,0:T(8,128)(2,1)S(1)}, bf16[128,2048]{1,0:T(8,128)(2,1)}, u32[]{:S(2)}) %copy-start.8) | copy-done | bytes 524312
  53.2 2.4 %shard_map.74 = (f32[512,256]{1,0:T(8,128)S(1)}, bf16[512,2048]{1,0:T(8,128)(2,1)S(1)}, f32[16,128,128]{2,1,0:T(8,128)S(1)}) custom-call(bf16[128,4096]{1,0:T(8,128)(2,1)S(1)} %copy-done.2, bf16[128,4096]{1,0:T(8,128)(2,1)S(1)} %copy-done.1, bf16[128,4096]{1,0:T(8,128)(2,1)S(1)} %copy-done.4, bf16[128,2048]{1,0:T(8,128)(2,1)S(1)} %copy-done.8, ...), custom_call_target="tpu_custom_call" | custom-call | flops 100000000 | bytes 500000 | tf_op jit(solution)/shard_map/pallas_call | solution.py:80
  55.6 0.6 collective-permute-done.5.blocks_ref
  56.2 1.6 %shard_map.75 = (f32[128,256]{1,0:T(8,128)S(1)}, f32[8,32,128]{2,1,0:T(8,128)}) custom-call(bf16[16,128,128]{2,1,0:T(8,128)(2,1)S(1)} %collective-permute-done.5.blocks_ref, bf16[512,2048]{1,0:T(8,128)(2,1)S(1)} %get-tuple-element.13.rest_ref, f32[512,256]{1,0:T(8,128)S(1)} %get-tuple-element.14.product_ref, f32[16,128,128]{2,1,0:T(8,128)S(1)} %get-tuple-element.15.into_ref), custom_call_target="tpu_custom_call" | custom-call | flops 100000000 | bytes 500000 | tf_op jit(solution)/shard_map/pallas_call | solution.py:80
  57.8 8.1 %all-to-all-start.1 = ((f32[8,32,128]{2,1,0:T(8,128)}), f32[8,32,128]{2,1,0:T(8,128)S(1)}, u32[]{:S(2)}, u32[]{:S(2)}) async-start(f32[8,32,128]{2,1,0:T(8,128)} %get-tuple-element.18), calls=%async_computation.1 | async-start | bytes 262144 | tf_op jit(solution)/shard_map/all_to_all | solution.py:369
  65.9 1.8 %shard_map.76.streams_ref = bf16[2,128,256]{2,1,0:T(8,128)(2,1)S(1)} custom-call(bf16[16,64,128]{2,1,0:T(8,128)(2,1)} %collective-permute-done.blocks_ref, bf16[512,2048]{1,0:T(8,128)(2,1)S(1)} %get-tuple-element.13.rest_ref, f32[512,256]{1,0:T(8,128)S(1)} %get-tuple-element.14.product_ref, f32[128,256]{1,0:T(8,128)S(1)} %get-tuple-element.16.signal_ref), custom_call_target="tpu_custom_call" | custom-call | flops 100000000 | bytes 500000 | tf_op jit(solution)/shard_map/pallas_call | solution.py:80
  67.7 3.9 %collective-permute-start.6 = (bf16[2,128,256]{2,1,0:T(8,128)(2,1)S(1)}, bf16[2,128,256]{2,1,0:T(8,128)(2,1)S(1)}, u32[]{:S(2)}, u32[]{:S(2)}) collective-permute-start(bf16[2,128,256]{2,1,0:T(8,128)(2,1)S(1)} %shard_map.76.streams_ref), channel_id=1, source_target_pairs={{0,16},{16,32},{32,48},{48,64},{64,80},{80,96},{96,112},{112,0},{1... | collective-permute-start | bytes 393224 | tf_op jit(solution)/shard_map/ppermute | solution.py:380
  71.7 0.8 copy-done.11
  72.5 0.7 copy-done.12
  73.2 0.7 shard_map.77
  73.9 0.5 shard_map.78.local_ref
  74.4 1.8 %collective-permute-done.6.arrived_ref = bf16[2,128,256]{2,1,0:T(8,128)(2,1)S(1)} collective-permute-done((bf16[2,128,256]{2,1,0:T(8,128)(2,1)S(1)}, bf16[2,128,256]{2,1,0:T(8,128)(2,1)S(1)}, u32[]{:S(2)}, u32[]{:S(2)}) %collective-permute-start.6) | collective-permute-done | bytes 131104 | tf_op jit(solution)/shard_map/ppermute | solution.py:380
  76.3 1.3 %shard_map.79 = bf16[4,64,128]{2,1,0:T(8,128)(2,1)S(1)} custom-call(bf16[2,128,256]{2,1,0:T(8,128)(2,1)S(1)} %shard_map.76.streams_ref, f32[128,256]{1,0:T(8,128)S(1)} %shard_map.78.local_ref, bf16[2,128,256]{2,1,0:T(8,128)(2,1)S(1)} %collective-permute-done.6.arrived_ref, f32[8,32,128]{2,1,0:T(8,128)S(1)} %all-to-all-done.1.states_ref, ...), custom_call_target="tpu_custom_call" | custom-call | flops 100000000 | bytes 500000 | tf_op jit(solution)/shard_map/pallas_call | solution.py:80
  77.6 8.0 %all_to_all.15.packed_ref = bf16[4,64,128]{2,1,0:T(8,128)(2,1)S(1)} all-to-all(bf16[4,64,128]{2,1,0:T(8,128)(2,1)S(1)} %shard_map.79), channel_id=1, replica_groups={{0,128,256,384},{16,144,272,400},{32,160,288,416},{48,176,304,432},{64,..., dimensions={0} | all-to-all | bytes 131072 | tf_op jit(solution)/shard_map/all_to_all | solution.py:396
  85.6 0.7 shard_map.80
  (24 shorter events, 0.1 us)
Async XLA Ops:
  0.0 18.1 %collective-permute-start.1 = (bf16[128,4096]{1,0:T(8,128)(2,1)}, bf16[128,4096]{1,0:T(8,128)(2,1)S(1)}, u32[]{:S(2)}, u32[]{:S(2)}) collective-permute-start(bf16[128,4096]{1,0:T(8,128)(2,1)} %t0.1), channel_id=1, source_target_pairs={{0,128},{1,385},{2,130},{3,387},{4,132},{5,389},{6,134},{7,391},{8... | collective-permute-start | bytes 3145736 | tf_op jit(solution)/shard_map/ppermute | solution.py:316
  3.4 0.9 %copy-start.9 = (bf16[3,128,256]{2,1,0:T(8,128)(2,1)S(1)}, bf16[3,128,256]{2,1,0:T(8,128)(2,1)}, u32[]{:S(2)}) copy-start(bf16[3,128,256]{2,1,0:T(8,128)(2,1)} %w_ref.1) | copy-start | bytes 589828
  5.5 43.0 %copy-start.10 = (f32[256,16]{0,1:T(8,128)S(1)}, f32[256,16]{0,1:T(8,128)}, u32[]{:S(2)}) copy-start(f32[256,16]{0,1:T(8,128)} %param.9) | copy-start | bytes 49156
  5.5 32.8 %all-to-all-start = ((bf16[16,192,128]{2,1,0:T(8,128)(2,1)}), bf16[16,192,128]{2,1,0:T(8,128)(2,1)S(1)}, u32[]{:S(2)}, u32[]{:S(2)}) async-start(bf16[16,192,128]{2,1,0:T(8,128)(2,1)} %shard_map.73), calls=%async_computation | async-start | bytes 1572864 | tf_op jit(solution)/shard_map/all_to_all | solution.py:324
  18.1 29.4 %copy-start = (bf16[128,4096]{1,0:T(8,128)(2,1)}, bf16[128,4096]{1,0:T(8,128)(2,1)S(1)}, u32[]{:S(2)}) copy-start(bf16[128,4096]{1,0:T(8,128)(2,1)S(1)} %collective-permute-done.1.t1) | copy-start | bytes 3145732
  18.2 16.8 %collective-permute-start.3 = (bf16[128,2048]{1,0:T(8,128)(2,1)S(1)}, bf16[128,2048]{1,0:T(8,128)(2,1)S(1)}, u32[]{:S(2)}, u32[]{:S(2)}) collective-permute-start(bf16[128,2048]{1,0:T(8,128)(2,1)S(1)} %constant_dynamic-slice_fusion), channel_id=1, source_target_pairs={{0,128},{1,385},{2,130},{3,387},{4,132},{5,389},{6,134},{7,391},{8... | collective-permute-start | bytes 1572872 | tf_op jit(solution)/shard_map/ppermute | solution.py:331
  22.0 25.5 %collective-permute-start.2 = (bf16[128,4096]{1,0:T(8,128)(2,1)S(1)}, bf16[128,4096]{1,0:T(8,128)(2,1)S(1)}, u32[]{:S(2)}, u32[]{:S(2)}) collective-permute-start(bf16[128,4096]{1,0:T(8,128)(2,1)S(1)} %collective-permute-done.1.t1), channel_id=1, source_target_pairs={{0,1},{1,0},{2,3},{3,2},{4,5},{5,4},{6,7},{7,6},{8,9},{9,8},{10,11... | collective-permute-start | bytes 3145736 | tf_op jit(solution)/shard_map/ppermute | solution.py:330
  35.0 12.5 %copy-start.7 = (bf16[128,2048]{1,0:T(8,128)(2,1)}, bf16[128,2048]{1,0:T(8,128)(2,1)S(1)}, u32[]{:S(2)}) copy-start(bf16[128,2048]{1,0:T(8,128)(2,1)S(1)} %collective-permute-done.3.t3) | copy-start | bytes 1572868
  35.0 12.5 %collective-permute-start.4 = (bf16[128,2048]{1,0:T(8,128)(2,1)S(1)}, bf16[128,2048]{1,0:T(8,128)(2,1)}, u32[]{:S(2)}, u32[]{:S(2)}) collective-permute-start(bf16[128,2048]{1,0:T(8,128)(2,1)S(1)} %collective-permute-done.3.t3), channel_id=1, source_target_pairs={{0,1},{1,0},{2,3},{3,2},{4,5},{5,4},{6,7},{7,6},{8,9},{9,8},{10,11... | collective-permute-start | bytes 1572872 | tf_op jit(solution)/shard_map/ppermute | solution.py:332
  38.3 17.9 %collective-permute-start.5 = (bf16[16,128,128]{2,1,0:T(8,128)(2,1)S(1)}, bf16[16,128,128]{2,1,0:T(8,128)(2,1)S(1)}, u32[]{:S(2)}, u32[]{:S(2)}) collective-permute-start(bf16[16,128,128]{2,1,0:T(8,128)(2,1)S(1)} %slice.9), channel_id=1, source_target_pairs={{0,16},{1,113},{2,18},{3,115},{4,20},{5,117},{6,22},{7,119},{8,24}... | collective-permute-start | bytes 1572872 | tf_op jit(solution)/shard_map/ppermute | solution.py:328
  45.5 20.4 %collective-permute-start = (bf16[16,64,128]{2,1,0:T(8,128)(2,1)}, bf16[16,64,128]{2,1,0:T(8,128)(2,1)}, u32[]{:S(2)}, u32[]{:S(2)}) collective-permute-start(bf16[16,64,128]{2,1,0:T(8,128)(2,1)} %slice.8), channel_id=1, source_target_pairs={{0,16},{1,113},{2,18},{3,115},{4,20},{5,117},{6,22},{7,119},{8,24}... | collective-permute-start | bytes 786440 | tf_op jit(solution)/shard_map/ppermute | solution.py:329
  47.5 1.0 %copy-start.3 = (bf16[128,4096]{1,0:T(8,128)(2,1)}, bf16[128,4096]{1,0:T(8,128)(2,1)S(1)}, u32[]{:S(2)}) copy-start(bf16[128,4096]{1,0:T(8,128)(2,1)S(1)} %collective-permute-done.2.t2) | copy-start | bytes 3145732
  48.4 1.2 %copy-start.1 = (bf16[128,4096]{1,0:T(8,128)(2,1)S(1)}, bf16[128,4096]{1,0:T(8,128)(2,1)}, u32[]{:S(2)}) copy-start(bf16[128,4096]{1,0:T(8,128)(2,1)} %copy-done) | copy-start | bytes 3145732
  49.7 1.2 %copy-start.2 = (bf16[128,4096]{1,0:T(8,128)(2,1)S(1)}, bf16[128,4096]{1,0:T(8,128)(2,1)}, u32[]{:S(2)}) copy-start(bf16[128,4096]{1,0:T(8,128)(2,1)} %t0.1) | copy-start | bytes 3145732
  50.9 1.2 %copy-start.4 = (bf16[128,4096]{1,0:T(8,128)(2,1)S(1)}, bf16[128,4096]{1,0:T(8,128)(2,1)}, u32[]{:S(2)}) copy-start(bf16[128,4096]{1,0:T(8,128)(2,1)} %copy-done.3) | copy-start | bytes 3145732
  52.1 1.0 %copy-start.8 = (bf16[128,2048]{1,0:T(8,128)(2,1)S(1)}, bf16[128,2048]{1,0:T(8,128)(2,1)}, u32[]{:S(2)}) copy-start(bf16[128,2048]{1,0:T(8,128)(2,1)} %copy-done.7) | copy-start | bytes 1572868
  57.8 13.8 %copy-start.5 = (f32[256,256]{1,0:T(8,128)S(1)}, f32[256,256]{1,0:T(8,128)}, u32[]{:S(2)}) copy-start(f32[256,256]{1,0:T(8,128)} %constant.26.clone.fwd_ref) | copy-start | bytes 786436
  57.8 16.1 %copy-start.6 = (f32[256,256]{1,0:T(8,128)S(1)}, f32[256,256]{1,0:T(8,128)}, u32[]{:S(2)}) copy-start(f32[256,256]{1,0:T(8,128)} %constant.27.clone.inv_ref) | copy-start | bytes 786436
  57.8 18.4 %all-to-all-start.1 = ((f32[8,32,128]{2,1,0:T(8,128)}), f32[8,32,128]{2,1,0:T(8,128)S(1)}, u32[]{:S(2)}, u32[]{:S(2)}) async-start(f32[8,32,128]{2,1,0:T(8,128)} %get-tuple-element.18), calls=%async_computation.1 | async-start | bytes 262144 | tf_op jit(solution)/shard_map/all_to_all | solution.py:369
  67.7 8.6 %collective-permute-start.6 = (bf16[2,128,256]{2,1,0:T(8,128)(2,1)S(1)}, bf16[2,128,256]{2,1,0:T(8,128)(2,1)S(1)}, u32[]{:S(2)}, u32[]{:S(2)}) collective-permute-start(bf16[2,128,256]{2,1,0:T(8,128)(2,1)S(1)} %shard_map.76.streams_ref), channel_id=1, source_target_pairs={{0,16},{16,32},{32,48},{48,64},{64,80},{80,96},{96,112},{112,0},{1... | collective-permute-start | bytes 393224 | tf_op jit(solution)/shard_map/ppermute | solution.py:380
  71.6 0.8 copy-start.11
  72.5 0.7 copy-start.12

commit v9 on v6

--- a/solution.py
+++ b/solution.py
@@ -76,19 +76,26 @@
 VMEM, ANY = pl.BlockSpec(memory_space=pltpu.VMEM), pl.BlockSpec(memory_space=pltpu.HBM)
 
 
-def call(body, outs, *args, scratch=(), flops=10**8, far=0, out_specs=None):
+def call(body, outs, *args, scratch=(), flops=10**8, far=0, out_specs=None, limit=16):
     return pl.pallas_call(
         body,
         out_shape=outs,
         in_specs=[ANY] * far + [VMEM] * (len(args) - far),
         out_specs=jax.tree.map(lambda _: VMEM, outs) if out_specs is None else out_specs,
         scratch_shapes=scratch,
-        compiler_params=pltpu.CompilerParams(vmem_limit_bytes=16 << 20),
+        compiler_params=pltpu.CompilerParams(vmem_limit_bytes=limit << 20),
         cost_estimate=pl.CostEstimate(flops=flops, bytes_accessed=flops // 200, transcendentals=0),
     )(*args)
 
 
-def spread_weights(w_ref, out_ref, block_ref, sems):
+def y_side():
+    return lax.rem(lax.div(lax.axis_index("ch"), NC), 2)
+
+
+def spread_weights(tokens_ref, w_ref, out_ref, rows_ref, block_ref, sems, row_sem):
+    first = pl.multiple_of(y_side() * HALF, HALF)
+    rows = pltpu.make_async_copy(tokens_ref.at[pl.ds(first, HALF)], rows_ref, row_sem)
+    rows.start()
     low = lower_lanes((ROWS, LANES))
     low_half = lower_lanes((HALF, LANES))
     for x in range(NX):
@@ -110,6 +117,7 @@
         for z in range(NZ // 2):
             at = x * (NZ // 2) + z
             pltpu.make_async_copy(block_ref.at[x], out_ref.at[at], sems.at[at]).wait()
+    rows.wait()
 
 
 def own_channels(ref):
@@ -157,29 +165,25 @@
         wide_ref[bottom, LANES:] = jnp.where(low_half, turned, packed).astype(bf16)
 
 
-def project_first(t0, t1, t2, t3, t4, blocks_ref, a_ref, product_ref, rest_ref, into_ref, tokens_ref, wide_ref, sems):
+def project_first(t0, n0, n1, f0, f1, c0, c1, blocks_ref, a_ref, product_ref, rest_ref, into_ref, tokens_ref, wide_ref, sems):
     x, z, core = positions()
+    side_y = y_side()
     near = lax.rem(x + NX - 1 + 2 * core, NX)
     far = lax.rem(x + NX + 1 - 2 * core, NX)
     across = lax.rem(x + 2, NX)
-    half = BLOCKS // NC
-
-    def rows_of(k):
-        return pl.ds(pl.multiple_of(k * ROWS, ROWS), ROWS)
-
+    odd = lax.rem(side_y + core, 2)
+    pieces = [(1, n0, near, side_y), (1, n1, near, 1 - side_y), (2, f0, far, side_y), (2, f1, far, 1 - side_y)]
+    pieces += [(3, c0, across, odd), (3, c1, across, 1 - odd)]
     for side, target in ((0, tokens_ref), (1, rest_ref)):
         parity = lax.rem(z + side, 2)
         for i in range(BLOCKS):
             to = pl.ds(LANES * i, LANES)
             at = pl.ds(pl.multiple_of((2 * i + parity) * LANES, LANES), LANES)
-            for k, (ref, place) in enumerate(((t0, x), (t1, near), (t2, far))):
-                pltpu.make_async_copy(ref.at[:, at], target.at[rows_of(place), to], sems.at[k, side]).start()
-            inner = pl.ds(pl.multiple_of((2 * (i % half) + parity) * LANES, LANES), LANES)
-            mine = (i // half) == core
-            first = pltpu.make_async_copy(t3.at[:, inner], target.at[rows_of(across), to], sems.at[3, side])
-            second = pltpu.make_async_copy(t4.at[:, inner], target.at[rows_of(across), to], sems.at[3, side])
-            pl.when(mine)(first.start)
-            pl.when(jnp.logical_not(mine))(second.start)
+            own = pl.ds(pl.multiple_of(x * ROWS, ROWS), ROWS)
+            pltpu.make_async_copy(t0.at[:, at], target.at[own, to], sems.at[0, side]).start()
+            for k, ref, place, part in pieces:
+                rows = pl.ds(pl.multiple_of(place * ROWS + part * HALF, HALF), HALF)
+                pltpu.make_async_copy(ref.at[:, at], target.at[rows, to], sems.at[k, side]).start()
     widen(blocks_ref, wide_ref)
     back = ROWS - 1.0 - lax.broadcasted_iota(jnp.int32, (ROWS, LANES), 0).astype(f32)
     rates = own_channels(a_ref)
@@ -297,7 +301,6 @@
     sds = jax.ShapeDtypeStruct
     core = lax.axis_index("ch") % NC
     rows, features = tokens.shape
-    width = features // NC
     wide = lax.axis_size("ch")
 
     def place(a, b, k):
@@ -307,22 +310,31 @@
         (place(a, b, k), place(a + 1 - 2 * (k % NC), b, k)) for a in range(NX) for b in range(NZ) for k in range(wide)
     ]
     swap = [(k, k ^ 1) for k in range(wide)]
-    near = lax.ppermute(tokens, ("ctx", "ch"), outward)
-    blocks = call(
+    blocks, own_rows = call(
         spread_weights,
-        sds((BLOCKS, ROWS + HALF, LANES), bf16),
+        (sds((BLOCKS, ROWS + HALF, LANES), bf16), sds((HALF, features), bf16)),
+        tokens,
         projections,
-        scratch=[pltpu.VMEM((NX, ROWS + HALF, LANES), bf16), pltpu.SemaphoreType.DMA((BLOCKS,))],
-        out_specs=ANY,
-    )
+        scratch=[
+            pltpu.VMEM((NX, ROWS + HALF, LANES), bf16),
+            pltpu.SemaphoreType.DMA((BLOCKS,)),
+            pltpu.SemaphoreType.DMA,
+        ],
+        far=1,
+        out_specs=(ANY, VMEM),
+        limit=59,
+    )
+    near = lax.ppermute(own_rows, ("ctx", "ch"), outward)
     blocks = lax.all_to_all(blocks, "ctx", 0, 0, tiled=True, axis_index_groups=parity_groups)
     across = [
         (place(a, b, k), place(a, (b + 1 - 2 * (k % NC)) % NZ, k)) for a in range(NX) for b in range(NZ) for k in range(wide)
     ]
     rest_blocks = lax.ppermute(blocks, ("ctx", "ch"), across)
+    near_other = lax.ppermute(near, "ch", [(k, k ^ NC) for k in range(wide)])
     far = lax.ppermute(near, "ch", swap)
-    half = lax.ppermute(lax.dynamic_slice_in_dim(near, core * width, width, 1), ("ctx", "ch"), outward)
-    other = lax.ppermute(half, "ch", swap)
+    across_rows = lax.ppermute(jnp.where(core == 0, near, near_other), ("ctx", "ch"), outward)
+    far_other = lax.ppermute(near_other, "ch", swap)
+    across_other = lax.ppermute(across_rows, "ch", swap)
 
     rates = decay_rates.T
     forward, inverse = jnp.asarray(real_transform()), jnp.asarray(inverse_transform())
@@ -337,9 +349,11 @@
         (sds((NX * rows, 2 * LANES), f32), sds((NX * rows, half_depth), bf16), table),
         tokens,
         near,
+        near_other,
         far,
-        half,
-        other,
+        far_other,
+        across_rows,
+        across_other,
         blocks,
         rates,
         scratch=[
@@ -347,7 +361,7 @@
             pltpu.VMEM((half_depth, 2 * LANES), bf16),
             pltpu.SemaphoreType.DMA((4, 2)),
         ],
-        far=5,
+        far=7,
     )
     signal, streams, states = call(
         project_rest,

time: 80.6 us -> 94.5 us (1.17)
  the two profiles are of different devices: /device:TPU:40 before, /device:TPU:16 now
where the time goes in v9:
time: 94.5 us; the launch traced here: 93.9 us
  starting transfers between devices  42.9 us (45%)
  waiting for transfers between devices  31.2 us (33%)
  Pallas kernels  10.7 us (11%)
  blocking collectives  7.99 us (8%)
    all_to_all x1, waiting for transfers between devices, per_device(): lax.all_to_all(blocks, 'ctx', 0, 0, tiled=True, axis_index_groups=parity_...  15.3 us
    all_to_all x1, starting transfers between devices, per_device(): lax.all_to_all(blocks, 'ctx', 0, 0, tiled=True, axis_index_groups=parity_...  11.7 us
    pallas_call x7, Pallas kernels, call(): pl.pallas_call(body, out_shape=outs, in_specs=[ANY] * far + [VMEM] * (len...  10.7 us
    ppermute x1, waiting for transfers between devices, per_device(): near = lax.ppermute(own_rows, ('ctx', 'ch'), outward)  9.09 us
    all_to_all x1, blocking collectives, per_device(): lax.all_to_all(packed, 'ctx', 0, 0, tiled=True, axis_index_groups=x_groups)  7.99 us
    ppermute x1, starting transfers between devices, per_device(): rest_blocks = lax.ppermute(blocks, ('ctx', 'ch'), across)  7.09 us
    ppermute x1, waiting for transfers between devices, per_device(): arrived = lax.ppermute(streams, 'ctx', onward)  4.91 us
    ppermute x1, starting transfers between devices, per_device(): arrived = lax.ppermute(streams, 'ctx', onward)  3.82 us
  transfers between devices with their start and end apart: 10, of which 4 were waited for; matrix products, arithmetic and copies ran while one was open for 1% of the time, Pallas kernels for 4%

profile of v9, /device:TPU:16, one launch (start us, length us, event | category | flops | bytes accessed | tf_op | source)
XLA Modules:
  0.0 93.9 jit_solution(11003657501893737502)
XLA Ops:
  0.0 3.2 %shard_map.73 = (bf16[16,192,128]{2,1,0:T(8,128)(2,1)}, bf16[64,4096]{1,0:T(8,128)(2,1)}) custom-call(bf16[128,4096]{1,0:T(8,128)(2,1)} %t0.1, bf16[3,128,256]{2,1,0:T(8,128)(2,1)} %w_ref.1), custom_call_target="tpu_custom_call" | custom-call | flops 100000000 | bytes 500000 | tf_op jit(solution)/shard_map/pallas_call | solution.py:80
  3.2 3.4 %collective-permute-start.1 = (bf16[64,4096]{1,0:T(8,128)(2,1)}, bf16[64,4096]{1,0:T(8,128)(2,1)S(1)}, u32[]{:S(2)}, u32[]{:S(2)}) collective-permute-start(bf16[64,4096]{1,0:T(8,128)(2,1)} %get-tuple-element.17), channel_id=1, source_target_pairs={{0,128},{1,385},{2,130},{3,387},{4,132},{5,389},{6,134},{7,391},{8... | collective-permute-start | bytes 1572872 | tf_op jit(solution)/shard_map/ppermute | solution.py:327
  6.6 9.1 %collective-permute-done.1.n0 = bf16[64,4096]{1,0:T(8,128)(2,1)S(1)} collective-permute-done((bf16[64,4096]{1,0:T(8,128)(2,1)}, bf16[64,4096]{1,0:T(8,128)(2,1)S(1)}, u32[]{:S(2)}, u32[]{:S(2)}) %collective-permute-start.1) | collective-permute-done | bytes 524320 | tf_op jit(solution)/shard_map/ppermute | solution.py:327
  15.7 3.5 %collective-permute-start.2 = (bf16[64,4096]{1,0:T(8,128)(2,1)S(1)}, bf16[64,4096]{1,0:T(8,128)(2,1)S(1)}, u32[]{:S(2)}, u32[]{:S(2)}) collective-permute-start(bf16[64,4096]{1,0:T(8,128)(2,1)S(1)} %collective-permute-done.1.n0), channel_id=1, source_target_pairs={{0,2},{1,3},{2,0},{3,1},{4,6},{5,7},{6,4},{7,5},{8,10},{9,11},{10,... | collective-permute-start | bytes 1572872 | tf_op jit(solution)/shard_map/ppermute | solution.py:333
  19.2 11.7 %all-to-all-start = ((bf16[16,192,128]{2,1,0:T(8,128)(2,1)}), bf16[16,192,128]{2,1,0:T(8,128)(2,1)S(1)}, u32[]{:S(2)}, u32[]{:S(2)}) async-start(bf16[16,192,128]{2,1,0:T(8,128)(2,1)} %get-tuple-element.16), calls=%async_computation | async-start | bytes 1572864 | tf_op jit(solution)/shard_map/all_to_all | solution.py:328
  30.9 0.0 collective-permute-done.2.n1
  30.9 0.9 broadcast_select_fusion
  31.7 3.8 %collective-permute-start.5 = (bf16[64,4096]{1,0:T(8,128)(2,1)}, bf16[64,4096]{1,0:T(8,128)(2,1)S(1)}, u32[]{:S(2)}, u32[]{:S(2)}) collective-permute-start(bf16[64,4096]{1,0:T(8,128)(2,1)} %broadcast_select_fusion), channel_id=1, source_target_pairs={{0,128},{1,385},{2,130},{3,387},{4,132},{5,389},{6,134},{7,391},{8... | collective-permute-start | bytes 1572872 | tf_op jit(solution)/shard_map/ppermute | solution.py:335
  35.6 15.3 %all-to-all-done.blocks_ref = bf16[16,192,128]{2,1,0:T(8,128)(2,1)S(1)} async-done(((bf16[16,192,128]{2,1,0:T(8,128)(2,1)}), bf16[16,192,128]{2,1,0:T(8,128)(2,1)S(1)}, u32[]{:S(2)}, u32[]{:S(2)}) %all-to-all-start) | async-done | bytes 786464 | tf_op jit(solution)/shard_map/all_to_all | solution.py:328
  50.9 7.1 %collective-permute-start = (bf16[16,192,128]{2,1,0:T(8,128)(2,1)S(1)}, bf16[16,192,128]{2,1,0:T(8,128)(2,1)S(1)}, u32[]{:S(2)}, u32[]{:S(2)}) collective-permute-start(bf16[16,192,128]{2,1,0:T(8,128)(2,1)S(1)} %all-to-all-done.blocks_ref), channel_id=1, source_target_pairs={{0,16},{1,113},{2,18},{3,115},{4,20},{5,117},{6,22},{7,119},{8,24}... | collective-permute-start | bytes 2359304 | tf_op jit(solution)/shard_map/ppermute | solution.py:332
  58.0 1.9 %collective-permute-start.3 = (bf16[64,4096]{1,0:T(8,128)(2,1)S(1)}, bf16[64,4096]{1,0:T(8,128)(2,1)S(1)}, u32[]{:S(2)}, u32[]{:S(2)}) collective-permute-start(bf16[64,4096]{1,0:T(8,128)(2,1)S(1)} %collective-permute-done.1.n0), channel_id=1, source_target_pairs={{0,1},{1,0},{2,3},{3,2},{4,5},{5,4},{6,7},{7,6},{8,9},{9,8},{10,11... | collective-permute-start | bytes 1572872 | tf_op jit(solution)/shard_map/ppermute | solution.py:334
  59.9 2.4 %collective-permute-start.4 = (bf16[64,4096]{1,0:T(8,128)(2,1)S(1)}, bf16[64,4096]{1,0:T(8,128)(2,1)S(1)}, u32[]{:S(2)}, u32[]{:S(2)}) collective-permute-start(bf16[64,4096]{1,0:T(8,128)(2,1)S(1)} %collective-permute-done.2.n1), channel_id=1, source_target_pairs={{0,1},{1,0},{2,3},{3,2},{4,5},{5,4},{6,7},{7,6},{8,9},{9,8},{10,11... | collective-permute-start | bytes 1572872 | tf_op jit(solution)/shard_map/ppermute | solution.py:336
  62.3 1.9 %collective-permute-start.6 = (bf16[64,4096]{1,0:T(8,128)(2,1)S(1)}, bf16[64,4096]{1,0:T(8,128)(2,1)S(1)}, u32[]{:S(2)}, u32[]{:S(2)}) collective-permute-start(bf16[64,4096]{1,0:T(8,128)(2,1)S(1)} %collective-permute-done.5.c0), channel_id=1, source_target_pairs={{0,1},{1,0},{2,3},{3,2},{4,5},{5,4},{6,7},{7,6},{8,9},{9,8},{10,11... | collective-permute-start | bytes 1572872 | tf_op jit(solution)/shard_map/ppermute | solution.py:337
  64.3 0.0 collective-permute-done.3.f0
  64.3 0.0 collective-permute-done.4.f1
  64.3 1.9 %collective-permute-done.6.c1 = bf16[64,4096]{1,0:T(8,128)(2,1)S(1)} collective-permute-done((bf16[64,4096]{1,0:T(8,128)(2,1)S(1)}, bf16[64,4096]{1,0:T(8,128)(2,1)S(1)}, u32[]{:S(2)}, u32[]{:S(2)}) %collective-permute-start.6) | collective-permute-done | bytes 524320 | tf_op jit(solution)/shard_map/ppermute | solution.py:337
  66.1 2.6 %shard_map.74 = (f32[512,256]{1,0:T(8,128)S(1)}, bf16[512,2048]{1,0:T(8,128)(2,1)S(1)}, f32[16,128,128]{2,1,0:T(8,128)S(1)}) custom-call(bf16[128,4096]{1,0:T(8,128)(2,1)S(1)} %copy-done, bf16[64,4096]{1,0:T(8,128)(2,1)S(1)} %collective-permute-done.1.n0, bf16[64,4096]{1,0:T(8,128)(2,1)S(1)} %collective-permute-done.2.n1, ...), custom_call_target="tpu_custom_call" | custom-call | flops 100000000 | bytes 500000 | tf_op jit(solution)/shard_map/pallas_call | solution.py:80
  68.7 0.0 collective-permute-done.blocks_ref
  68.7 0.0 copy-start.1
  68.7 0.0 copy-start.4
  68.7 0.0 copy-start.5
  68.7 0.0 copy-start.2
  68.8 1.7 %shard_map.75 = (f32[128,256]{1,0:T(8,128)S(1)}, bf16[2,128,256]{2,1,0:T(8,128)(2,1)S(1)}, f32[8,32,128]{2,1,0:T(8,128)}) custom-call(bf16[16,192,128]{2,1,0:T(8,128)(2,1)S(1)} %collective-permute-done.blocks_ref, bf16[512,2048]{1,0:T(8,128)(2,1)S(1)} %get-tuple-element.18.rest_ref, f32[512,256]{1,0:T(8,128)S(1)} %get-tuple-element.19.product_ref, ...), custom_call_target="tpu_custom_call" | custom-call | flops 100000000 | bytes 500000 | tf_op jit(solution)/shard_map/pallas_call | solution.py:80
  70.5 3.4 %all-to-all-start.1 = ((f32[8,32,128]{2,1,0:T(8,128)}), f32[8,32,128]{2,1,0:T(8,128)S(1)}, u32[]{:S(2)}, u32[]{:S(2)}) async-start(f32[8,32,128]{2,1,0:T(8,128)} %get-tuple-element.24), calls=%async_computation.1 | async-start | bytes 262144 | tf_op jit(solution)/shard_map/all_to_all | solution.py:378
  73.9 3.8 %collective-permute-start.7 = (bf16[2,128,256]{2,1,0:T(8,128)(2,1)S(1)}, bf16[2,128,256]{2,1,0:T(8,128)(2,1)S(1)}, u32[]{:S(2)}, u32[]{:S(2)}) collective-permute-start(bf16[2,128,256]{2,1,0:T(8,128)(2,1)S(1)} %get-tuple-element.21.streams_ref), channel_id=1, source_target_pairs={{0,16},{16,32},{32,48},{48,64},{64,80},{80,96},{96,112},{112,0},{1... | collective-permute-start | bytes 393224 | tf_op jit(solution)/shard_map/ppermute | solution.py:380
  77.7 0.7 shard_map.76
  78.4 0.5 shard_map.77.local_ref
  79.0 4.9 %collective-permute-done.7.arrived_ref = bf16[2,128,256]{2,1,0:T(8,128)(2,1)S(1)} collective-permute-done((bf16[2,128,256]{2,1,0:T(8,128)(2,1)S(1)}, bf16[2,128,256]{2,1,0:T(8,128)(2,1)S(1)}, u32[]{:S(2)}, u32[]{:S(2)}) %collective-permute-start.7) | collective-permute-done | bytes 131104 | tf_op jit(solution)/shard_map/ppermute | solution.py:380
  83.9 0.0 all-to-all-done.1.states_ref
  83.9 1.3 %shard_map.78 = bf16[4,64,128]{2,1,0:T(8,128)(2,1)S(1)} custom-call(bf16[2,128,256]{2,1,0:T(8,128)(2,1)S(1)} %get-tuple-element.21.streams_ref, f32[128,256]{1,0:T(8,128)S(1)} %shard_map.77.local_ref, bf16[2,128,256]{2,1,0:T(8,128)(2,1)S(1)} %collective-permute-done.7.arrived_ref, f32[8,32,128]{2,1,0:T(8,128)S(1)} %all-to-all-done.1.states_ref, ...), custom_call_target="tpu_custom_call" | custom-call | flops 100000000 | bytes 500000 | tf_op jit(solution)/shard_map/pallas_call | solution.py:80
  85.2 8.0 %all_to_all.15.packed_ref = bf16[4,64,128]{2,1,0:T(8,128)(2,1)S(1)} all-to-all(bf16[4,64,128]{2,1,0:T(8,128)(2,1)S(1)} %shard_map.78), channel_id=1, replica_groups={{0,128,256,384},{16,144,272,400},{32,160,288,416},{48,176,304,432},{64,..., dimensions={0} | all-to-all | bytes 131072 | tf_op jit(solution)/shard_map/all_to_all | solution.py:396
  93.2 0.7 shard_map.79
  (9 shorter events, 0.0 us)
Async XLA Ops:
  0.0 66.1 %copy-start = (bf16[128,4096]{1,0:T(8,128)(2,1)S(1)}, bf16[128,4096]{1,0:T(8,128)(2,1)}, u32[]{:S(2)}) copy-start(bf16[128,4096]{1,0:T(8,128)(2,1)} %t0.1) | copy-start | bytes 3145732
  0.0 66.1 %copy-start.3 = (f32[256,16]{0,1:T(8,128)S(1)}, f32[256,16]{0,1:T(8,128)}, u32[]{:S(2)}) copy-start(f32[256,16]{0,1:T(8,128)} %param.9) | copy-start | bytes 49156
  3.2 12.5 %collective-permute-start.1 = (bf16[64,4096]{1,0:T(8,128)(2,1)}, bf16[64,4096]{1,0:T(8,128)(2,1)S(1)}, u32[]{:S(2)}, u32[]{:S(2)}) collective-permute-start(bf16[64,4096]{1,0:T(8,128)(2,1)} %get-tuple-element.17), channel_id=1, source_target_pairs={{0,128},{1,385},{2,130},{3,387},{4,132},{5,389},{6,134},{7,391},{8... | collective-permute-start | bytes 1572872 | tf_op jit(solution)/shard_map/ppermute | solution.py:327
  15.7 15.2 %collective-permute-start.2 = (bf16[64,4096]{1,0:T(8,128)(2,1)S(1)}, bf16[64,4096]{1,0:T(8,128)(2,1)S(1)}, u32[]{:S(2)}, u32[]{:S(2)}) collective-permute-start(bf16[64,4096]{1,0:T(8,128)(2,1)S(1)} %collective-permute-done.1.n0), channel_id=1, source_target_pairs={{0,2},{1,3},{2,0},{3,1},{4,6},{5,7},{6,4},{7,5},{8,10},{9,11},{10,... | collective-permute-start | bytes 1572872 | tf_op jit(solution)/shard_map/ppermute | solution.py:333
  19.2 31.7 %all-to-all-start = ((bf16[16,192,128]{2,1,0:T(8,128)(2,1)}), bf16[16,192,128]{2,1,0:T(8,128)(2,1)S(1)}, u32[]{:S(2)}, u32[]{:S(2)}) async-start(bf16[16,192,128]{2,1,0:T(8,128)(2,1)} %get-tuple-element.16), calls=%async_computation | async-start | bytes 1572864 | tf_op jit(solution)/shard_map/all_to_all | solution.py:328
  31.7 30.6 %collective-permute-start.5 = (bf16[64,4096]{1,0:T(8,128)(2,1)}, bf16[64,4096]{1,0:T(8,128)(2,1)S(1)}, u32[]{:S(2)}, u32[]{:S(2)}) collective-permute-start(bf16[64,4096]{1,0:T(8,128)(2,1)} %broadcast_select_fusion), channel_id=1, source_target_pairs={{0,128},{1,385},{2,130},{3,387},{4,132},{5,389},{6,134},{7,391},{8... | collective-permute-start | bytes 1572872 | tf_op jit(solution)/shard_map/ppermute | solution.py:335
  50.9 17.8 %collective-permute-start = (bf16[16,192,128]{2,1,0:T(8,128)(2,1)S(1)}, bf16[16,192,128]{2,1,0:T(8,128)(2,1)S(1)}, u32[]{:S(2)}, u32[]{:S(2)}) collective-permute-start(bf16[16,192,128]{2,1,0:T(8,128)(2,1)S(1)} %all-to-all-done.blocks_ref), channel_id=1, source_target_pairs={{0,16},{1,113},{2,18},{3,115},{4,20},{5,117},{6,22},{7,119},{8,24}... | collective-permute-start | bytes 2359304 | tf_op jit(solution)/shard_map/ppermute | solution.py:332
  58.0 6.3 %collective-permute-start.3 = (bf16[64,4096]{1,0:T(8,128)(2,1)S(1)}, bf16[64,4096]{1,0:T(8,128)(2,1)S(1)}, u32[]{:S(2)}, u32[]{:S(2)}) collective-permute-start(bf16[64,4096]{1,0:T(8,128)(2,1)S(1)} %collective-permute-done.1.n0), channel_id=1, source_target_pairs={{0,1},{1,0},{2,3},{3,2},{4,5},{5,4},{6,7},{7,6},{8,9},{9,8},{10,11... | collective-permute-start | bytes 1572872 | tf_op jit(solution)/shard_map/ppermute | solution.py:334
  59.9 4.4 %collective-permute-start.4 = (bf16[64,4096]{1,0:T(8,128)(2,1)S(1)}, bf16[64,4096]{1,0:T(8,128)(2,1)S(1)}, u32[]{:S(2)}, u32[]{:S(2)}) collective-permute-start(bf16[64,4096]{1,0:T(8,128)(2,1)S(1)} %collective-permute-done.2.n1), channel_id=1, source_target_pairs={{0,1},{1,0},{2,3},{3,2},{4,5},{5,4},{6,7},{7,6},{8,9},{9,8},{10,11... | collective-permute-start | bytes 1572872 | tf_op jit(solution)/shard_map/ppermute | solution.py:336
  62.3 3.8 %collective-permute-start.6 = (bf16[64,4096]{1,0:T(8,128)(2,1)S(1)}, bf16[64,4096]{1,0:T(8,128)(2,1)S(1)}, u32[]{:S(2)}, u32[]{:S(2)}) collective-permute-start(bf16[64,4096]{1,0:T(8,128)(2,1)S(1)} %collective-permute-done.5.c0), channel_id=1, source_target_pairs={{0,1},{1,0},{2,3},{3,2},{4,5},{5,4},{6,7},{7,6},{8,9},{9,8},{10,11... | collective-permute-start | bytes 1572872 | tf_op jit(solution)/shard_map/ppermute | solution.py:337
  68.7 9.0 %copy-start.1 = (f32[256,256]{1,0:T(8,128)S(1)}, f32[256,256]{1,0:T(8,128)}, u32[]{:S(2)}) copy-start(f32[256,256]{1,0:T(8,128)} %constant.22.clone.fwd_ref) | copy-start | bytes 786436
  68.7 9.0 %copy-start.4 = (bf16[256,128]{1,0:T(8,128)(2,1)S(1)}, bf16[256,128]{1,0:T(8,128)(2,1)}, u32[]{:S(2)}) copy-start(bf16[256,128]{1,0:T(8,128)(2,1)} %taps_ref.1) | copy-start | bytes 196612
  68.7 9.0 %copy-start.5 = (f32[256,16]{0,1:T(8,128)S(1)}, f32[256,16]{0,1:T(8,128)}, u32[]{:S(2)}) copy-start(f32[256,16]{0,1:T(8,128)} %param.10) | copy-start | bytes 49156
  68.7 9.7 %copy-start.2 = (f32[256,256]{1,0:T(8,128)S(1)}, f32[256,256]{1,0:T(8,128)}, u32[]{:S(2)}) copy-start(f32[256,256]{1,0:T(8,128)} %constant.23.clone.inv_ref) | copy-start | bytes 786436
  70.5 13.4 %all-to-all-start.1 = ((f32[8,32,128]{2,1,0:T(8,128)}), f32[8,32,128]{2,1,0:T(8,128)S(1)}, u32[]{:S(2)}, u32[]{:S(2)}) async-start(f32[8,32,128]{2,1,0:T(8,128)} %get-tuple-element.24), calls=%async_computation.1 | async-start | bytes 262144 | tf_op jit(solution)/shard_map/all_to_all | solution.py:378
  73.9 10.0 %collective-permute-start.7 = (bf16[2,128,256]{2,1,0:T(8,128)(2,1)S(1)}, bf16[2,128,256]{2,1,0:T(8,128)(2,1)S(1)}, u32[]{:S(2)}, u32[]{:S(2)}) collective-permute-start(bf16[2,128,256]{2,1,0:T(8,128)(2,1)S(1)} %get-tuple-element.21.streams_ref), channel_id=1, source_target_pairs={{0,16},{16,32},{32,48},{48,64},{64,80},{80,96},{96,112},{112,0},{1... | collective-permute-start | bytes 393224 | tf_op jit(solution)/shard_map/ppermute | solution.py:380

commit v10 on v6

--- a/solution.py
+++ b/solution.py
@@ -209,7 +209,7 @@
         gate_out = jnp.where(low, total_ref[chunks[0], LANES:], total_ref[chunks[1], LANES:])
         signal = gate_in * values
         signal_ref[:, lanes] = signal
-        for k, value in enumerate((signal, gate_out)):
+        for k, value in enumerate((*halves(signal), gate_out)):
             streams_ref[k, :, lanes] = value.astype(bf16)
         for m in range(MODES):
             state = jnp.sum(signal * into_ref[m], axis=0, keepdims=True)
@@ -260,14 +260,14 @@
         value = local[:, lanes]
         for m in range(MODES):
             value = value + out_ref[m] * carries[pair][m : m + 1, :]
-        parts.append((streams_ref[1, :, lanes].astype(f32) * value).astype(bf16).astype(f32))
+        parts.append((streams_ref[2, :, lanes].astype(f32) * value).astype(bf16).astype(f32))
     return parts
 
 
 def finish(streams_ref, local_ref, arrived_ref, states_ref, a_ref, out_ref, fwd_ref, inv_ref, long_ref, short_ref, packed_ref):
     _, z, _ = positions()
     low = lower_lanes((ROWS, LANES))
-    before = filter_inside(arrived_ref[0], fwd_ref, inv_ref, long_ref)
+    before = filter_inside(arrived_ref[0].astype(f32) + arrived_ref[1].astype(f32), fwd_ref, inv_ref, long_ref)
     own = gate_rows(streams_ref, local_ref[...], carry_in(states_ref, a_ref, z), out_ref)
     arrived = gate_rows(arrived_ref, before, carry_in(states_ref, a_ref, lax.rem(z + NZ - 1, NZ)), out_ref)
     turned = [swap_halves(v) for v in arrived]
@@ -351,7 +351,7 @@
     )
     signal, streams, states = call(
         project_rest,
-        (sds((ROWS, 2 * LANES), f32), sds((2, ROWS, 2 * LANES), bf16), sds((NZ, 2 * MODES, LANES), f32)),
+        (sds((ROWS, 2 * LANES), f32), sds((3, ROWS, 2 * LANES), bf16), sds((NZ, 2 * MODES, LANES), f32)),
         rest_blocks,
         rest,
         product,

time: 80.6 us -> 81.8 us (1.015)
  the two profiles are of different devices: /device:TPU:40 before, /device:TPU:32 now
where the time goes in v10:
time: 81.8 us; the launch traced here: 81.3 us
  starting transfers between devices  38.2 us (47%)
  waiting for transfers between devices  24.1 us (29%)
  Pallas kernels  8.56 us (10%)
  blocking collectives  8.52 us (10%)
  local copies, waits for them, and re-layouts  1.77 us (2%)
    all_to_all x1, waiting for transfers between devices, per_device(): lax.all_to_all(blocks, 'ctx', 0, 0, tiled=True, axis_index_groups=parity_...  13.6 us
    all_to_all x1, starting transfers between devices, per_device(): lax.all_to_all(blocks, 'ctx', 0, 0, tiled=True, axis_index_groups=parity_...  12.6 us
    pallas_call x7, Pallas kernels, call(): pl.pallas_call(body, out_shape=outs, in_specs=[ANY] * far + [VMEM] * (len...  8.56 us
    all_to_all x1, blocking collectives, per_device(): lax.all_to_all(packed, 'ctx', 0, 0, tiled=True, axis_index_groups=x_groups)  8.52 us
    ppermute x1, starting transfers between devices, per_device(): rest_blocks = lax.ppermute(blocks, ('ctx', 'ch'), across)  6.47 us
    ppermute x1, waiting for transfers between devices, per_device(): arrived = lax.ppermute(streams, 'ctx', onward)  5.36 us
    all_to_all x1, starting transfers between devices, per_device(): lax.all_to_all(states, 'ctx', 0, 0, tiled=True, axis_index_groups=z_groups)  4.03 us
    ppermute x1, starting transfers between devices, per_device(): arrived = lax.ppermute(streams, 'ctx', onward)  3.92 us
  transfers between devices with their start and end apart: 8, of which 4 were waited for; matrix products, arithmetic and copies ran while one was open for 1% of the time, Pallas kernels for 6%

profile of v10, /device:TPU:32, one launch (start us, length us, event | category | flops | bytes accessed | tf_op | source)
XLA Modules:
  0.0 81.3 jit_solution(17753412112146211310)
XLA Ops:
  0.0 3.5 %collective-permute-start.1 = (bf16[128,4096]{1,0:T(8,128)(2,1)}, bf16[128,4096]{1,0:T(8,128)(2,1)S(1)}, u32[]{:S(2)}, u32[]{:S(2)}) collective-permute-start(bf16[128,4096]{1,0:T(8,128)(2,1)} %t0.1), channel_id=1, source_target_pairs={{0,128},{1,385},{2,130},{3,387},{4,132},{5,389},{6,134},{7,391},{8... | collective-permute-start | bytes 3145736 | tf_op jit(solution)/shard_map/ppermute | solution.py:310
  3.5 0.0 copy-start.3
  3.5 0.9 %copy-done.3 = bf16[3,128,256]{2,1,0:T(8,128)(2,1)S(1)} copy-done((bf16[3,128,256]{2,1,0:T(8,128)(2,1)S(1)}, bf16[3,128,256]{2,1,0:T(8,128)(2,1)}, u32[]{:S(2)}) %copy-start.3) | copy-done | bytes 196632
  4.5 1.1 %shard_map.73 = bf16[16,192,128]{2,1,0:T(8,128)(2,1)} custom-call(bf16[3,128,256]{2,1,0:T(8,128)(2,1)S(1)} %copy-done.3), custom_call_target="tpu_custom_call" | custom-call | flops 100000000 | bytes 500000 | tf_op jit(solution)/shard_map/pallas_call | solution.py:80
  5.6 12.6 %all-to-all-start = ((bf16[16,192,128]{2,1,0:T(8,128)(2,1)}), bf16[16,192,128]{2,1,0:T(8,128)(2,1)S(1)}, u32[]{:S(2)}, u32[]{:S(2)}) async-start(bf16[16,192,128]{2,1,0:T(8,128)(2,1)} %shard_map.73), calls=%async_computation | async-start | bytes 1572864 | tf_op jit(solution)/shard_map/all_to_all | solution.py:318
  18.2 0.0 collective-permute-done.1.t1
  18.2 0.8 %constant_dynamic-slice_fusion = bf16[128,2048]{1,0:T(8,128)(2,1)} fusion(bf16[128,4096]{1,0:T(8,128)(2,1)S(1)} %collective-permute-done.1.t1, s32[]{:T(128)S(6)} %select_n.11), kind=kLoop, calls=%fused_computation | loop fusion | bytes 1048580 | tf_op jit(solution)/shard_map/dynamic_slice | solution.py:324
  19.1 3.8 %collective-permute-start.3 = (bf16[128,2048]{1,0:T(8,128)(2,1)}, bf16[128,2048]{1,0:T(8,128)(2,1)S(1)}, u32[]{:S(2)}, u32[]{:S(2)}) collective-permute-start(bf16[128,2048]{1,0:T(8,128)(2,1)} %constant_dynamic-slice_fusion), channel_id=1, source_target_pairs={{0,128},{1,385},{2,130},{3,387},{4,132},{5,389},{6,134},{7,391},{8... | collective-permute-start | bytes 1572872 | tf_op jit(solution)/shard_map/ppermute | solution.py:324
  22.9 1.9 %collective-permute-start.2 = (bf16[128,4096]{1,0:T(8,128)(2,1)S(1)}, bf16[128,4096]{1,0:T(8,128)(2,1)}, u32[]{:S(2)}, u32[]{:S(2)}) collective-permute-start(bf16[128,4096]{1,0:T(8,128)(2,1)S(1)} %collective-permute-done.1.t1), channel_id=1, source_target_pairs={{0,1},{1,0},{2,3},{3,2},{4,5},{5,4},{6,7},{7,6},{8,9},{9,8},{10,11... | collective-permute-start | bytes 3145736 | tf_op jit(solution)/shard_map/ppermute | solution.py:323
  24.8 13.6 %all-to-all-done.blocks_ref = bf16[16,192,128]{2,1,0:T(8,128)(2,1)S(1)} async-done(((bf16[16,192,128]{2,1,0:T(8,128)(2,1)}), bf16[16,192,128]{2,1,0:T(8,128)(2,1)S(1)}, u32[]{:S(2)}, u32[]{:S(2)}) %all-to-all-start) | async-done | bytes 786464 | tf_op jit(solution)/shard_map/all_to_all | solution.py:318
  38.4 6.5 %collective-permute-start = (bf16[16,192,128]{2,1,0:T(8,128)(2,1)S(1)}, bf16[16,192,128]{2,1,0:T(8,128)(2,1)S(1)}, u32[]{:S(2)}, u32[]{:S(2)}) collective-permute-start(bf16[16,192,128]{2,1,0:T(8,128)(2,1)S(1)} %all-to-all-done.blocks_ref), channel_id=1, source_target_pairs={{0,16},{1,113},{2,18},{3,115},{4,20},{5,117},{6,22},{7,119},{8,24}... | collective-permute-start | bytes 2359304 | tf_op jit(solution)/shard_map/ppermute | solution.py:322
  44.9 0.0 collective-permute-done.3.t3
  44.9 1.9 %collective-permute-start.4 = (bf16[128,2048]{1,0:T(8,128)(2,1)S(1)}, bf16[128,2048]{1,0:T(8,128)(2,1)S(1)}, u32[]{:S(2)}, u32[]{:S(2)}) collective-permute-start(bf16[128,2048]{1,0:T(8,128)(2,1)S(1)} %collective-permute-done.3.t3), channel_id=1, source_target_pairs={{0,1},{1,0},{2,3},{3,2},{4,5},{5,4},{6,7},{7,6},{8,9},{9,8},{10,11... | collective-permute-start | bytes 1572872 | tf_op jit(solution)/shard_map/ppermute | solution.py:325
  46.8 1.9 %collective-permute-done.4.t4 = bf16[128,2048]{1,0:T(8,128)(2,1)S(1)} collective-permute-done((bf16[128,2048]{1,0:T(8,128)(2,1)S(1)}, bf16[128,2048]{1,0:T(8,128)(2,1)S(1)}, u32[]{:S(2)}, u32[]{:S(2)}) %collective-permute-start.4) | collective-permute-done | bytes 524320 | tf_op jit(solution)/shard_map/ppermute | solution.py:325
  48.7 0.0 collective-permute-done.2.t2
  48.7 0.0 copy-done
  48.7 0.0 copy-done.4
  48.7 2.4 %shard_map.74 = (f32[512,256]{1,0:T(8,128)S(1)}, bf16[512,2048]{1,0:T(8,128)(2,1)S(1)}, f32[16,128,128]{2,1,0:T(8,128)S(1)}) custom-call(bf16[128,4096]{1,0:T(8,128)(2,1)S(1)} %copy-done, bf16[128,4096]{1,0:T(8,128)(2,1)S(1)} %collective-permute-done.1.t1, bf16[128,4096]{1,0:T(8,128)(2,1)} %collective-permute-done.2.t2, ...), custom_call_target="tpu_custom_call" | custom-call | flops 100000000 | bytes 500000 | tf_op jit(solution)/shard_map/pallas_call | solution.py:80
  51.1 3.3 %collective-permute-done.blocks_ref = bf16[16,192,128]{2,1,0:T(8,128)(2,1)S(1)} collective-permute-done((bf16[16,192,128]{2,1,0:T(8,128)(2,1)S(1)}, bf16[16,192,128]{2,1,0:T(8,128)(2,1)S(1)}, u32[]{:S(2)}, u32[]{:S(2)}) %collective-permute-start) | collective-permute-done | bytes 786464 | tf_op jit(solution)/shard_map/ppermute | solution.py:322
  54.4 1.8 %shard_map.75 = (f32[128,256]{1,0:T(8,128)S(1)}, bf16[3,128,256]{2,1,0:T(8,128)(2,1)S(1)}, f32[8,32,128]{2,1,0:T(8,128)}) custom-call(bf16[16,192,128]{2,1,0:T(8,128)(2,1)S(1)} %collective-permute-done.blocks_ref, bf16[512,2048]{1,0:T(8,128)(2,1)S(1)} %get-tuple-element.14.rest_ref, f32[512,256]{1,0:T(8,128)S(1)} %get-tuple-element.15.product_ref, ...), custom_call_target="tpu_custom_call" | custom-call | flops 100000000 | bytes 500000 | tf_op jit(solution)/shard_map/pallas_call | solution.py:80
  56.1 4.0 %all-to-all-start.1 = ((f32[8,32,128]{2,1,0:T(8,128)}), f32[8,32,128]{2,1,0:T(8,128)S(1)}, u32[]{:S(2)}, u32[]{:S(2)}) async-start(f32[8,32,128]{2,1,0:T(8,128)} %get-tuple-element.20), calls=%async_computation.1 | async-start | bytes 262144 | tf_op jit(solution)/shard_map/all_to_all | solution.py:364
  60.2 3.9 %collective-permute-start.5 = (bf16[3,128,256]{2,1,0:T(8,128)(2,1)S(1)}, bf16[3,128,256]{2,1,0:T(8,128)(2,1)S(1)}, u32[]{:S(2)}, u32[]{:S(2)}) collective-permute-start(bf16[3,128,256]{2,1,0:T(8,128)(2,1)S(1)} %get-tuple-element.17.streams_ref), channel_id=1, source_target_pairs={{0,16},{16,32},{32,48},{48,64},{64,80},{80,96},{96,112},{112,0},{1... | collective-permute-start | bytes 589832 | tf_op jit(solution)/shard_map/ppermute | solution.py:366
  64.1 0.0 copy-done.1
  64.1 0.0 copy-done.5
  64.1 0.0 copy-done.6
  64.1 0.7 shard_map.76
  64.8 0.5 shard_map.77.local_ref
  65.4 5.4 %collective-permute-done.5.arrived_ref = bf16[3,128,256]{2,1,0:T(8,128)(2,1)S(1)} collective-permute-done((bf16[3,128,256]{2,1,0:T(8,128)(2,1)S(1)}, bf16[3,128,256]{2,1,0:T(8,128)(2,1)S(1)}, u32[]{:S(2)}, u32[]{:S(2)}) %collective-permute-start.5) | collective-permute-done | bytes 196640 | tf_op jit(solution)/shard_map/ppermute | solution.py:366
  70.7 0.0 all-to-all-done.1.states_ref
  70.7 1.3 %shard_map.78 = bf16[4,64,128]{2,1,0:T(8,128)(2,1)S(1)} custom-call(bf16[3,128,256]{2,1,0:T(8,128)(2,1)S(1)} %get-tuple-element.17.streams_ref, f32[128,256]{1,0:T(8,128)S(1)} %shard_map.77.local_ref, bf16[3,128,256]{2,1,0:T(8,128)(2,1)S(1)} %collective-permute-done.5.arrived_ref, f32[8,32,128]{2,1,0:T(8,128)S(1)} %all-to-all-done.1.states_ref, ...), custom_call_target="tpu_custom_call" | custom-call | flops 100000000 | bytes 500000 | tf_op jit(solution)/shard_map/pallas_call | solution.py:80
  72.1 8.5 %all_to_all.15.packed_ref = bf16[4,64,128]{2,1,0:T(8,128)(2,1)S(1)} all-to-all(bf16[4,64,128]{2,1,0:T(8,128)(2,1)S(1)} %shard_map.78), channel_id=1, replica_groups={{0,128,256,384},{16,144,272,400},{32,160,288,416},{48,176,304,432},{64,..., dimensions={0} | all-to-all | bytes 131072 | tf_op jit(solution)/shard_map/all_to_all | solution.py:382
  80.6 0.7 shard_map.79
  (7 shorter events, 0.0 us)
Async XLA Ops:
  0.0 48.7 %copy-start = (bf16[128,4096]{1,0:T(8,128)(2,1)S(1)}, bf16[128,4096]{1,0:T(8,128)(2,1)}, u32[]{:S(2)}) copy-start(bf16[128,4096]{1,0:T(8,128)(2,1)} %t0.1) | copy-start | bytes 3145732
  0.0 18.2 %collective-permute-start.1 = (bf16[128,4096]{1,0:T(8,128)(2,1)}, bf16[128,4096]{1,0:T(8,128)(2,1)S(1)}, u32[]{:S(2)}, u32[]{:S(2)}) collective-permute-start(bf16[128,4096]{1,0:T(8,128)(2,1)} %t0.1), channel_id=1, source_target_pairs={{0,128},{1,385},{2,130},{3,387},{4,132},{5,389},{6,134},{7,391},{8... | collective-permute-start | bytes 3145736 | tf_op jit(solution)/shard_map/ppermute | solution.py:310
  3.5 0.9 %copy-start.3 = (bf16[3,128,256]{2,1,0:T(8,128)(2,1)S(1)}, bf16[3,128,256]{2,1,0:T(8,128)(2,1)}, u32[]{:S(2)}) copy-start(bf16[3,128,256]{2,1,0:T(8,128)(2,1)} %w_ref.1) | copy-start | bytes 589828
  4.5 44.3 %copy-start.4 = (f32[256,16]{0,1:T(8,128)S(1)}, f32[256,16]{0,1:T(8,128)}, u32[]{:S(2)}) copy-start(f32[256,16]{0,1:T(8,128)} %param.9) | copy-start | bytes 49156
  5.6 32.8 %all-to-all-start = ((bf16[16,192,128]{2,1,0:T(8,128)(2,1)}), bf16[16,192,128]{2,1,0:T(8,128)(2,1)S(1)}, u32[]{:S(2)}, u32[]{:S(2)}) async-start(bf16[16,192,128]{2,1,0:T(8,128)(2,1)} %shard_map.73), calls=%async_computation | async-start | bytes 1572864 | tf_op jit(solution)/shard_map/all_to_all | solution.py:318
  19.1 25.8 %collective-permute-start.3 = (bf16[128,2048]{1,0:T(8,128)(2,1)}, bf16[128,2048]{1,0:T(8,128)(2,1)S(1)}, u32[]{:S(2)}, u32[]{:S(2)}) collective-permute-start(bf16[128,2048]{1,0:T(8,128)(2,1)} %constant_dynamic-slice_fusion), channel_id=1, source_target_pairs={{0,128},{1,385},{2,130},{3,387},{4,132},{5,389},{6,134},{7,391},{8... | collective-permute-start | bytes 1572872 | tf_op jit(solution)/shard_map/ppermute | solution.py:324
  22.9 25.8 %collective-permute-start.2 = (bf16[128,4096]{1,0:T(8,128)(2,1)S(1)}, bf16[128,4096]{1,0:T(8,128)(2,1)}, u32[]{:S(2)}, u32[]{:S(2)}) collective-permute-start(bf16[128,4096]{1,0:T(8,128)(2,1)S(1)} %collective-permute-done.1.t1), channel_id=1, source_target_pairs={{0,1},{1,0},{2,3},{3,2},{4,5},{5,4},{6,7},{7,6},{8,9},{9,8},{10,11... | collective-permute-start | bytes 3145736 | tf_op jit(solution)/shard_map/ppermute | solution.py:323
  38.4 16.0 %collective-permute-start = (bf16[16,192,128]{2,1,0:T(8,128)(2,1)S(1)}, bf16[16,192,128]{2,1,0:T(8,128)(2,1)S(1)}, u32[]{:S(2)}, u32[]{:S(2)}) collective-permute-start(bf16[16,192,128]{2,1,0:T(8,128)(2,1)S(1)} %all-to-all-done.blocks_ref), channel_id=1, source_target_pairs={{0,16},{1,113},{2,18},{3,115},{4,20},{5,117},{6,22},{7,119},{8,24}... | collective-permute-start | bytes 2359304 | tf_op jit(solution)/shard_map/ppermute | solution.py:322
  44.9 3.8 %collective-permute-start.4 = (bf16[128,2048]{1,0:T(8,128)(2,1)S(1)}, bf16[128,2048]{1,0:T(8,128)(2,1)S(1)}, u32[]{:S(2)}, u32[]{:S(2)}) collective-permute-start(bf16[128,2048]{1,0:T(8,128)(2,1)S(1)} %collective-permute-done.3.t3), channel_id=1, source_target_pairs={{0,1},{1,0},{2,3},{3,2},{4,5},{5,4},{6,7},{7,6},{8,9},{9,8},{10,11... | collective-permute-start | bytes 1572872 | tf_op jit(solution)/shard_map/ppermute | solution.py:325
  54.4 9.7 %copy-start.1 = (f32[256,256]{1,0:T(8,128)S(1)}, f32[256,256]{1,0:T(8,128)}, u32[]{:S(2)}) copy-start(f32[256,256]{1,0:T(8,128)} %constant.26.clone.fwd_ref) | copy-start | bytes 786436
  54.4 9.7 %copy-start.5 = (bf16[256,128]{1,0:T(8,128)(2,1)S(1)}, bf16[256,128]{1,0:T(8,128)(2,1)}, u32[]{:S(2)}) copy-start(bf16[256,128]{1,0:T(8,128)(2,1)} %taps_ref.1) | copy-start | bytes 196612
  54.4 9.7 %copy-start.6 = (f32[256,16]{0,1:T(8,128)S(1)}, f32[256,16]{0,1:T(8,128)}, u32[]{:S(2)}) copy-start(f32[256,16]{0,1:T(8,128)} %param.10) | copy-start | bytes 49156
  54.4 10.5 %copy-start.2 = (f32[256,256]{1,0:T(8,128)S(1)}, f32[256,256]{1,0:T(8,128)}, u32[]{:S(2)}) copy-start(f32[256,256]{1,0:T(8,128)} %constant.27.clone.inv_ref) | copy-start | bytes 786436
  56.1 14.6 %all-to-all-start.1 = ((f32[8,32,128]{2,1,0:T(8,128)}), f32[8,32,128]{2,1,0:T(8,128)S(1)}, u32[]{:S(2)}, u32[]{:S(2)}) async-start(f32[8,32,128]{2,1,0:T(8,128)} %get-tuple-element.20), calls=%async_computation.1 | async-start | bytes 262144 | tf_op jit(solution)/shard_map/all_to_all | solution.py:364
  60.2 10.6 %collective-permute-start.5 = (bf16[3,128,256]{2,1,0:T(8,128)(2,1)S(1)}, bf16[3,128,256]{2,1,0:T(8,128)(2,1)S(1)}, u32[]{:S(2)}, u32[]{:S(2)}) collective-permute-start(bf16[3,128,256]{2,1,0:T(8,128)(2,1)S(1)} %get-tuple-element.17.streams_ref), channel_id=1, source_target_pairs={{0,16},{16,32},{32,48},{48,64},{64,80},{80,96},{96,112},{112,0},{1... | collective-permute-start | bytes 589832 | tf_op jit(solution)/shard_map/ppermute | solution.py:366

commit v11 on v7

--- a/solution.py
+++ b/solution.py
@@ -248,23 +248,27 @@
     return [before[0] + decay_here * first, before[1] + decay_here * second]
 
 
-def gate_rows(streams_ref, local, carries, out_ref):
-    parts = []
+def gate_rows(chunks, out_ref):
+    gated = [[] for _ in chunks]
     for pair in range(NX // 2):
         lanes = slice(LANES * pair, LANES * (pair + 1))
-        value = local[:, lanes]
+        values = [local[:, lanes] for _, local, _ in chunks]
         for m in range(MODES):
-            value = value + out_ref[m] * carries[pair][m : m + 1, :]
-        parts.append((streams_ref[1, :, lanes].astype(f32) * value).astype(bf16).astype(f32))
-    return parts
+            table = out_ref[m]
+            values = [v + table * c[2][pair][m : m + 1, :] for v, c in zip(values, chunks)]
+        for rows, value, (streams_ref, _, _) in zip(gated, values, chunks):
+            rows.append((streams_ref[1, :, lanes].astype(f32) * value).astype(bf16).astype(f32))
+    return gated
 
 
 def finish(streams_ref, local_ref, arrived_ref, states_ref, a_ref, out_ref, fwd_ref, inv_ref, long_ref, short_ref, packed_ref):
     _, z, _ = positions()
     low = lower_lanes((ROWS, LANES))
     before = filter_inside(arrived_ref[0], fwd_ref, inv_ref, long_ref)
-    own = gate_rows(streams_ref, local_ref[...], carry_in(states_ref, a_ref, z), out_ref)
-    arrived = gate_rows(arrived_ref, before, carry_in(states_ref, a_ref, lax.rem(z + NZ - 1, NZ)), out_ref)
+    carries = [carry_in(states_ref, a_ref, place) for place in (z, lax.rem(z + NZ - 1, NZ))]
+    own, arrived = gate_rows(
+        ((streams_ref, local_ref[...], carries[0]), (arrived_ref, before, carries[1])), out_ref
+    )
     turned = [swap_halves(v) for v in arrived]
     shifted = [jnp.where(low, 0.0, turned[0]), jnp.where(low, turned[0], turned[1])]
     previous = jnp.concatenate([jnp.where(z == 0, s, a) for s, a in zip(shifted, arrived)], axis=1)
@@ -302,8 +306,8 @@
         (place(a, b, k), place(a + 1 - 2 * (k % NC), b, k)) for a in range(NX) for b in range(NZ) for k in range(wide)
     ]
     swap = [(k, k ^ 1) for k in range(wide)]
+    near = lax.ppermute(tokens, ("ctx", "ch"), outward)
     blocks = call(spread_weights, sds((BLOCKS, ROWS + HALF, LANES), bf16), projections)
-    near = lax.ppermute(tokens, ("ctx", "ch"), outward)
     blocks = lax.all_to_all(blocks, "ctx", 0, 0, tiled=True, axis_index_groups=parity_groups)
     across = [
         (place(a, b, k), place(a, (b + 1 - 2 * (k % NC)) % NZ, k)) for a in range(NX) for b in range(NZ) for k in range(wide)

time: 80.5 us -> 80.5 us (level)
  the two profiles are of different devices: /device:TPU:40 before, /device:TPU:48 now
where the time goes in v11:
time: 80.5 us; the launch traced here: 80 us
  starting transfers between devices  38 us (47%)
  waiting for transfers between devices  23.5 us (29%)
  Pallas kernels  8.39 us (10%)
  blocking collectives  8.12 us (10%)
  local copies, waits for them, and re-layouts  1.77 us (2%)
    all_to_all x1, waiting for transfers between devices, per_device(): lax.all_to_all(blocks, 'ctx', 0, 0, tiled=True, axis_index_groups=parity_...  13.6 us
    all_to_all x1, starting transfers between devices, per_device(): lax.all_to_all(blocks, 'ctx', 0, 0, tiled=True, axis_index_groups=parity_...  12.6 us
    pallas_call x7, Pallas kernels, call(): pl.pallas_call(body, out_shape=outs, in_specs=[ANY] * far + [VMEM] * (len...  8.39 us
    all_to_all x1, blocking collectives, per_device(): lax.all_to_all(packed, 'ctx', 0, 0, tiled=True, axis_index_groups=x_groups)  8.12 us
    ppermute x1, starting transfers between devices, per_device(): rest_blocks = lax.ppermute(blocks, ('ctx', 'ch'), across)  6.47 us
    all_to_all x1, starting transfers between devices, per_device(): lax.all_to_all(states, 'ctx', 0, 0, tiled=True, axis_index_groups=z_groups)  4.03 us
    ppermute x1, starting transfers between devices, per_device(): arrived = lax.ppermute(streams, 'ctx', onward)  3.92 us
    ppermute x1, waiting for transfers between devices, per_device(): arrived = lax.ppermute(streams, 'ctx', onward)  3.78 us
  transfers between devices with their start and end apart: 8, of which 6 were waited for; matrix products, arithmetic and copies ran while one was open for 1% of the time, Pallas kernels for 6%

profile of v11, /device:TPU:48, one launch (start us, length us, event | category | flops | bytes accessed | tf_op | source)
XLA Modules:
  0.0 80.0 jit_solution(7765723081196435692)
XLA Ops:
  0.0 3.5 %collective-permute-start.1 = (bf16[128,4096]{1,0:T(8,128)(2,1)}, bf16[128,4096]{1,0:T(8,128)(2,1)S(1)}, u32[]{:S(2)}, u32[]{:S(2)}) collective-permute-start(bf16[128,4096]{1,0:T(8,128)(2,1)} %t0.1), channel_id=1, source_target_pairs={{0,128},{1,385},{2,130},{3,387},{4,132},{5,389},{6,134},{7,391},{8... | collective-permute-start | bytes 3145736 | tf_op jit(solution)/shard_map/ppermute | solution.py:309
  3.5 0.0 copy-start.3
  3.5 0.9 %copy-done.3 = bf16[3,128,256]{2,1,0:T(8,128)(2,1)S(1)} copy-done((bf16[3,128,256]{2,1,0:T(8,128)(2,1)S(1)}, bf16[3,128,256]{2,1,0:T(8,128)(2,1)}, u32[]{:S(2)}) %copy-start.3) | copy-done | bytes 196632
  4.5 1.0 %shard_map.73 = bf16[16,192,128]{2,1,0:T(8,128)(2,1)} custom-call(bf16[3,128,256]{2,1,0:T(8,128)(2,1)S(1)} %copy-done.3), custom_call_target="tpu_custom_call" | custom-call | flops 100000000 | bytes 500000 | tf_op jit(solution)/shard_map/pallas_call | solution.py:80
  5.5 12.6 %all-to-all-start = ((bf16[16,192,128]{2,1,0:T(8,128)(2,1)}), bf16[16,192,128]{2,1,0:T(8,128)(2,1)S(1)}, u32[]{:S(2)}, u32[]{:S(2)}) async-start(bf16[16,192,128]{2,1,0:T(8,128)(2,1)} %shard_map.73), calls=%async_computation | async-start | bytes 1572864 | tf_op jit(solution)/shard_map/all_to_all | solution.py:311
  18.1 0.1 collective-permute-done.1.t1
  18.2 0.8 %constant_dynamic-slice_fusion = bf16[128,2048]{1,0:T(8,128)(2,1)} fusion(bf16[128,4096]{1,0:T(8,128)(2,1)S(1)} %collective-permute-done.1.t1, s32[]{:T(128)S(6)} %select_n.11), kind=kLoop, calls=%fused_computation | loop fusion | bytes 1048580 | tf_op jit(solution)/shard_map/dynamic_slice | solution.py:317
  19.1 3.7 %collective-permute-start.3 = (bf16[128,2048]{1,0:T(8,128)(2,1)}, bf16[128,2048]{1,0:T(8,128)(2,1)S(1)}, u32[]{:S(2)}, u32[]{:S(2)}) collective-permute-start(bf16[128,2048]{1,0:T(8,128)(2,1)} %constant_dynamic-slice_fusion), channel_id=1, source_target_pairs={{0,128},{1,385},{2,130},{3,387},{4,132},{5,389},{6,134},{7,391},{8... | collective-permute-start | bytes 1572872 | tf_op jit(solution)/shard_map/ppermute | solution.py:317
  22.8 1.9 %collective-permute-start.2 = (bf16[128,4096]{1,0:T(8,128)(2,1)S(1)}, bf16[128,4096]{1,0:T(8,128)(2,1)}, u32[]{:S(2)}, u32[]{:S(2)}) collective-permute-start(bf16[128,4096]{1,0:T(8,128)(2,1)S(1)} %collective-permute-done.1.t1), channel_id=1, source_target_pairs={{0,1},{1,0},{2,3},{3,2},{4,5},{5,4},{6,7},{7,6},{8,9},{9,8},{10,11... | collective-permute-start | bytes 3145736 | tf_op jit(solution)/shard_map/ppermute | solution.py:316
  24.7 13.6 %all-to-all-done.blocks_ref = bf16[16,192,128]{2,1,0:T(8,128)(2,1)S(1)} async-done(((bf16[16,192,128]{2,1,0:T(8,128)(2,1)}), bf16[16,192,128]{2,1,0:T(8,128)(2,1)S(1)}, u32[]{:S(2)}, u32[]{:S(2)}) %all-to-all-start) | async-done | bytes 786464 | tf_op jit(solution)/shard_map/all_to_all | solution.py:311
  38.3 6.5 %collective-permute-start = (bf16[16,192,128]{2,1,0:T(8,128)(2,1)S(1)}, bf16[16,192,128]{2,1,0:T(8,128)(2,1)S(1)}, u32[]{:S(2)}, u32[]{:S(2)}) collective-permute-start(bf16[16,192,128]{2,1,0:T(8,128)(2,1)S(1)} %all-to-all-done.blocks_ref), channel_id=1, source_target_pairs={{0,16},{1,113},{2,18},{3,115},{4,20},{5,117},{6,22},{7,119},{8,24}... | collective-permute-start | bytes 2359304 | tf_op jit(solution)/shard_map/ppermute | solution.py:315
  44.8 0.0 collective-permute-done.3.t3
  44.8 1.9 %collective-permute-start.4 = (bf16[128,2048]{1,0:T(8,128)(2,1)S(1)}, bf16[128,2048]{1,0:T(8,128)(2,1)S(1)}, u32[]{:S(2)}, u32[]{:S(2)}) collective-permute-start(bf16[128,2048]{1,0:T(8,128)(2,1)S(1)} %collective-permute-done.3.t3), channel_id=1, source_target_pairs={{0,1},{1,0},{2,3},{3,2},{4,5},{5,4},{6,7},{7,6},{8,9},{9,8},{10,11... | collective-permute-start | bytes 1572872 | tf_op jit(solution)/shard_map/ppermute | solution.py:318
  46.7 1.9 %collective-permute-done.4.t4 = bf16[128,2048]{1,0:T(8,128)(2,1)S(1)} collective-permute-done((bf16[128,2048]{1,0:T(8,128)(2,1)S(1)}, bf16[128,2048]{1,0:T(8,128)(2,1)S(1)}, u32[]{:S(2)}, u32[]{:S(2)}) %collective-permute-start.4) | collective-permute-done | bytes 524320 | tf_op jit(solution)/shard_map/ppermute | solution.py:318
  48.6 0.0 collective-permute-done.2.t2
  48.6 0.0 copy-done
  48.6 0.0 copy-done.4
  48.6 2.4 %shard_map.74 = (f32[512,256]{1,0:T(8,128)S(1)}, bf16[512,2048]{1,0:T(8,128)(2,1)S(1)}, f32[16,128,128]{2,1,0:T(8,128)S(1)}) custom-call(bf16[128,4096]{1,0:T(8,128)(2,1)S(1)} %copy-done, bf16[128,4096]{1,0:T(8,128)(2,1)S(1)} %collective-permute-done.1.t1, bf16[128,4096]{1,0:T(8,128)(2,1)} %collective-permute-done.2.t2, ...), custom_call_target="tpu_custom_call" | custom-call | flops 100000000 | bytes 500000 | tf_op jit(solution)/shard_map/pallas_call | solution.py:80
  51.0 3.3 %collective-permute-done.blocks_ref = bf16[16,192,128]{2,1,0:T(8,128)(2,1)S(1)} collective-permute-done((bf16[16,192,128]{2,1,0:T(8,128)(2,1)S(1)}, bf16[16,192,128]{2,1,0:T(8,128)(2,1)S(1)}, u32[]{:S(2)}, u32[]{:S(2)}) %collective-permute-start) | collective-permute-done | bytes 786464 | tf_op jit(solution)/shard_map/ppermute | solution.py:315
  54.3 1.7 %shard_map.75 = (f32[128,256]{1,0:T(8,128)S(1)}, bf16[2,128,256]{2,1,0:T(8,128)(2,1)S(1)}, f32[8,32,128]{2,1,0:T(8,128)}) custom-call(bf16[16,192,128]{2,1,0:T(8,128)(2,1)S(1)} %collective-permute-done.blocks_ref, bf16[512,2048]{1,0:T(8,128)(2,1)S(1)} %get-tuple-element.14.rest_ref, f32[512,256]{1,0:T(8,128)S(1)} %get-tuple-element.15.product_ref, ...), custom_call_target="tpu_custom_call" | custom-call | flops 100000000 | bytes 500000 | tf_op jit(solution)/shard_map/pallas_call | solution.py:80
  56.0 4.0 %all-to-all-start.1 = ((f32[8,32,128]{2,1,0:T(8,128)}), f32[8,32,128]{2,1,0:T(8,128)S(1)}, u32[]{:S(2)}, u32[]{:S(2)}) async-start(f32[8,32,128]{2,1,0:T(8,128)} %get-tuple-element.20), calls=%async_computation.1 | async-start | bytes 262144 | tf_op jit(solution)/shard_map/all_to_all | solution.py:357
  60.0 3.9 %collective-permute-start.5 = (bf16[2,128,256]{2,1,0:T(8,128)(2,1)S(1)}, bf16[2,128,256]{2,1,0:T(8,128)(2,1)S(1)}, u32[]{:S(2)}, u32[]{:S(2)}) collective-permute-start(bf16[2,128,256]{2,1,0:T(8,128)(2,1)S(1)} %get-tuple-element.17.streams_ref), channel_id=1, source_target_pairs={{0,16},{16,32},{32,48},{48,64},{64,80},{80,96},{96,112},{112,0},{1... | collective-permute-start | bytes 393224 | tf_op jit(solution)/shard_map/ppermute | solution.py:359
  64.0 0.0 copy-done.1
  64.0 0.0 copy-done.5
  64.0 0.0 copy-done.6
  64.0 0.7 shard_map.76
  64.7 0.5 shard_map.77.local_ref
  65.2 3.8 %collective-permute-done.5.arrived_ref = bf16[2,128,256]{2,1,0:T(8,128)(2,1)S(1)} collective-permute-done((bf16[2,128,256]{2,1,0:T(8,128)(2,1)S(1)}, bf16[2,128,256]{2,1,0:T(8,128)(2,1)S(1)}, u32[]{:S(2)}, u32[]{:S(2)}) %collective-permute-start.5) | collective-permute-done | bytes 131104 | tf_op jit(solution)/shard_map/ppermute | solution.py:359
  69.0 0.8 all-to-all-done.1.states_ref
  69.8 1.3 %shard_map.78 = bf16[4,64,128]{2,1,0:T(8,128)(2,1)S(1)} custom-call(bf16[2,128,256]{2,1,0:T(8,128)(2,1)S(1)} %get-tuple-element.17.streams_ref, f32[128,256]{1,0:T(8,128)S(1)} %shard_map.77.local_ref, bf16[2,128,256]{2,1,0:T(8,128)(2,1)S(1)} %collective-permute-done.5.arrived_ref, f32[8,32,128]{2,1,0:T(8,128)S(1)} %all-to-all-done.1.states_ref, ...), custom_call_target="tpu_custom_call" | custom-call | flops 100000000 | bytes 500000 | tf_op jit(solution)/shard_map/pallas_call | solution.py:80
  71.1 8.1 %all_to_all.15.packed_ref = bf16[4,64,128]{2,1,0:T(8,128)(2,1)S(1)} all-to-all(bf16[4,64,128]{2,1,0:T(8,128)(2,1)S(1)} %shard_map.78), channel_id=1, replica_groups={{0,128,256,384},{16,144,272,400},{32,160,288,416},{48,176,304,432},{64,..., dimensions={0} | all-to-all | bytes 131072 | tf_op jit(solution)/shard_map/all_to_all | solution.py:375
  79.2 0.7 shard_map.79
  (7 shorter events, 0.0 us)
Async XLA Ops:
  0.0 48.6 %copy-start = (bf16[128,4096]{1,0:T(8,128)(2,1)S(1)}, bf16[128,4096]{1,0:T(8,128)(2,1)}, u32[]{:S(2)}) copy-start(bf16[128,4096]{1,0:T(8,128)(2,1)} %t0.1) | copy-start | bytes 3145732
  0.0 18.2 %collective-permute-start.1 = (bf16[128,4096]{1,0:T(8,128)(2,1)}, bf16[128,4096]{1,0:T(8,128)(2,1)S(1)}, u32[]{:S(2)}, u32[]{:S(2)}) collective-permute-start(bf16[128,4096]{1,0:T(8,128)(2,1)} %t0.1), channel_id=1, source_target_pairs={{0,128},{1,385},{2,130},{3,387},{4,132},{5,389},{6,134},{7,391},{8... | collective-permute-start | bytes 3145736 | tf_op jit(solution)/shard_map/ppermute | solution.py:309
  3.5 0.9 %copy-start.3 = (bf16[3,128,256]{2,1,0:T(8,128)(2,1)S(1)}, bf16[3,128,256]{2,1,0:T(8,128)(2,1)}, u32[]{:S(2)}) copy-start(bf16[3,128,256]{2,1,0:T(8,128)(2,1)} %w_ref.1) | copy-start | bytes 589828
  4.5 44.1 %copy-start.4 = (f32[256,16]{0,1:T(8,128)S(1)}, f32[256,16]{0,1:T(8,128)}, u32[]{:S(2)}) copy-start(f32[256,16]{0,1:T(8,128)} %param.9) | copy-start | bytes 49156
  5.5 32.8 %all-to-all-start = ((bf16[16,192,128]{2,1,0:T(8,128)(2,1)}), bf16[16,192,128]{2,1,0:T(8,128)(2,1)S(1)}, u32[]{:S(2)}, u32[]{:S(2)}) async-start(bf16[16,192,128]{2,1,0:T(8,128)(2,1)} %shard_map.73), calls=%async_computation | async-start | bytes 1572864 | tf_op jit(solution)/shard_map/all_to_all | solution.py:311
  19.1 25.7 %collective-permute-start.3 = (bf16[128,2048]{1,0:T(8,128)(2,1)}, bf16[128,2048]{1,0:T(8,128)(2,1)S(1)}, u32[]{:S(2)}, u32[]{:S(2)}) collective-permute-start(bf16[128,2048]{1,0:T(8,128)(2,1)} %constant_dynamic-slice_fusion), channel_id=1, source_target_pairs={{0,128},{1,385},{2,130},{3,387},{4,132},{5,389},{6,134},{7,391},{8... | collective-permute-start | bytes 1572872 | tf_op jit(solution)/shard_map/ppermute | solution.py:317
  22.8 25.8 %collective-permute-start.2 = (bf16[128,4096]{1,0:T(8,128)(2,1)S(1)}, bf16[128,4096]{1,0:T(8,128)(2,1)}, u32[]{:S(2)}, u32[]{:S(2)}) collective-permute-start(bf16[128,4096]{1,0:T(8,128)(2,1)S(1)} %collective-permute-done.1.t1), channel_id=1, source_target_pairs={{0,1},{1,0},{2,3},{3,2},{4,5},{5,4},{6,7},{7,6},{8,9},{9,8},{10,11... | collective-permute-start | bytes 3145736 | tf_op jit(solution)/shard_map/ppermute | solution.py:316
  38.3 16.0 %collective-permute-start = (bf16[16,192,128]{2,1,0:T(8,128)(2,1)S(1)}, bf16[16,192,128]{2,1,0:T(8,128)(2,1)S(1)}, u32[]{:S(2)}, u32[]{:S(2)}) collective-permute-start(bf16[16,192,128]{2,1,0:T(8,128)(2,1)S(1)} %all-to-all-done.blocks_ref), channel_id=1, source_target_pairs={{0,16},{1,113},{2,18},{3,115},{4,20},{5,117},{6,22},{7,119},{8,24}... | collective-permute-start | bytes 2359304 | tf_op jit(solution)/shard_map/ppermute | solution.py:315
  44.8 3.8 %collective-permute-start.4 = (bf16[128,2048]{1,0:T(8,128)(2,1)S(1)}, bf16[128,2048]{1,0:T(8,128)(2,1)S(1)}, u32[]{:S(2)}, u32[]{:S(2)}) collective-permute-start(bf16[128,2048]{1,0:T(8,128)(2,1)S(1)} %collective-permute-done.3.t3), channel_id=1, source_target_pairs={{0,1},{1,0},{2,3},{3,2},{4,5},{5,4},{6,7},{7,6},{8,9},{9,8},{10,11... | collective-permute-start | bytes 1572872 | tf_op jit(solution)/shard_map/ppermute | solution.py:318
  54.3 9.7 %copy-start.1 = (f32[256,256]{1,0:T(8,128)S(1)}, f32[256,256]{1,0:T(8,128)}, u32[]{:S(2)}) copy-start(f32[256,256]{1,0:T(8,128)} %constant.26.clone.fwd_ref) | copy-start | bytes 786436
  54.3 9.7 %copy-start.5 = (bf16[256,128]{1,0:T(8,128)(2,1)S(1)}, bf16[256,128]{1,0:T(8,128)(2,1)}, u32[]{:S(2)}) copy-start(bf16[256,128]{1,0:T(8,128)(2,1)} %taps_ref.1) | copy-start | bytes 196612
  54.3 9.7 %copy-start.6 = (f32[256,16]{0,1:T(8,128)S(1)}, f32[256,16]{0,1:T(8,128)}, u32[]{:S(2)}) copy-start(f32[256,16]{0,1:T(8,128)} %param.10) | copy-start | bytes 49156
  54.3 10.4 %copy-start.2 = (f32[256,256]{1,0:T(8,128)S(1)}, f32[256,256]{1,0:T(8,128)}, u32[]{:S(2)}) copy-start(f32[256,256]{1,0:T(8,128)} %constant.27.clone.inv_ref) | copy-start | bytes 786436
  56.0 13.8 %all-to-all-start.1 = ((f32[8,32,128]{2,1,0:T(8,128)}), f32[8,32,128]{2,1,0:T(8,128)S(1)}, u32[]{:S(2)}, u32[]{:S(2)}) async-start(f32[8,32,128]{2,1,0:T(8,128)} %get-tuple-element.20), calls=%async_computation.1 | async-start | bytes 262144 | tf_op jit(solution)/shard_map/all_to_all | solution.py:357
  60.0 9.0 %collective-permute-start.5 = (bf16[2,128,256]{2,1,0:T(8,128)(2,1)S(1)}, bf16[2,128,256]{2,1,0:T(8,128)(2,1)S(1)}, u32[]{:S(2)}, u32[]{:S(2)}) collective-permute-start(bf16[2,128,256]{2,1,0:T(8,128)(2,1)S(1)} %get-tuple-element.17.streams_ref), channel_id=1, source_target_pairs={{0,16},{16,32},{32,48},{48,64},{64,80},{80,96},{96,112},{112,0},{1... | collective-permute-start | bytes 393224 | tf_op jit(solution)/shard_map/ppermute | solution.py:359
